TPU v7x, 32 devices: a whole 2x2x4 slice. The times are simulated.
32 devices in a mesh: section: 2 (over core), dp: 4 (over y, x), seq: 4 (over z).
Axes of the slice: x: 2, y: 2, z: 4, core: 2. Of those that a mesh axis runs over, the one named last changes fastest.
Arguments:
- inputs: bfloat16 [2, 4, 1024, 1024], P(None, 'dp', 'seq'), may hold values from -16 to 16
- doc_lengths: int32 [2, 4, 4], P(None, 'dp'), may hold values from 1 to 512, 1024 in all within a row
- out_grad: bfloat16 [2, 4, 1024, 1024], P(None, 'dp', 'seq'), may hold values from -6 to 6
- norm_gain: bfloat16 [2, 1024], P('section', ('dp', 'seq')), may hold values from 0.5 to 1.5
- in_weight: bfloat16 [2, 1024, 4096], P('section', ('dp', 'seq')), may hold values from -0.1875 to 0.1875
- conv_weight: bfloat16 [2, 4, 2048], P('section', None, ('dp', 'seq')), may hold values from -3 to 3
- conv_bias: bfloat16 [2, 2048], P('section', ('dp', 'seq')), may hold values from -0.5 to 0.5
- select_weight: bfloat16 [2, 2048, 96], P('section', ('dp', 'seq')), may hold values from -0.125 to 0.125
- step_weight: bfloat16 [2, 64, 2048], P('section', None, ('dp', 'seq')), may hold values from -0.75 to 0.75
- step_bias: bfloat16 [2, 2048], P('section', ('dp', 'seq')), may hold values from -6.875 to -2.296875
- log_decay: bfloat16 [2, 16, 2048], P('section', None, ('dp', 'seq')), may hold values from -4 to 2
- skip_gain: bfloat16 [2, 2048], P('section', ('dp', 'seq')), may hold values from 0.5 to 1.5
- out_weight: bfloat16 [2, 2048, 1024], P('section', ('dp', 'seq')), may hold values from -0.25 to 0.25
Outputs:
- layer_out: float32 [2, 2, 4, 1024, 1024], P('section', None, 'dp', 'seq')
- layer_in_grad: float32 [2, 2, 4, 1024, 1024], P('section', None, 'dp', 'seq')
- grad_norm_gain: float32 [2, 1024], P('section', ('dp', 'seq'))
- grad_in_weight: float32 [2, 1024, 4096], P('section', ('dp', 'seq'))
- grad_conv_weight: float32 [2, 4, 2048], P('section', None, ('dp', 'seq'))
- grad_conv_bias: float32 [2, 2048], P('section', ('dp', 'seq'))
- grad_select_weight: float32 [2, 2048, 96], P('section', ('dp', 'seq'))
- grad_step_weight: float32 [2, 64, 2048], P('section', None, ('dp', 'seq'))
- grad_step_bias: float32 [2, 2048], P('section', ('dp', 'seq'))
- grad_log_decay: float32 [2, 16, 2048], P('section', None, ('dp', 'seq'))
- grad_skip_gain: float32 [2, 2048], P('section', ('dp', 'seq'))
- grad_out_weight: float32 [2, 2048, 1024], P('section', ('dp', 'seq'))
- step_moments: float32 [2, 2, 2048], P('section', None, ('dp', 'seq'))
Inputs may be any that keep to these rules, and one draw needn't show every extreme that they name: `doc_lengths`: each row's 4 document lengths sum to 1024; the longest is exactly 512.
All inputs are finite; a program needn't handle non-finite values.
Results may differ from a plain program's by a relative error of at most 0.013.
Values may be sent and summed in bfloat16 or wider, within the bound.
A program may use at most 768 MiB of HBM per device.

v0:
```python
from functools import partial
import math

import jax
import jax.numpy as jnp
from jax import lax
from jax.sharding import PartitionSpec as P

eps = 1e-05


def shifted(value, axis, steps):
    count = lax.axis_size(axis)
    first, last = (max(0, -steps), min(count, count - steps))
    return lax.ppermute(value, axis, [(source, source + steps) for source in range(first, last)])


def entering_2(part, axis, combine, identity):
    place = lax.axis_index(axis)
    gathered = jax.tree.map(lambda a: lax.all_gather(a, axis), part)
    state = jax.tree.map(lambda a, e: jnp.zeros_like(a) + jnp.asarray(e, a.dtype), part, identity)

    def one(step, state):
        return combine(
            state, jax.tree.map(lambda a: lax.dynamic_index_in_dim(a, step, 0, False), gathered)
        )

    return lax.fori_loop(0, place, one, state)


def entering_3(value, axis, combine, identity):
    length, mine = (lax.axis_size(axis), lax.axis_index(axis))
    everything = jax.tree.map(
        lambda part, kind: lax.all_gather(part.astype(kind), axis),
        value,
        (jnp.bfloat16, jnp.bfloat16),
    )
    start = jax.tree.map(
        lambda part, zero: jnp.broadcast_to(jnp.asarray(zero, part.dtype), part.shape),
        value,
        identity,
    )

    def step(k, before):
        at = length - 1 - k
        reached = at > mine
        new = combine(
            before, jax.tree.map(lambda part, own: part[at].astype(own.dtype), everything, value)
        )
        return jax.tree.map(lambda a, b: jnp.where(reached, a, b), new, before)

    return lax.fori_loop(0, length, step, start)


def chain_join(earlier, later):
    return (earlier[0] * later[0], later[0] * earlier[1] + later[1])


def silu_slope(values):
    sigma = jax.nn.sigmoid(values)
    return sigma * (1.0 + values * (1.0 - sigma))


def outer_sum(left, right):
    return lax.dot_general(
        left, right, (((0,), (0,)), ((), ())), preferred_element_type=jnp.float32
    )


def times_transposed(left, right):
    return lax.dot_general(
        left, right, (((1,), (1,)), ((), ())), preferred_element_type=jnp.float32
    )


def chained(rates, terms, reverse):
    count = rates.shape[0]
    tail = rates.shape[1:]
    sub_len = math.gcd(count, 16)
    groups = count // sub_len
    rate_grid = rates.reshape((groups, sub_len) + tail)
    term_grid = terms.reshape((groups, sub_len) + tail)

    def stepper(index, carry):
        total, product, totals, products = carry
        place = sub_len - 1 - index if reverse else index
        rate_now = lax.dynamic_index_in_dim(rate_grid, place, 1, keepdims=False)
        term_now = lax.dynamic_index_in_dim(term_grid, place, 1, keepdims=False)
        total = rate_now * total + term_now
        product = rate_now * product
        totals = lax.dynamic_update_index_in_dim(totals, total, place, 1)
        products = lax.dynamic_update_index_in_dim(products, product, place, 1)
        return (total, product, totals, products)

    start = (
        jnp.zeros((groups,) + tail, jnp.float32),
        jnp.ones((groups,) + tail, jnp.float32),
        jnp.zeros(rate_grid.shape, jnp.float32),
        jnp.zeros(rate_grid.shape, jnp.float32),
    )
    last_total, last_product, totals, products = lax.fori_loop(0, sub_len, stepper, start)

    def linker(entering, item):
        product_end, total_end = item
        return (product_end * entering + total_end, entering)

    unused, entering = lax.scan(
        linker, jnp.zeros(tail, jnp.float32), (last_product, last_total), reverse=reverse
    )
    states = totals + products * entering[:, None]
    return states.reshape((count,) + tail)


def doc_layout(lengths, base, count):
    starts = jnp.cumsum(lengths, axis=-1) - lengths
    places = base + jnp.arange(count, dtype=jnp.int32)
    before = (starts[:, None, :] <= places[None, :, None]).astype(jnp.int32)
    segment = jnp.sum(before, axis=-1) - 1
    resets = jnp.sum((starts[:, None, :] == places[None, :, None]).astype(jnp.float32), axis=-1)
    return (segment, resets)


def triangles(count):
    row_at = jnp.arange(count)[:, None]
    col_at = jnp.arange(count)[None, :]
    return ((col_at > row_at).astype(jnp.float32), (col_at <= row_at).astype(jnp.float32))


def forward_totals(decay_rate, above_diag, pieces):
    step_size, resets, act_rows, input_map = pieces
    highest = lax.Precision.HIGHEST
    after_sum = jnp.dot(above_diag, step_size, precision=highest)
    clear_after = (jnp.dot(above_diag, resets[:, None], precision=highest) < 0.5).astype(
        jnp.float32
    )
    reach_rate = jnp.exp(decay_rate[None] * after_sum[:, None, :])
    end_state = jnp.einsum(
        "tnd,td,tn->nd",
        reach_rate,
        clear_after * step_size * act_rows,
        input_map,
        precision=highest,
    )
    whole_gain = jnp.exp(decay_rate * jnp.sum(step_size, axis=0)[None]) * (
        jnp.sum(resets) < 0.5
    ).astype(jnp.float32)
    return (whole_gain, end_state)


def backward_totals(decay_rate, below_diag, pieces):
    step_size, resets, scan_grad, output_map = pieces
    highest = lax.Precision.HIGHEST
    upto_sum = jnp.dot(below_diag, step_size, precision=highest)
    clear_upto = (jnp.dot(below_diag, resets[:, None], precision=highest) < 0.5).astype(jnp.float32)
    reach_rate = jnp.exp(decay_rate[None] * upto_sum[:, None, :])
    back_state = jnp.einsum(
        "tnd,td,tn->nd", reach_rate, clear_upto * scan_grad, output_map, precision=highest
    )
    whole_gain = jnp.exp(decay_rate * jnp.sum(step_size, axis=0)[None]) * (
        jnp.sum(resets) < 0.5
    ).astype(jnp.float32)
    return (whole_gain, back_state)


def state_rates(decay_rate, step_size, resets, act_rows, input_map, start_state):
    keep_rate = jnp.exp(decay_rate[None] * step_size[:, None, :]) * (1.0 - resets)[:, None, None]
    add_term = (step_size * act_rows)[:, None, :] * input_map[:, :, None]
    add_term = jnp.concatenate(
        [add_term[:1] + keep_rate[:1] * start_state[None], add_term[1:]], axis=0
    )
    states = chained(keep_rate, add_term, False)
    return (keep_rate, states)


def forward_row(decay_rate, pieces):
    step_size, resets, act_rows, input_map, output_map, start_state = pieces
    keep_rate, states = state_rates(decay_rate, step_size, resets, act_rows, input_map, start_state)
    return jnp.einsum("tnd,tn->td", states, output_map, precision=lax.Precision.HIGHEST)


def backward_row(decay_rate, pieces):
    step_size, resets, act_rows, input_map, output_map, start_state, incoming, scan_grad = pieces
    highest = lax.Precision.HIGHEST
    keep_rate, states = state_rates(decay_rate, step_size, resets, act_rows, input_map, start_state)
    emit_grad = output_map[:, :, None] * scan_grad[:, None, :]
    emit_grad = jnp.concatenate([emit_grad[:-1], emit_grad[-1:] + incoming[None]], axis=0)
    next_rate = jnp.concatenate([keep_rate[1:], jnp.ones_like(keep_rate[:1])], axis=0)
    state_grad = chained(next_rate, emit_grad, True)
    prior_state = jnp.concatenate([start_state[None], states[:-1]], axis=0)
    rate_grad = state_grad * prior_state * keep_rate
    mapped_grad = jnp.einsum("tnd,tn->td", state_grad, input_map, precision=highest)
    step_grad = (
        jnp.einsum("tnd,nd->td", rate_grad, decay_rate, precision=highest) + mapped_grad * act_rows
    )
    act_grad = mapped_grad * step_size
    in_map_grad = jnp.einsum("tnd,td->tn", state_grad, step_size * act_rows, precision=highest)
    out_map_grad = jnp.einsum("tnd,td->tn", states, scan_grad, precision=highest)
    decay_grad = jnp.einsum("tnd,td->nd", rate_grad, step_size, precision=highest)
    scan_out = jnp.einsum("tnd,tn->td", states, output_map, precision=highest)
    return (step_grad, act_grad, in_map_grad, out_map_grad, decay_grad, scan_out)


def front(xin, params, lengths):
    (
        norm_gain,
        in_weight,
        conv_weight,
        conv_bias,
        select_weight,
        step_weight,
        step_bias,
        log_decay,
        skip_gain,
        out_weight,
    ) = params
    row_count, block_len, model_width = xin.shape
    reach_back = conv_weight.shape[0] - 1
    inner_width = conv_weight.shape[1]
    low_rank = step_weight.shape[0]
    nstate = log_decay.shape[0]
    base = lax.axis_index("seq") * block_len
    segment, resets = doc_layout(lengths, base, block_len)
    seg_ext, unused = doc_layout(lengths, base - reach_back, block_len + reach_back)
    normal_scale = lax.rsqrt(jnp.mean(xin * xin, axis=-1, keepdims=True) + eps)
    unit_rows = xin * normal_scale
    normed = (unit_rows * norm_gain.astype(jnp.float32)).astype(jnp.bfloat16)
    mixed_proj = jnp.dot(
        normed.reshape(-1, model_width), in_weight, preferred_element_type=jnp.float32
    ).astype(jnp.bfloat16)
    conv_in = mixed_proj[:, :inner_width].reshape(row_count, block_len, inner_width)
    gate_in = mixed_proj[:, inner_width:].astype(jnp.float32)
    before = shifted(conv_in[:, block_len - reach_back :], "seq", 1)
    extended = jnp.concatenate([before, conv_in], axis=1)
    conv_float = conv_weight.astype(jnp.float32)
    same_doc = [
        (seg_ext[:, offset : offset + block_len] == segment).astype(jnp.float32)[..., None]
        for offset in range(reach_back + 1)
    ]
    pre_conv = conv_bias.astype(jnp.float32) + sum(
        (
            conv_float[offset]
            * extended[:, offset : offset + block_len].astype(jnp.float32)
            * same_doc[offset]
            for offset in range(reach_back + 1)
        )
    )
    inner_act = jax.nn.silu(pre_conv).astype(jnp.bfloat16)
    selected = jnp.dot(
        inner_act.reshape(-1, inner_width), select_weight, preferred_element_type=jnp.float32
    )
    step_low = selected[:, :low_rank].astype(jnp.bfloat16)
    input_map = selected[:, low_rank : low_rank + nstate].reshape(row_count, block_len, nstate)
    output_map = selected[:, low_rank + nstate :].reshape(row_count, block_len, nstate)
    step_pre = jnp.dot(
        step_low, step_weight, preferred_element_type=jnp.float32
    ) + step_bias.astype(jnp.float32)
    step_size = jax.nn.softplus(step_pre).reshape(row_count, block_len, inner_width)
    decay_rate = -jnp.exp(log_decay.astype(jnp.float32))
    act_rows = inner_act.astype(jnp.float32)
    return (
        unit_rows,
        normal_scale,
        normed,
        gate_in,
        extended,
        same_doc,
        pre_conv,
        inner_act,
        act_rows,
        step_low,
        step_pre,
        step_size,
        input_map,
        output_map,
        resets,
        decay_rate,
    )


def entry_states(decay_rate, step_size, resets, act_rows, input_map):
    above_diag, below_diag = triangles(step_size.shape[1])
    whole_gain, end_state = lax.map(
        partial(forward_totals, decay_rate, above_diag), (step_size, resets, act_rows, input_map)
    )
    carry_in = entering_2(
        (whole_gain, end_state),
        "seq",
        chain_join,
        (jnp.ones_like(whole_gain), jnp.zeros_like(end_state)),
    )
    return carry_in[1]


def layer_forward(xin, params, lengths):
    (
        unit_rows,
        normal_scale,
        normed,
        gate_in,
        extended,
        same_doc,
        pre_conv,
        inner_act,
        act_rows,
        step_low,
        step_pre,
        step_size,
        input_map,
        output_map,
        resets,
        decay_rate,
    ) = front(xin, params, lengths)
    inner_width = act_rows.shape[2]
    start_state = entry_states(decay_rate, step_size, resets, act_rows, input_map)
    scan_out = lax.map(
        partial(forward_row, decay_rate),
        (step_size, resets, act_rows, input_map, output_map, start_state),
    )
    full_out = scan_out + params[8].astype(jnp.float32) * act_rows
    gated_out = (full_out.reshape(-1, inner_width) * jax.nn.silu(gate_in)).astype(jnp.bfloat16)
    branch = jnp.dot(gated_out, params[9], preferred_element_type=jnp.float32)
    result = xin + branch.reshape(xin.shape)
    flat_step = step_size.reshape(-1, inner_width)
    moments = jnp.stack([jnp.sum(flat_step, axis=0), jnp.sum(flat_step * flat_step, axis=0)])
    return (result, start_state, moments)


def layer_backward(xin, params, lengths, known_state, grad_out):
    (
        norm_gain,
        in_weight,
        conv_weight,
        conv_bias,
        select_weight,
        step_weight,
        step_bias,
        log_decay,
        skip_gain,
        out_weight,
    ) = params
    (
        unit_rows,
        normal_scale,
        normed,
        gate_in,
        extended,
        same_doc,
        pre_conv,
        inner_act,
        act_rows,
        step_low,
        step_pre,
        step_size,
        input_map,
        output_map,
        resets,
        decay_rate,
    ) = front(xin, params, lengths)
    row_count, block_len, model_width = xin.shape
    inner_width = act_rows.shape[2]
    reach_back = conv_weight.shape[0] - 1
    skip_float = skip_gain.astype(jnp.float32)
    grad_low = grad_out.reshape(-1, model_width).astype(jnp.bfloat16)
    d_gated = times_transposed(grad_low, out_weight)
    gate_act = jax.nn.silu(gate_in)
    d_full = (d_gated * gate_act).reshape(row_count, block_len, inner_width)
    above_diag, below_diag = triangles(block_len)
    whole_gain, back_state = lax.map(
        partial(backward_totals, decay_rate, below_diag), (step_size, resets, d_full, output_map)
    )
    leaving = entering_3(
        (whole_gain, back_state),
        "seq",
        chain_join,
        (jnp.ones_like(whole_gain), jnp.zeros_like(back_state)),
    )
    step_grad, act_grad, in_map_grad, out_map_grad, decay_grad, scan_out = lax.map(
        partial(backward_row, decay_rate),
        (step_size, resets, act_rows, input_map, output_map, known_state, leaving[1], d_full),
    )
    full_out = (scan_out + skip_float * act_rows).reshape(-1, inner_width)
    gated_out = (full_out * gate_act).astype(jnp.bfloat16)
    d_out_weight = outer_sum(gated_out, grad_low)
    d_gate = d_gated * full_out * silu_slope(gate_in)
    d_skip = jnp.sum(d_full * act_rows, axis=(0, 1))
    d_act = (act_grad + d_full * skip_float).reshape(-1, inner_width)
    d_pre = step_grad.reshape(-1, inner_width) * jax.nn.sigmoid(step_pre)
    d_step_bias = jnp.sum(d_pre, axis=0)
    d_pre_low = d_pre.astype(jnp.bfloat16)
    d_step_weight = outer_sum(step_low, d_pre_low)
    d_step_low = times_transposed(d_pre_low, step_weight)
    d_selected = jnp.concatenate(
        [
            d_step_low,
            in_map_grad.reshape(row_count * block_len, -1),
            out_map_grad.reshape(row_count * block_len, -1),
        ],
        axis=-1,
    ).astype(jnp.bfloat16)
    d_select_weight = outer_sum(inner_act.reshape(-1, inner_width), d_selected)
    d_act = d_act + times_transposed(d_selected, select_weight)
    d_conv = d_act.reshape(row_count, block_len, inner_width) * silu_slope(pre_conv)
    conv_float = conv_weight.astype(jnp.float32)
    d_extended = jnp.zeros(extended.shape, jnp.float32)
    conv_terms = []
    for offset in range(reach_back + 1):
        masked = d_conv * same_doc[offset]
        conv_terms.append(
            jnp.sum(
                masked * extended[:, offset : offset + block_len].astype(jnp.float32), axis=(0, 1)
            )
        )
        d_extended = d_extended + jnp.pad(
            masked * conv_float[offset], ((0, 0), (offset, reach_back - offset), (0, 0))
        )
    d_conv_weight = jnp.stack(conv_terms)
    d_conv_bias = jnp.sum(d_conv, axis=(0, 1))
    spill = shifted(d_extended[:, :reach_back], "seq", -1)
    d_conv_in = d_extended[:, reach_back:] + jnp.pad(
        spill, ((0, 0), (block_len - reach_back, 0), (0, 0))
    )
    d_mixed = jnp.concatenate([d_conv_in.reshape(-1, inner_width), d_gate], axis=-1).astype(
        jnp.bfloat16
    )
    d_in_weight = outer_sum(normed.reshape(-1, model_width), d_mixed)
    d_normed = times_transposed(d_mixed, in_weight).reshape(xin.shape)
    d_norm_gain = jnp.sum(d_normed * unit_rows, axis=(0, 1))
    d_unit = d_normed * norm_gain.astype(jnp.float32)
    d_input = (
        normal_scale * (d_unit - unit_rows * jnp.mean(d_unit * unit_rows, axis=-1, keepdims=True))
        + grad_out
    )
    d_log_decay = jnp.sum(decay_grad, axis=0) * decay_rate
    return (
        d_input,
        (
            d_norm_gain,
            d_in_weight,
            d_conv_weight,
            d_conv_bias,
            d_select_weight,
            d_step_weight,
            d_step_bias,
            d_log_decay,
            d_skip,
            d_out_weight,
        ),
    )


def body(
    inputs,
    doc_lengths,
    out_grad,
    norm_gain,
    in_weight,
    conv_weight,
    conv_bias,
    select_weight,
    step_weight,
    step_bias,
    log_decay,
    skip_gain,
    out_weight,
):
    params = (
        lax.all_gather(norm_gain[0], ("dp", "seq"), axis=0, tiled=True),
        lax.all_gather(in_weight[0], ("dp", "seq"), axis=0, tiled=True),
        lax.all_gather(conv_weight[0], ("dp", "seq"), axis=1, tiled=True),
        lax.all_gather(conv_bias[0], ("dp", "seq"), axis=0, tiled=True),
        lax.all_gather(select_weight[0], ("dp", "seq"), axis=0, tiled=True),
        lax.all_gather(step_weight[0], ("dp", "seq"), axis=1, tiled=True),
        lax.all_gather(step_bias[0], ("dp", "seq"), axis=0, tiled=True),
        lax.all_gather(log_decay[0], ("dp", "seq"), axis=1, tiled=True),
        lax.all_gather(skip_gain[0], ("dp", "seq"), axis=0, tiled=True),
        lax.all_gather(out_weight[0], ("dp", "seq"), axis=0, tiled=True),
    )
    first_section = lax.axis_index("section") == 0
    micro = inputs.shape[0]
    row_count, block_len, model_width = (inputs.shape[1], inputs.shape[2], inputs.shape[3])
    inner_width = conv_weight.shape[2] * lax.axis_size(("dp", "seq"))
    carried = jnp.zeros((row_count, block_len, model_width), jnp.float32)
    moments = jnp.zeros((2, inner_width), jnp.float32)
    held_in = []
    held_len = []
    held_start = []
    results = []
    for turn_index in range(micro + 1):
        fresh_rows = inputs[min(turn_index, micro - 1)].astype(jnp.float32)
        layer_in = jnp.where(first_section, fresh_rows, carried)
        lengths = jnp.where(
            first_section,
            doc_lengths[min(turn_index, micro - 1)],
            doc_lengths[max(turn_index - 1, 0)],
        )
        valid_now = jnp.where(first_section, float(turn_index < micro), float(turn_index >= 1))
        result, start_state, step_moments = layer_forward(layer_in, params, lengths)
        moments = moments + valid_now * step_moments
        held_in.append(layer_in)
        held_len.append(lengths)
        held_start.append(start_state)
        results.append(result)
        if turn_index < micro:
            carried = shifted(result, "section", 1)
    params = (
        lax.all_gather(norm_gain[0], ("dp", "seq"), axis=0, tiled=True),
        lax.all_gather(in_weight[0], ("dp", "seq"), axis=0, tiled=True),
        lax.all_gather(conv_weight[0], ("dp", "seq"), axis=1, tiled=True),
        lax.all_gather(conv_bias[0], ("dp", "seq"), axis=0, tiled=True),
        lax.all_gather(select_weight[0], ("dp", "seq"), axis=0, tiled=True),
        lax.all_gather(step_weight[0], ("dp", "seq"), axis=1, tiled=True),
        lax.all_gather(step_bias[0], ("dp", "seq"), axis=0, tiled=True),
        lax.all_gather(log_decay[0], ("dp", "seq"), axis=1, tiled=True),
        lax.all_gather(skip_gain[0], ("dp", "seq"), axis=0, tiled=True),
        lax.all_gather(out_weight[0], ("dp", "seq"), axis=0, tiled=True),
    )
    arriving = jnp.zeros((row_count, block_len, model_width), jnp.float32)
    totals = None
    in_grads = []
    for turn_index in range(micro + 1):
        source = micro - turn_index
        last_micro = micro - 1 - turn_index
        seed_grad = out_grad[max(last_micro, 0)].astype(jnp.float32) * float(last_micro >= 0)
        grad_here = jnp.where(first_section, arriving, seed_grad)
        known_state = held_start[source]
        grad_in, weight_grads = layer_backward(
            held_in[source], params, held_len[source], known_state, grad_here
        )
        totals = (
            weight_grads
            if totals is None
            else tuple((left + right for left, right in zip(totals, weight_grads)))
        )
        in_grads.append(grad_in)
        if turn_index < micro:
            arriving = shifted(grad_in.astype(jnp.bfloat16), "section", -1).astype(grad_in.dtype)
    total_tokens = micro * row_count * lax.axis_size("dp") * block_len * lax.axis_size("seq")
    reduced = (
        lax.psum_scatter(totals[0], ("dp", "seq"), scatter_dimension=0, tiled=True),
        lax.psum_scatter(totals[1], ("dp", "seq"), scatter_dimension=0, tiled=True),
        lax.psum_scatter(totals[2], ("dp", "seq"), scatter_dimension=1, tiled=True),
        lax.psum_scatter(totals[3], ("dp", "seq"), scatter_dimension=0, tiled=True),
        lax.psum_scatter(totals[4], ("dp", "seq"), scatter_dimension=0, tiled=True),
        lax.psum_scatter(totals[5], ("dp", "seq"), scatter_dimension=1, tiled=True),
        lax.psum_scatter(totals[6], ("dp", "seq"), scatter_dimension=0, tiled=True),
        lax.psum_scatter(totals[7], ("dp", "seq"), scatter_dimension=1, tiled=True),
        lax.psum_scatter(totals[8], ("dp", "seq"), scatter_dimension=0, tiled=True),
        lax.psum_scatter(totals[9], ("dp", "seq"), scatter_dimension=0, tiled=True),
        lax.psum_scatter(moments / total_tokens, ("dp", "seq"), scatter_dimension=1, tiled=True),
    )
    layer_out = jnp.stack(
        [jnp.where(first_section, results[index], results[index + 1]) for index in range(micro)]
    )
    layer_in_grad = jnp.stack(
        [
            jnp.where(first_section, in_grads[micro - index], in_grads[micro - 1 - index])
            for index in range(micro)
        ]
    )
    return (
        layer_out[None],
        layer_in_grad[None],
        reduced[0][None],
        reduced[1][None],
        reduced[2][None],
        reduced[3][None],
        reduced[4][None],
        reduced[5][None],
        reduced[6][None],
        reduced[7][None],
        reduced[8][None],
        reduced[9][None],
        reduced[10][None],
    )


def solution(mesh):
    in_specs = (
        P(None, "dp", "seq", None),
        P(None, "dp", None),
        P(None, "dp", "seq", None),
        P("section", ("dp", "seq")),
        P("section", ("dp", "seq"), None),
        P("section", None, ("dp", "seq")),
        P("section", ("dp", "seq")),
        P("section", ("dp", "seq"), None),
        P("section", None, ("dp", "seq")),
        P("section", ("dp", "seq")),
        P("section", None, ("dp", "seq")),
        P("section", ("dp", "seq")),
        P("section", ("dp", "seq"), None),
    )
    out_specs = (
        P("section", None, "dp", "seq", None),
        P("section", None, "dp", "seq", None),
        P("section", ("dp", "seq")),
        P("section", ("dp", "seq"), None),
        P("section", None, ("dp", "seq")),
        P("section", ("dp", "seq")),
        P("section", ("dp", "seq"), None),
        P("section", None, ("dp", "seq")),
        P("section", ("dp", "seq")),
        P("section", None, ("dp", "seq")),
        P("section", ("dp", "seq")),
        P("section", ("dp", "seq"), None),
        P("section", None, ("dp", "seq")),
    )
    return jax.shard_map(body, mesh=mesh, in_specs=in_specs, out_specs=out_specs, check_vma=False)
```

profile of v0, /device:TPU:0, one launch (start us, length us, event | category | flops | bytes accessed | tf_op | source)
XLA Modules:
  0.0 4145.9 jit_solution(3250406991814690686)
XLA Ops:
  20.6 44.8 %all-reduce.18 = bf16[1024]{0:T(1024)(128)(2,1)S(1)} all-reduce(bf16[1024]{0:T(1024)(128)(2,1)S(1)} %dynamic-update-slice), channel_id=5, replica_groups=mesh['section'=2,'dp'=4,'seq'=4] {'dp','seq'}, use_global_device_ids=true, to_apply=%add.18 | all-reduce | flops 1024 | bytes 4096
  65.4 36.2 all-gather.2
  101.6 44.2 %all-gather.5 = bf16[1,2048,96]{1,2,0:T(8,128)(2,1)S(1)} all-gather(bf16[1,128,96]{1,2,0:T(8,128)(2,1)} %param.56), channel_id=7, replica_groups=mesh['section'=2,'dp'=4,'seq'=4] {'dp','seq'}, dimensions={1}, use_global_device_ids=true | all-gather | bytes 417792 | tf_op jit(solution)/shard_map/all_gather | solution.py:471
  146.2 36.9 all-gather
  195.0 38.8 all-gather.6
  233.7 37.1 all-gather.1
  270.9 35.5 all-gather.7
  307.8 37.5 all-gather.10
  362.5 34.6 exponential_multiply_fusion.4
  397.1 60.5 %fusion.16 = f32[16,1,2048]{2,1,0:T(1,128)S(1)} fusion(f32[256,2048,16]{1,2,0:T(8,128)} %get-tuple-element.3576, f32[256,16,1]{0,1,2:T(8,128)S(1)} %get-tuple-element.3578), kind=kOutput, calls=%fused_computation.91 | convolution fusion | flops 100663296 | bytes 33701888 | tf_op jit(solution)/shard_map/while/body/eval_jaxpr/tnd,td,tn->nd/dot_general | solution.py:137
  552.7 110.8 %while.495 = (s32[]{:T(128)}, f32[16,16,2048]{2,1,0:T(8,128)S(1)}, f32[16,16,2048]{2,1,0:T(8,128)}, f32[16,16,16,2048]{3,2,1,0:T(8,128)}, f32[16,16,16,2048]{3,2...) while((s32[]{:T(128)}, f32[16,16,2048]{2,1,0:T(8,128)S(1)}, ...), condition=%wide.region_10.11_spmd.clone, body=%wide.region_9.10_spmd.clone.sunk | while | flops 2621443 | bytes 16777828 | solution.py:101
  665.1 26.6 while.496
  691.8 33.3 multiply_add_fusion.5
  811.0 46.2 %fusion.14 = f32[16,1,2048]{2,1,0:T(1,128)S(1)} fusion(f32[256,2048,16]{1,2,0:T(8,128)} %get-tuple-element.3574, f32[256,16,1]{0,1,2:T(8,128)S(1)} %get-tuple-element.3582), kind=kOutput, calls=%fused_computation.89 | convolution fusion | flops 100663296 | bytes 33701888 | tf_op jit(solution)/shard_map/while/body/eval_jaxpr/tnd,td,tn->nd/dot_general | solution.py:137
  968.8 110.9 %while.497 = (s32[]{:T(128)}, f32[16,16,2048]{2,1,0:T(8,128)S(1)}, f32[16,16,2048]{2,1,0:T(8,128)}, f32[16,16,16,2048]{3,2,1,0:T(8,128)}, f32[16,16,16,2048]{3,2...) while((s32[]{:T(128)}, f32[16,16,2048]{2,1,0:T(8,128)S(1)}, ...), condition=%wide.region_23.24_spmd.clone, body=%wide.region_22.23_spmd.clone.sunk | while | flops 2621443 | bytes 16777828 | solution.py:101
  1081.3 26.6 while.498
  1108.0 33.2 multiply_add_fusion.4
  1171.6 27.1 slice.491
  1283.7 27.7 slice.492
  1391.1 34.6 multiply_bitcast_fusion.2
  1425.7 46.2 %fusion.10 = bf16[16,1,2048]{2,1,0:T(2,128)(2,1)S(1)} fusion(f32[256,2048,16]{1,2,0:T(8,128)} %get-tuple-element.3570, f32[256,16,1]{0,1,2:T(8,128)S(1)} %get-tuple-element.3587), kind=kOutput, calls=%fused_computation.85 | convolution fusion | flops 100663296 | bytes 33636352 | tf_op jit(solution)/shard_map/while/body/eval_jaxpr/tnd,td,tn->nd/dot_general | solution.py:156
  1593.3 110.9 %while.502 = (s32[]{:T(128)}, f32[16,16,2048]{2,1,0:T(8,128)S(1)}, f32[16,16,2048]{2,1,0:T(8,128)}, f32[16,16,16,2048]{3,2,1,0:T(8,128)}, f32[16,16,16,2048]{3,2...) while((s32[]{:T(128)}, f32[16,16,2048]{2,1,0:T(8,128)S(1)}, ...), condition=%wide.region_42.43_spmd.clone, body=%wide.region_41.42_spmd.clone.sunk | while | flops 2621447 | bytes 16777384 | solution.py:101
  1705.7 26.7 while.503
  1732.4 33.4 multiply_add_fusion.2
  1765.8 41.2 fusion.160
  1808.5 46.1 %fusion.12 = f32[16,1,2048]{2,1,0:T(1,128)S(1)} fusion(f32[256,2048,16]{1,2,0:T(8,128)} %get-tuple-element.3572, f32[256,16,1]{0,1,2:T(8,128)S(1)} %copy-done.183), kind=kOutput, calls=%fused_computation.87 | convolution fusion | flops 100663296 | bytes 33701888 | tf_op jit(solution)/shard_map/while/body/eval_jaxpr/tnd,td,tn->nd/dot_general | solution.py:137
  1960.0 111.0 %while.499 = (s32[]{:T(128)}, f32[16,16,2048]{2,1,0:T(8,128)S(1)}, f32[16,16,2048]{2,1,0:T(8,128)}, f32[16,16,16,2048]{3,2,1,0:T(8,128)}, f32[16,16,16,2048]{3,2...) while((s32[]{:T(128)}, f32[16,16,2048]{2,1,0:T(8,128)S(1)}, ...), condition=%wide.region_36.37_spmd.clone, body=%wide.region_35.36_spmd.clone.sunk | while | flops 2621443 | bytes 16777828 | solution.py:101
  2072.5 26.7 while.500
  2099.2 33.3 multiply_add_fusion.3
  2155.9 41.3 fusion.158
  2242.8 25.7 multiply_reduce_fusion.5
  2341.7 46.2 %fusion.8 = bf16[16,1,2048]{2,1,0:T(2,128)(2,1)S(1)} fusion(f32[256,2048,16]{1,2,0:T(8,128)} %multiply_bitcast_fusion.1, f32[256,16,1]{0,1,2:T(8,128)S(1)} %copy-done.178), kind=kOutput, calls=%fused_computation.82 | convolution fusion | flops 100663296 | bytes 33636352 | tf_op jit(solution)/shard_map/while/body/eval_jaxpr/tnd,td,tn->nd/dot_general | solution.py:156
  2452.5 110.7 %while.505 = (s32[]{:T(128)}, f32[16,16,2048]{2,1,0:T(8,128)S(1)}, f32[16,16,2048]{2,1,0:T(8,128)}, f32[16,16,16,2048]{3,2,1,0:T(8,128)}, f32[16,16,16,2048]{3,2...) while((s32[]{:T(128)}, f32[16,16,2048]{2,1,0:T(8,128)S(1)}, ...), condition=%wide.region_49.50_spmd.clone, body=%wide.region_48.49_spmd.clone.sunk | while | flops 2621447 | bytes 16777384 | solution.py:101
  2564.7 26.6 while.506
  2591.4 33.5 multiply_add_fusion.1
  2678.1 41.3 fusion.156
  2719.6 41.4 fusion.154
  2803.2 46.2 %fusion.6 = bf16[16,1,2048]{2,1,0:T(2,128)(2,1)S(1)} fusion(f32[256,2048,16]{1,2,0:T(8,128)} %multiply_bitcast_fusion, f32[256,16,1]{0,1,2:T(8,128)S(1)} %copy-done.176), kind=kOutput, calls=%fused_computation.79 | convolution fusion | flops 100663296 | bytes 33636352 | tf_op jit(solution)/shard_map/while/body/eval_jaxpr/tnd,td,tn->nd/dot_general | solution.py:156
  2929.0 110.8 %while.508 = (s32[]{:T(128)}, f32[16,16,2048]{2,1,0:T(8,128)S(1)}, f32[16,16,2048]{2,1,0:T(8,128)}, f32[16,16,16,2048]{3,2,1,0:T(8,128)}, f32[16,16,16,2048]{3,2...) while((s32[]{:T(128)}, f32[16,16,2048]{2,1,0:T(8,128)S(1)}, ...), condition=%wide.region_56.57_spmd.clone, body=%wide.region_55.56_spmd.clone.sunk | while | flops 2621447 | bytes 16777384 | solution.py:101
  3041.4 26.6 while.509
  3068.0 33.4 multiply_add_fusion
  3154.8 41.2 fusion.150
  3196.7 41.4 fusion.152
  3252.7 72.4 %multiply_reduce_fusion.1 = (f32[2048,16]{0,1:T(8,128)}, f32[2048,16]{0,1:T(8,128)}, f32[2048,16]{0,1:T(8,128)}) fusion(f32[2048,256]{0,1:T(8,128)} %get-tuple-element.3556, f32[256]{0:T(256)S(1)} %copy-done.256, f32[256,2048]{1,0:T(8,128)} %get-tuple-element.3562, f32[16,2048]{1,0:T(8,128)S(1)} %copy-done.39, f32[255,16,2048]{2,1,0:T(8,128)} %slice.500, ...), kind=kLoop, calls=%fused_computation.76 | loop fusion | flops 176062464 | bytes 214436864 | tf_op jit(solution)/shard_map/while/body/eval_jaxpr/tnd,td->nd/dot_general | solution.py:198
  3402.2 72.2 %all-reduce.23 = (f32[1024]{0:T(1024)S(1)}, f32[2048]{0:T(1024)S(1)}, f32[2048]{0:T(1024)S(1)}, f32[2048]{0:T(1024)S(1)}) all-reduce(f32[1024]{0:T(1024)S(1)} %add_add_fusion.5, f32[2048]{0:T(1024)S(1)} %add_add_fusion.4, f32[2048]{0:T(1024)S(1)} %add_add_fusion.3, ...), channel_id=24, replica_groups=mesh['section'=2,'dp'=4,'seq'=4] {'dp','seq'}, use_global_device_ids=true, to_apply=%region_63.64.clone | all-reduce | flops 7168 | bytes 57344
  3482.5 121.9 %reduce-scatter.14.cloned.1.call-done = f32[128,96]{0,1:T(8,128)} async-done(((f32[2048,96]{0,1:T(8,128)}), f32[128,96]{0,1:T(8,128)}) %reduce-scatter.14.cloned.1.call-update) | async-done | bytes 49168 | tf_op jit(solution)/shard_map/reduce_scatter | solution.py:543
  3604.5 184.3 %reduce-scatter.20.cloned.1.call-done = f32[128,1024]{1,0:T(8,128)} async-done(((f32[2048,1024]{1,0:T(8,128)}), f32[128,1024]{1,0:T(8,128)}) %reduce-scatter.20.cloned.1.call-update) | async-done | bytes 524304 | tf_op jit(solution)/shard_map/reduce_scatter | solution.py:548
  3788.7 350.5 %reduce-scatter.12.cloned.1.call-done = f32[64,4096]{1,0:T(8,128)} async-done(((f32[1024,4096]{1,0:T(8,128)}), f32[64,4096]{1,0:T(8,128)}) %reduce-scatter.12.cloned.1.call-update) | async-done | bytes 1048592 | tf_op jit(solution)/shard_map/reduce_scatter | solution.py:540
  (1333 shorter events, 2128.5 us)
Async XLA Ops:
  7.2 177.2 %copy-start.98 = (bf16[2,1,256,1024]{3,2,1,0:T(8,128)(2,1)S(1)}, bf16[2,1,256,1024]{3,2,1,0:T(8,128)(2,1)}, u32[]{:S(2)}) copy-start(bf16[2,1,256,1024]{3,2,1,0:T(8,128)(2,1)} %param.49) | copy-start | bytes 3145732
  7.2 139.0 %copy-start.301 = (bf16[1,16,128]{2,1,0:T(8,128)(2,1)S(1)}, bf16[1,16,128]{2,1,0:T(8,128)(2,1)}, u32[]{:S(2)}) copy-start(bf16[1,16,128]{2,1,0:T(8,128)(2,1)} %param.59) | copy-start | bytes 12292
  7.2 177.2 %all-gather.25.cloned.1.call-start = ((), (), s32[]{:S(2)}) async-start(), calls=%async_computation.12 | async-start | bytes 8912896 | tf_op jit(solution)/shard_map/all_gather | solution.py:468
  7.9 742.7 %all-gather.27.cloned.1.call-start = ((), (), s32[]{:S(2)}) async-start(), calls=%async_computation.13 | async-start | bytes 4456448 | tf_op jit(solution)/shard_map/all_gather | solution.py:476
  8.7 3384.4 %reduce-scatter.24.cloned.1.call-start = ((), (), s32[]{:S(2)}) async-start(), calls=%async_computation.15 | async-start | bytes 1114112
  12.0 134.0 %copy-start.302 = (f32[256]{0:T(256)}, f32[256]{0:T(256)S(1)}, u32[]{:S(2)}) copy-start(f32[256]{0:T(256)S(1)} %get-tuple-element.3259) | copy-start | bytes 3076
  17.8 172.5 %copy-start.266 = (f32[256]{0:T(256)}, f32[256]{0:T(256)S(1)}, u32[]{:S(2)}) copy-start(f32[256]{0:T(256)S(1)} %add_rsqrt_fusion.2) | copy-start | bytes 3076
  65.4 124.8 %copy-start.147 = (f32[1024]{0:T(1024)}, f32[1024]{0:T(1024)S(1)}, u32[]{:S(2)}) copy-start(f32[1024]{0:T(1024)S(1)} %convert_element_type.764) | copy-start | bytes 12292
  101.6 244.8 %copy-start.195 = (f32[1,1,2048]{2,1,0:T(1,128)}, f32[1,1,2048]{2,1,0:T(1,128)S(1)}, u32[]{:S(2)}) copy-start(f32[1,1,2048]{2,1,0:T(1,128)S(1)} %get-tuple-element.3597) | copy-start | bytes 24580
  101.6 244.8 %copy-start.201 = (f32[1,1,2048]{2,1,0:T(1,128)}, f32[1,1,2048]{2,1,0:T(1,128)S(1)}, u32[]{:S(2)}) copy-start(f32[1,1,2048]{2,1,0:T(1,128)S(1)} %get-tuple-element.3598) | copy-start | bytes 24580
  101.6 244.8 %copy-start.206 = (f32[1,1,2048]{2,1,0:T(1,128)}, f32[1,1,2048]{2,1,0:T(1,128)S(1)}, u32[]{:S(2)}) copy-start(f32[1,1,2048]{2,1,0:T(1,128)S(1)} %get-tuple-element.3599) | copy-start | bytes 24580
  101.6 244.8 %copy-start.211 = (f32[1,1,2048]{2,1,0:T(1,128)}, f32[1,1,2048]{2,1,0:T(1,128)S(1)}, u32[]{:S(2)}) copy-start(f32[1,1,2048]{2,1,0:T(1,128)S(1)} %get-tuple-element.3600) | copy-start | bytes 24580
  145.9 206.0 %copy-start.103 = (bf16[1,2048,96]{1,2,0:T(8,128)(2,1)}, bf16[1,2048,96]{1,2,0:T(8,128)(2,1)S(1)}, u32[]{:S(2)}) copy-start(bf16[1,2048,96]{1,2,0:T(8,128)(2,1)S(1)} %all-gather.5) | copy-start | bytes 1179652
  145.9 216.6 %copy-start.257 = (f32[256]{0:T(256)}, f32[256]{0:T(256)S(1)}, u32[]{:S(2)}) copy-start(f32[256]{0:T(256)S(1)} %broadcast_subtract_fusion.2) | copy-start | bytes 3076
  183.0 289.4 %copy-start.129 = (bf16[1,16,2048]{2,1,0:T(8,128)(2,1)}, bf16[1,16,2048]{2,1,0:T(8,128)(2,1)S(1)}, u32[]{:S(2)}) copy-start(bf16[1,16,2048]{2,1,0:T(8,128)(2,1)S(1)} %all-gather) | copy-start | bytes 196612
  183.7 751.1 %copy-start.37 = (f32[16,2048]{1,0:T(8,128)}, f32[16,2048]{1,0:T(8,128)S(1)}, u32[]{:S(2)}) copy-start(f32[16,2048]{1,0:T(8,128)S(1)} %get-tuple-element.3596) | copy-start | bytes 393220
  183.8 162.6 %copy-start.285 = (f32[1,256]{1,0:T(1,128)}, f32[1,256]{1,0:T(1,128)S(1)}, u32[]{:S(2)}) copy-start(f32[1,256]{1,0:T(1,128)S(1)} %get-tuple-element.3609) | copy-start | bytes 3076
  183.8 162.6 %copy-start.286 = (f32[1,256]{1,0:T(1,128)}, f32[1,256]{1,0:T(1,128)S(1)}, u32[]{:S(2)}) copy-start(f32[1,256]{1,0:T(1,128)S(1)} %get-tuple-element.3610) | copy-start | bytes 3076
  183.8 162.6 %copy-start.287 = (f32[1,256]{1,0:T(1,128)}, f32[1,256]{1,0:T(1,128)S(1)}, u32[]{:S(2)}) copy-start(f32[1,256]{1,0:T(1,128)S(1)} %get-tuple-element.3611) | copy-start | bytes 3076
  183.8 162.6 %copy-start.288 = (f32[1,256]{1,0:T(1,128)}, f32[1,256]{1,0:T(1,128)S(1)}, u32[]{:S(2)}) copy-start(f32[1,256]{1,0:T(1,128)S(1)} %get-tuple-element.3612) | copy-start | bytes 3076
  190.3 117.5 %copy-start.324 = (bf16[1,128]{1,0:T(2,128)(2,1)S(1)}, bf16[1,128]{1,0:T(2,128)(2,1)}, u32[]{:S(2)}) copy-start(bf16[1,128]{1,0:T(2,128)(2,1)} %param.60) | copy-start | bytes 772
  191.6 154.8 %collective-permute-start = (bf16[1,3,2048]{2,1,0:T(4,128)(2,1)S(1)}, bf16[1,3,2048]{2,1,0:T(4,128)(2,1)S(1)}, u32[]{:S(2)}, u32[]{:S(2)}) collective-permute-start(bf16[1,3,2048]{2,1,0:T(4,128)(2,1)S(1)} %slice.438), channel_id=1, source_target_pairs={{0,1},{1,2},{2,3},{4,5},{5,6},{6,7},{8,9},{9,10},{10,11},{12,13},{... | collective-permute-start | bytes 36872 | tf_op jit(solution)/shard_map/ppermute | solution.py:15
  233.7 119.2 %copy-start.59 = (bf16[1,64,2048]{2,1,0:T(8,128)(2,1)}, bf16[1,64,2048]{2,1,0:T(8,128)(2,1)S(1)}, u32[]{:S(2)}) copy-start(bf16[1,64,2048]{2,1,0:T(8,128)(2,1)S(1)} %all-gather.6) | copy-start | bytes 786436
  353.0 338.7 %copy-start.175 = (f32[256,16,1]{0,1,2:T(8,128)}, f32[256,16,1]{0,1,2:T(8,128)S(1)}, u32[]{:S(2)}) copy-start(f32[256,16,1]{0,1,2:T(8,128)S(1)} %get-tuple-element.3579) | copy-start | bytes 49156
  362.4 110.0 %copy-start.216 = (f32[2048]{0:T(1024)}, f32[2048]{0:T(1024)S(1)}, u32[]{:S(2)}) copy-start(f32[2048]{0:T(1024)S(1)} %get-tuple-element.3563) | copy-start | bytes 24580
  754.5 3.6 collective-permute-start.1
  765.9 5.4 collective-permute-start.2
  777.4 330.5 %copy-start.177 = (f32[256,16,1]{0,1,2:T(8,128)}, f32[256,16,1]{0,1,2:T(8,128)S(1)}, u32[]{:S(2)}) copy-start(f32[256,16,1]{0,1,2:T(8,128)S(1)} %get-tuple-element.3583) | copy-start | bytes 49156
  786.4 87.0 %copy-start.218 = (f32[2048]{0:T(1024)}, f32[2048]{0:T(1024)S(1)}, u32[]{:S(2)}) copy-start(f32[2048]{0:T(1024)S(1)} %get-tuple-element.3560) | copy-start | bytes 24580
  1168.7 91.1 %collective-permute-start.3 = (f32[1,256,1024]{2,1,0:T(8,128)S(1)}, f32[1,256,1024]{2,1,0:T(8,128)S(1)}, u32[]{:S(2)}, u32[]{:S(2)}) collective-permute-start(f32[1,256,1024]{2,1,0:T(8,128)S(1)} %fusion.179), channel_id=1, source_target_pairs={{0,16},{1,17},{2,18},{3,19},{4,20},{5,21},{6,22},{7,23},{8,24},{9,... | collective-permute-start | bytes 3145736 | tf_op jit(solution)/shard_map/ppermute | solution.py:15
  1171.5 180.1 %copy-start.309 = (f32[1,256]{1,0:T(1,128)}, f32[1,256]{1,0:T(1,128)S(1)}, u32[]{:S(2)}) copy-start(f32[1,256]{1,0:T(1,128)S(1)} %get-tuple-element.3601) | copy-start | bytes 3076
  1171.5 180.1 %copy-start.311 = (f32[1,256]{1,0:T(1,128)}, f32[1,256]{1,0:T(1,128)S(1)}, u32[]{:S(2)}) copy-start(f32[1,256]{1,0:T(1,128)S(1)} %get-tuple-element.3602) | copy-start | bytes 3076
  1171.5 180.1 %copy-start.313 = (f32[1,256]{1,0:T(1,128)}, f32[1,256]{1,0:T(1,128)S(1)}, u32[]{:S(2)}) copy-start(f32[1,256]{1,0:T(1,128)S(1)} %get-tuple-element.3603) | copy-start | bytes 3076
  1171.5 180.1 %copy-start.315 = (f32[1,256]{1,0:T(1,128)}, f32[1,256]{1,0:T(1,128)S(1)}, u32[]{:S(2)}) copy-start(f32[1,256]{1,0:T(1,128)S(1)} %get-tuple-element.3604) | copy-start | bytes 3076
  1266.7 85.0 %copy-start.140 = (bf16[256,4096]{1,0:T(8,128)(2,1)}, bf16[256,4096]{1,0:T(8,128)(2,1)S(1)}, u32[]{:S(2)}) copy-start(bf16[256,4096]{1,0:T(8,128)(2,1)S(1)} %fusion.36) | copy-start | bytes 6291460
  1266.8 84.8 %collective-permute-start.4 = (bf16[1,3,2048]{2,1,0:T(4,128)(2,1)S(1)}, bf16[1,3,2048]{2,1,0:T(4,128)(2,1)S(1)}, u32[]{:S(2)}, u32[]{:S(2)}) collective-permute-start(bf16[1,3,2048]{2,1,0:T(4,128)(2,1)S(1)} %slice.475), channel_id=1, source_target_pairs={{0,1},{1,2},{2,3},{4,5},{5,6},{6,7},{8,9},{9,10},{10,11},{12,13},{... | collective-permute-start | bytes 36872 | tf_op jit(solution)/shard_map/ppermute | solution.py:15
  1372.3 113.8 %copy-start.220 = (f32[2048]{0:T(1024)}, f32[2048]{0:T(1024)S(1)}, u32[]{:S(2)}) copy-start(f32[2048]{0:T(1024)S(1)} %get-tuple-element.3557) | copy-start | bytes 24580
  2279.5 6.1 collective-permute-start.5
  2290.7 6.7 collective-permute-start.6
  2297.4 1183.6 %reduce-scatter.22.cloned.1.call-start = ((), (), s32[]{:S(2)}) async-start(), calls=%async_computation.14 | async-start | bytes 1114112
  2769.8 6.1 collective-permute-start.7
  2780.9 4.1 collective-permute-start.8
  3252.6 229.9 %reduce-scatter.18.cloned.1.call-start = ((), (), s32[]{:S(2)}) async-start(), calls=%async_computation.10 | async-start | bytes 139264 | tf_op jit(solution)/shard_map/reduce_scatter | solution.py:546
  3327.0 155.6 %reduce-scatter.16.cloned.1.call-start = ((), (), s32[]{:S(2)}) async-start(), calls=%async_computation.9 | async-start | bytes 557056 | tf_op jit(solution)/shard_map/reduce_scatter | solution.py:544
  3329.6 274.8 %reduce-scatter.14.cloned.1.call-start = ((), (), s32[]{:S(2)}) async-start(), calls=%async_computation.8 | async-start | bytes 835584 | tf_op jit(solution)/shard_map/reduce_scatter | solution.py:543
  3331.6 457.1 %reduce-scatter.20.cloned.1.call-start = ((), (), s32[]{:S(2)}) async-start(), calls=%async_computation.11 | async-start | bytes 8912896 | tf_op jit(solution)/shard_map/reduce_scatter | solution.py:548
  3339.7 799.6 %reduce-scatter.12.cloned.1.call-start = ((), (), s32[]{:S(2)}) async-start(), calls=%async_computation.7 | async-start | bytes 17825792 | tf_op jit(solution)/shard_map/reduce_scatter | solution.py:540
  3359.2 5.8 collective-permute-start.9
  (320 other events, 5002.3 us)
Sparse Core Ops, SparseCore 0:
  10.8 120.2 all-gather.24
  133.9 76.7 all-gather.26
  2297.5 76.5 reduce-scatter.23
  3252.7 76.1 reduce-scatter.21
  3331.6 72.3 reduce-scatter.17
  3406.8 73.5 reduce-scatter.15
  3485.6 118.7 reduce-scatter.13
  3607.3 181.3 reduce-scatter.19
  3791.6 347.5 reduce-scatter.11
where the time goes:
time: 4150 us
  other arithmetic  1550 us (37%)
  matrix products  838 us (20%)
  waiting for transfers between devices  669 us (16%)
  blocking collectives  559 us (13%)
  local copies, waits for them, and re-layouts  491 us (12%)
    dynamic_update_slice x96, other arithmetic, stepper(): products = lax.dynamic_update_index_in_dim(products, product, place, 1)  665 us
    reduce_scatter x1, waiting for transfers between devices, body(): lax.psum_scatter(totals[1], ('dp', 'seq'), scatter_dimension=0, tiled=True)  351 us
    add x6, other arithmetic, chained(): states = totals + products * entering[:, None]  200 us
    reduce_scatter x1, waiting for transfers between devices, body(): lax.psum_scatter(totals[9], ('dp', 'seq'), scatter_dimension=0, tiled=True)  184 us
    dot_general x3, matrix products, forward_totals(): jnp.einsum('tnd,td,tn->nd', reach_rate, clear_after * step_size * act_row...  153 us
    another operation x21, local copies, waits for them, and re-layouts  145 us
    dot_general x3, matrix products, backward_totals(): jnp.einsum('tnd,td,tn->nd', reach_rate, clear_upto * scan_grad, output_ma...  139 us
    dot_general x3, matrix products, backward_row(): jnp.einsum('tnd,td->tn', states, scan_grad, precision=highest)  124 us
  transfers between devices with their start and end apart: 19, of which 8 were waited for; matrix products, arithmetic and copies ran while one was open for 39% of the time, Pallas kernels for 0%

commit v1 on v0

v1 whole, which is shorter than its diff:
```python
import functools
import math

import jax
import jax.numpy as jnp
from jax import lax
from jax.experimental import pallas as pl
from jax.experimental.pallas import tpu as pltpu
from jax.sharding import PartitionSpec as P

EPS = 1e-05
LOG2E = math.log2(math.e)
LN2 = math.log(2.0)
CUT = 1e30
LANES = 128
CHUNKS = 8
VMEM_LIMIT = 60 * 1024 * 1024
F32 = jnp.float32
BF16 = jnp.bfloat16
HIGHEST = lax.Precision.HIGHEST


def silu_slope(values):
    sigma = jax.nn.sigmoid(values)
    return sigma * (1.0 + values * (1.0 - sigma))


def interleave(rows):
    count = rows.shape[0]
    return rows.reshape(CHUNKS, count // CHUNKS, -1).swapaxes(0, 1).reshape(count, -1)


def in_order(rows):
    count = rows.shape[0]
    return rows.reshape(count // CHUNKS, CHUNKS, -1).swapaxes(0, 1).reshape(count, -1)


def column_params(**kw):
    return pltpu.CompilerParams(
        dimension_semantics=("arbitrary",), vmem_limit_bytes=VMEM_LIMIT, **kw
    )


def cols(rows, width=LANES):
    return pl.BlockSpec((rows, width), lambda j: (0, j))


def whole(*shape):
    return pl.BlockSpec(shape, lambda j: (0,) * len(shape))


def conv_taps(conv_ref, halo_ref, steps, reach):
    width = conv_ref.shape[1]
    own = conv_ref[...].astype(F32).reshape(steps, CHUNKS, width)
    tail = own[steps - reach :]
    moved = pltpu.roll(tail.reshape(reach * CHUNKS, width), 1, 0).reshape(reach, CHUNKS, width)
    first = lax.broadcasted_iota(jnp.int32, moved.shape, 1) == 0
    halo = halo_ref[...].astype(F32)[:, None, :]
    head = jnp.where(first, jnp.broadcast_to(halo, moved.shape), moved)
    return jnp.concatenate([head, own], axis=0)


def select_kernel(conv_ref, halo_ref, same_ref, small_ref, sel_ref, act_ref, pre_ref, out_ref, acc):
    j = pl.program_id(0)
    count, width = conv_ref.shape
    reach = halo_ref.shape[0]
    steps = count // CHUNKS
    ext = conv_taps(conv_ref, halo_ref, steps, reach)
    pre = jnp.broadcast_to(small_ref[reach + 1 : reach + 2, :], (count, width)).reshape(
        steps, CHUNKS, width
    )
    for k in range(reach + 1):
        weight = small_ref[k : k + 1, :]
        same = same_ref[k][:, :, None]
        pre = pre + (weight[None] * ext[k : k + steps]) * same
    pre = pre.reshape(count, width)
    pre_ref[...] = pre
    act = (pre * jax.nn.sigmoid(pre)).astype(BF16)
    act_ref[...] = act

    @pl.when(j == 0)
    def _():
        acc[...] = jnp.zeros_like(acc)

    acc[...] += lax.dot_general(
        act, sel_ref[...], (((1,), (1,)), ((), ())), preferred_element_type=F32
    )
    out_ref[...] = acc[...]


def select_call(conv_in, halo, same, small, sel):
    count, inner = conv_in.shape
    width = min(512, inner)
    wide = sel.shape[0]
    return pl.pallas_call(
        select_kernel,
        grid=(inner // width,),
        in_specs=[
            cols(count, width),
            cols(halo.shape[0], width),
            whole(*same.shape),
            cols(small.shape[0], width),
            cols(wide, width),
        ],
        out_specs=[cols(count, width), cols(count, width), whole(count, wide)],
        out_shape=[
            jax.ShapeDtypeStruct((count, inner), BF16),
            jax.ShapeDtypeStruct((count, inner), F32),
            jax.ShapeDtypeStruct((count, wide), F32),
        ],
        scratch_shapes=[pltpu.VMEM((count, wide), F32)],
        compiler_params=column_params(),
        name="conv_select",
    )(conv_in, halo, same, small, sel)


def spread(dst, src_ref, nstate):
    for n in range(nstate):
        dst[n] = jnp.broadcast_to(src_ref[:, n : n + 1], dst.shape[1:])


def chunk_links(ends, sums, rates, backward):
    row = lax.broadcasted_iota(jnp.int32, (CHUNKS, LANES), 0)
    gains = [jnp.exp2(sums * rate) for rate in rates]
    ends = list(ends)
    total = sums
    k = 1
    while k < CHUNKS:
        turn = CHUNKS - k if backward else k
        mask = row < CHUNKS - k if backward else row >= k
        ends = [
            jnp.where(mask, g * pltpu.roll(e, turn, 0) + e, e) for g, e in zip(gains, ends)
        ]
        gains = [jnp.where(mask, g * pltpu.roll(g, turn, 0), g) for g in gains]
        total = jnp.where(mask, pltpu.roll(total, turn, 0) + total, total)
        k *= 2
    turn = CHUNKS - 1 if backward else 1
    mask = row < CHUNKS - 1 if backward else row >= 1
    entering = [jnp.where(mask, pltpu.roll(e, turn, 0), 0.0) for e in ends]
    before = jnp.where(mask, pltpu.roll(total, turn, 0), 0.0)
    last = 0 if backward else CHUNKS - 1
    return entering, [e[last : last + 1] for e in ends], before, total[last : last + 1]


def rate_rows(rate_ref, nstate):
    return [jnp.broadcast_to(rate_ref[n : n + 1, :], (CHUNKS, LANES)) for n in range(nstate)]


def forward_totals_kernel(
    low_ref, stepw_ref, small_ref, act_ref, in_ref, cut_ref, rate_ref,
    step_ref, sig_ref, enter_ref, total_ref, before_ref, sum_ref, moment_ref, inb,
):
    count = act_ref.shape[0]
    nstate = rate_ref.shape[0]

    @pl.when(pl.program_id(0) == 0)
    def _():
        spread(inb, in_ref, nstate)

    pre = jnp.dot(low_ref[...], stepw_ref[...], preferred_element_type=F32) + small_ref[5:6, :]
    near = jnp.exp(-jnp.abs(pre))
    step_all = jnp.maximum(pre, 0.0) + jnp.log1p(near)
    step_ref[...] = step_all
    sig_ref[...] = jnp.where(pre >= 0.0, 1.0, near) / (1.0 + near)
    moment_ref[0:1, :] = jnp.sum(step_all, axis=0, keepdims=True)
    moment_ref[1:2, :] = jnp.sum(step_all * step_all, axis=0, keepdims=True)
    rates = rate_rows(rate_ref, nstate)

    def body(pair, carry):
        states, sums = carry
        act = act_ref[pl.ds(pl.multiple_of(pair * 16, 16), 16), :].astype(F32)
        for half in (0, 1):
            at = pl.ds(pl.multiple_of(pair * 16 + half * 8, 8), 8)
            step = step_ref[at, :]
            away = step + cut_ref[at, :]
            drive = step * act[half * 8 : half * 8 + 8]
            sums = sums + away
            states = tuple(
                jnp.exp2(away * rates[n]) * states[n] + drive * inb[n, at, :]
                for n in range(nstate)
            )
        return states, sums

    zero = jnp.zeros((CHUNKS, LANES), F32)
    ends, sums = lax.fori_loop(0, count // 16, body, ((zero,) * nstate, zero))
    entering, totals, before, total = chunk_links(ends, sums, rates, False)
    for n in range(nstate):
        enter_ref[n] = entering[n]
        total_ref[n : n + 1, :] = totals[n].astype(total_ref.dtype)
    before_ref[...] = before
    sum_ref[...] = total


def forward_totals(low, stepw, small, act, in_map, cut, rate):
    count, inner = act.shape
    nstate = rate.shape[0]
    return pl.pallas_call(
        forward_totals_kernel,
        grid=(inner // LANES,),
        in_specs=[
            whole(*low.shape),
            cols(stepw.shape[0]),
            cols(small.shape[0]),
            cols(count),
            whole(count, nstate),
            whole(count, LANES),
            cols(nstate),
        ],
        out_specs=[
            cols(count),
            cols(count),
            pl.BlockSpec((nstate, CHUNKS, LANES), lambda j: (0, 0, j)),
            cols(nstate),
            cols(CHUNKS),
            cols(1),
            cols(2),
        ],
        out_shape=[
            jax.ShapeDtypeStruct((count, inner), F32),
            jax.ShapeDtypeStruct((count, inner), F32),
            jax.ShapeDtypeStruct((nstate, CHUNKS, inner), F32),
            jax.ShapeDtypeStruct((nstate, inner), BF16),
            jax.ShapeDtypeStruct((CHUNKS, inner), F32),
            jax.ShapeDtypeStruct((1, inner), F32),
            jax.ShapeDtypeStruct((2, inner), F32),
        ],
        scratch_shapes=[pltpu.VMEM((nstate, count, LANES), F32)],
        compiler_params=column_params(),
        name="forward_totals",
    )(low, stepw, small, act, in_map, cut, rate)


def arriving_state(me, totals_ref, sums_ref, rate_ref, backward):
    devices = totals_ref.shape[0]
    state = jnp.zeros(rate_ref.shape, F32)
    order = range(devices - 1, 0, -1) if backward else range(devices - 1)
    for k in order:
        new = jnp.exp2(rate_ref[...] * sums_ref[k]) * state + totals_ref[k].astype(F32)
        state = jnp.where((k > me) if backward else (k < me), new, state)
    return state


def forward_states_kernel(
    me_ref, step_ref, act_ref, gate_ref, in_ref, outm_ref, cut_ref, rate_ref, small_ref,
    enter_ref, before_ref, totals_ref, sums_ref,
    full_ref, gated_ref, keep_ref, inb, outb,
):
    count = act_ref.shape[0]
    nstate = rate_ref.shape[0]

    @pl.when(pl.program_id(0) == 0)
    def _():
        spread(inb, in_ref, nstate)
        spread(outb, outm_ref, nstate)

    rates = rate_rows(rate_ref, nstate)
    arrived = arriving_state(me_ref[0], totals_ref, sums_ref, rate_ref, False)
    before = before_ref[...]
    states = []
    for n in range(nstate):
        state = enter_ref[n] + jnp.exp2(before * rates[n]) * arrived[n : n + 1, :]
        keep_ref[0, n, 0:CHUNKS, :] = state
        states.append(state)
    skip = jnp.broadcast_to(small_ref[6:7, :], (CHUNKS, LANES))

    def body(pair, states):
        rows = pl.ds(pl.multiple_of(pair * 16, 16), 16)
        act = act_ref[rows, :].astype(F32)
        fulls = []
        for half in (0, 1):
            at = pl.ds(pl.multiple_of(pair * 16 + half * 8, 8), 8)
            after = pl.ds(pl.multiple_of(pair * 16 + half * 8 + 8, 8), 8)
            step = step_ref[at, :]
            away = step + cut_ref[at, :]
            act_now = act[half * 8 : half * 8 + 8]
            drive = step * act_now
            out = skip * act_now
            new = []
            for n in range(nstate):
                state = jnp.exp2(away * rates[n]) * states[n] + drive * inb[n, at, :]
                keep_ref[0, n, after, :] = state
                out = out + state * outb[n, at, :]
                new.append(state)
            states = tuple(new)
            fulls.append(out)
        full = jnp.concatenate(fulls, axis=0)
        full_ref[rows, :] = full
        gate = gate_ref[rows, :].astype(F32)
        gated_ref[rows, :] = (full * (gate * jax.nn.sigmoid(gate))).astype(BF16)
        return states

    lax.fori_loop(0, count // 16, body, tuple(states))


def forward_states(me, step, act, mixed, in_map, out_map, cut, rate, small, enter, before, totals, sums):
    count, inner = act.shape
    nstate = rate.shape[0]
    devices = totals.shape[0]
    blocks = inner // LANES
    return pl.pallas_call(
        forward_states_kernel,
        grid=(blocks,),
        in_specs=[
            pl.BlockSpec(memory_space=pltpu.SMEM),
            cols(count),
            cols(count),
            pl.BlockSpec((count, LANES), lambda j: (0, j + blocks)),
            whole(count, nstate),
            whole(count, nstate),
            whole(count, LANES),
            cols(nstate),
            cols(small.shape[0]),
            pl.BlockSpec((nstate, CHUNKS, LANES), lambda j: (0, 0, j)),
            cols(CHUNKS),
            pl.BlockSpec((devices, nstate, LANES), lambda j: (0, 0, j)),
            pl.BlockSpec((devices, 1, LANES), lambda j: (0, 0, j)),
        ],
        out_specs=[
            cols(count),
            cols(count),
            pl.BlockSpec((1, nstate, count + CHUNKS, LANES), lambda j: (j, 0, 0, 0)),
        ],
        out_shape=[
            jax.ShapeDtypeStruct((count, inner), F32),
            jax.ShapeDtypeStruct((count, inner), BF16),
            jax.ShapeDtypeStruct((blocks, nstate, count + CHUNKS, LANES), F32),
        ],
        scratch_shapes=[pltpu.VMEM((nstate, count, LANES), F32)] * 2,
        compiler_params=column_params(),
        name="forward_states",
    )(me, step, act, mixed, in_map, out_map, cut, rate, small, enter, before, totals, sums)


def backward_totals_kernel(
    dgated_ref, gate_ref, full_ref, act_ref, step_ref, outm_ref, cut_ref, rate_ref,
    dfull_ref, dgate_ref, gskip_ref, enter_ref, total_ref, before_ref, sum_ref, outb,
):
    count = act_ref.shape[0]
    nstate = rate_ref.shape[0]
    pairs = count // 16

    @pl.when(pl.program_id(0) == 0)
    def _():
        spread(outb, outm_ref, nstate)

    rates = rate_rows(rate_ref, nstate)

    def body(turn, carry):
        states, sums, gskip = carry
        pair = pairs - 1 - turn
        rows = pl.ds(pl.multiple_of(pair * 16, 16), 16)
        act = act_ref[rows, :].astype(F32)
        gate = gate_ref[rows, :].astype(F32)
        sigma = jax.nn.sigmoid(gate)
        dgated = dgated_ref[rows, :]
        dfull = dgated * (gate * sigma)
        dfull_ref[rows, :] = dfull
        slope = sigma * (1.0 + gate * (1.0 - sigma))
        dgate_ref[rows, :] = (dgated * full_ref[rows, :] * slope).astype(BF16)
        both = dfull * act
        gskip = gskip + both[0:8] + both[8:16]
        for half in (1, 0):
            at = pl.ds(pl.multiple_of(pair * 16 + half * 8, 8), 8)
            away = step_ref[at, :] + cut_ref[at, :]
            grad = dfull[half * 8 : half * 8 + 8]
            sums = sums + away
            states = tuple(
                jnp.exp2(away * rates[n]) * (states[n] + outb[n, at, :] * grad)
                for n in range(nstate)
            )
        return states, sums, gskip

    zero = jnp.zeros((CHUNKS, LANES), F32)
    ends, sums, gskip = lax.fori_loop(0, pairs, body, ((zero,) * nstate, zero, zero))
    gskip_ref[...] = jnp.sum(gskip, axis=0, keepdims=True)
    entering, totals, before, total = chunk_links(ends, sums, rates, True)
    for n in range(nstate):
        enter_ref[n] = entering[n]
        total_ref[n : n + 1, :] = totals[n].astype(total_ref.dtype)
    before_ref[...] = before
    sum_ref[...] = total


def backward_totals(dgated, mixed, full, act, step, out_map, cut, rate):
    count, inner = act.shape
    nstate = rate.shape[0]
    blocks = inner // LANES
    return pl.pallas_call(
        backward_totals_kernel,
        grid=(blocks,),
        in_specs=[
            cols(count),
            pl.BlockSpec((count, LANES), lambda j: (0, j + blocks)),
            cols(count),
            cols(count),
            cols(count),
            whole(count, nstate),
            whole(count, LANES),
            cols(nstate),
        ],
        out_specs=[
            cols(count),
            cols(count),
            cols(1),
            pl.BlockSpec((nstate, CHUNKS, LANES), lambda j: (0, 0, j)),
            cols(nstate),
            cols(CHUNKS),
            cols(1),
        ],
        out_shape=[
            jax.ShapeDtypeStruct((count, inner), F32),
            jax.ShapeDtypeStruct((count, inner), BF16),
            jax.ShapeDtypeStruct((1, inner), F32),
            jax.ShapeDtypeStruct((nstate, CHUNKS, inner), F32),
            jax.ShapeDtypeStruct((nstate, inner), BF16),
            jax.ShapeDtypeStruct((CHUNKS, inner), F32),
            jax.ShapeDtypeStruct((1, inner), F32),
        ],
        scratch_shapes=[pltpu.VMEM((nstate, count, LANES), F32)],
        compiler_params=column_params(),
        name="backward_totals",
    )(dgated, mixed, full, act, step, out_map, cut, rate)


def backward_states_kernel(
    me_ref, step_ref, sig_ref, act_ref, dfull_ref, in_ref, outm_ref, cut_ref, rate_ref, small_ref,
    enter_ref, before_ref, totals_ref, sums_ref, keep_ref, low_ref, stepw_ref,
    dact_ref, gbias_ref, gdecay_ref, gstepw_ref, dsel_ref,
    inb, outb, din_acc, dout_acc, dlow_acc, dstep_buf, dstep_low,
):
    count = act_ref.shape[0]
    nstate = rate_ref.shape[0]
    pairs = count // 16
    j = pl.program_id(0)

    @pl.when(j == 0)
    def _():
        spread(inb, in_ref, nstate)
        spread(outb, outm_ref, nstate)
        din_acc[...] = jnp.zeros_like(din_acc)
        dout_acc[...] = jnp.zeros_like(dout_acc)
        dlow_acc[...] = jnp.zeros_like(dlow_acc)

    rates = rate_rows(rate_ref, nstate)
    arrived = arriving_state(me_ref[0], totals_ref, sums_ref, rate_ref, True)
    before = before_ref[...]
    states = tuple(
        enter_ref[n] + jnp.exp2(before * rates[n]) * arrived[n : n + 1, :] for n in range(nstate)
    )
    skip = jnp.broadcast_to(small_ref[6:7, :], (CHUNKS, LANES))

    def body(turn, carry):
        states, decays = carry
        pair = pairs - 1 - turn
        rows = pl.ds(pl.multiple_of(pair * 16, 16), 16)
        act = act_ref[rows, :].astype(F32)
        for half in (1, 0):
            at = pl.ds(pl.multiple_of(pair * 16 + half * 8, 8), 8)
            after = pl.ds(pl.multiple_of(pair * 16 + half * 8 + 8, 8), 8)
            step = step_ref[at, :]
            away = step + cut_ref[at, :]
            act_now = act[half * 8 : half * 8 + 8]
            drive = step * act_now
            grad = dfull_ref[at, :]
            by_rate = jnp.zeros((CHUNKS, LANES), F32)
            mapped = jnp.zeros((CHUNKS, LANES), F32)
            new, new_decays = [], []
            for n in range(nstate):
                adjoint = states[n] + outb[n, at, :] * grad
                passed = adjoint * jnp.exp2(away * rates[n])
                rho = passed * keep_ref[0, n, at, :]
                by_rate = by_rate + rho * rates[n]
                mapped = mapped + adjoint * inb[n, at, :]
                new_decays.append(decays[n] + rho * step)
                din_acc[n, at, :] += adjoint * drive
                dout_acc[n, at, :] += keep_ref[0, n, after, :] * grad
                new.append(passed)
            states, decays = tuple(new), tuple(new_decays)
            dstep_buf[at, :] = by_rate * LN2 + act_now * mapped
            dact_ref[at, :] = step * mapped + skip * grad
        return states, decays

    zero = jnp.zeros((CHUNKS, LANES), F32)
    states, decays = lax.fori_loop(0, pairs, body, (states, (zero,) * nstate))
    for n in range(nstate):
        gdecay_ref[n : n + 1, :] = (rate_ref[n : n + 1, :] * LN2) * jnp.sum(
            decays[n], axis=0, keepdims=True
        )
    dpre = dstep_buf[...] * sig_ref[...]
    gbias_ref[...] = jnp.sum(dpre, axis=0, keepdims=True)
    dstep_low[...] = dpre.astype(BF16)
    low_dpre = dstep_low[...]
    gstepw_ref[...] = lax.dot_general(
        low_ref[...], low_dpre, (((0,), (0,)), ((), ())), preferred_element_type=F32
    )
    dlow_acc[...] += lax.dot_general(
        low_dpre, stepw_ref[...], (((1,), (1,)), ((), ())), preferred_element_type=F32
    )

    @pl.when(j == pl.num_programs(0) - 1)
    def _():
        column = lax.broadcasted_iota(jnp.int32, (LANES, nstate), 1)
        din = jnp.zeros((count, nstate), F32)
        dout = jnp.zeros((count, nstate), F32)
        for n in range(nstate):
            pick = (column == n).astype(F32)
            din = din + jnp.dot(din_acc[n], pick, precision=HIGHEST, preferred_element_type=F32)
            dout = dout + jnp.dot(dout_acc[n], pick, precision=HIGHEST, preferred_element_type=F32)
        dsel_ref[...] = jnp.concatenate([dlow_acc[...], din, dout], axis=1).astype(BF16)


def backward_states(
    me, step, sig, act, dfull, in_map, out_map, cut, rate, small, enter, before, totals, sums, keep, low, stepw
):
    count, inner = act.shape
    nstate = rate.shape[0]
    devices = totals.shape[0]
    rank = stepw.shape[0]
    wide = rank + 2 * nstate
    blocks = inner // LANES
    return pl.pallas_call(
        backward_states_kernel,
        grid=(blocks,),
        in_specs=[
            pl.BlockSpec(memory_space=pltpu.SMEM),
            cols(count),
            cols(count),
            cols(count),
            cols(count),
            whole(count, nstate),
            whole(count, nstate),
            whole(count, LANES),
            cols(nstate),
            cols(small.shape[0]),
            pl.BlockSpec((nstate, CHUNKS, LANES), lambda j: (0, 0, j)),
            cols(CHUNKS),
            pl.BlockSpec((devices, nstate, LANES), lambda j: (0, 0, j)),
            pl.BlockSpec((devices, 1, LANES), lambda j: (0, 0, j)),
            pl.BlockSpec((1, nstate, count + CHUNKS, LANES), lambda j: (j, 0, 0, 0)),
            whole(count, rank),
            cols(rank),
        ],
        out_specs=[cols(count), cols(1), cols(nstate), cols(rank), whole(count, wide)],
        out_shape=[
            jax.ShapeDtypeStruct((count, inner), F32),
            jax.ShapeDtypeStruct((1, inner), F32),
            jax.ShapeDtypeStruct((nstate, inner), F32),
            jax.ShapeDtypeStruct((rank, inner), F32),
            jax.ShapeDtypeStruct((count, wide), BF16),
        ],
        scratch_shapes=[pltpu.VMEM((nstate, count, LANES), F32)] * 4
        + [
            pltpu.VMEM((count, rank), F32),
            pltpu.VMEM((count, LANES), F32),
            pltpu.VMEM((count, LANES), BF16),
        ],
        compiler_params=column_params(),
        name="backward_states",
    )(me, step, sig, act, dfull, in_map, out_map, cut, rate, small, enter, before, totals, sums, keep, low, stepw)


def conv_grad_kernel(
    conv_ref, halo_ref, same_ref, small_ref, sel_ref, act_ref, pre_ref, dact_ref, dsel_ref,
    dconv_ref, tail_ref, spill_ref, gsel_ref, gsmall_ref,
):
    count, width = conv_ref.shape
    reach = halo_ref.shape[0]
    steps = count // CHUNKS
    ext = conv_taps(conv_ref, halo_ref, steps, reach)
    dsel = dsel_ref[...]
    gsel_ref[...] = lax.dot_general(
        dsel, act_ref[...], (((0,), (0,)), ((), ())), preferred_element_type=F32
    )
    dact = dact_ref[...] + jnp.dot(dsel, sel_ref[...], preferred_element_type=F32)
    dpre = dact * silu_slope(pre_ref[...])
    gsmall_ref[reach + 1 : reach + 2, :] = jnp.sum(dpre, axis=0, keepdims=True)
    dpre = dpre.reshape(steps, CHUNKS, width)
    parts = []
    for k in range(reach + 1):
        masked = dpre * same_ref[k][:, :, None]
        gsmall_ref[k : k + 1, :] = jnp.sum(
            (masked * ext[k : k + steps]).reshape(count, width), axis=0, keepdims=True
        )
        parts.append(masked * small_ref[k : k + 1, :][None])
    own = parts[reach]
    for k in range(reach):
        back = reach - k
        own = own + jnp.concatenate(
            [parts[k][back:], jnp.zeros((back, CHUNKS, width), F32)], axis=0
        )
    heads = []
    for e in range(reach):
        total = parts[0][e]
        for k in range(1, e + 1):
            total = total + parts[k][e - k]
        heads.append(total)
    head = jnp.stack(heads)
    spill_ref[...] = head[:, 0, :]
    row = lax.broadcasted_iota(jnp.int32, head.shape, 1)
    moved = pltpu.roll(head.reshape(reach * CHUNKS, width), reach * CHUNKS - 1, 0)
    moved = jnp.where(row == CHUNKS - 1, 0.0, moved.reshape(head.shape))
    tail = own[steps - reach :] + moved
    tail_ref[...] = tail[:, CHUNKS - 1, :]
    dconv = jnp.concatenate([own[: steps - reach], tail], axis=0)
    dconv_ref[...] = dconv.reshape(count, width).astype(BF16)


def conv_grad(conv_in, halo, same, small, sel, act, pre, dact, dsel):
    count, inner = act.shape
    width = min(512, inner)
    reach = halo.shape[0]
    wide = sel.shape[0]
    return pl.pallas_call(
        conv_grad_kernel,
        grid=(inner // width,),
        in_specs=[
            cols(count, width),
            cols(reach, width),
            whole(*same.shape),
            cols(small.shape[0], width),
            cols(wide, width),
            cols(count, width),
            cols(count, width),
            cols(count, width),
            whole(count, wide),
        ],
        out_specs=[
            cols(count, width),
            cols(reach, width),
            cols(reach, width),
            cols(wide, width),
            cols(8, width),
        ],
        out_shape=[
            jax.ShapeDtypeStruct((count, inner), BF16),
            jax.ShapeDtypeStruct((reach, inner), F32),
            jax.ShapeDtypeStruct((reach, inner), F32),
            jax.ShapeDtypeStruct((wide, inner), F32),
            jax.ShapeDtypeStruct((8, inner), F32),
        ],
        compiler_params=column_params(),
        name="conv_grad",
    )(conv_in, halo, same, small, sel, act, pre, dact, dsel)


def share_kernel(total_ref, sum_ref, totals_ref, sums_ref, send, recv, local):
    count = totals_ref.shape[0]
    me = lax.axis_index("seq")
    barrier = pltpu.get_barrier_semaphore()
    peers = [lax.rem(me + k, count) for k in range(1, count)]
    for peer in peers:
        pl.semaphore_signal(
            barrier, inc=1, device_id={"seq": peer}, device_id_type=pl.DeviceIdType.MESH
        )
    pl.semaphore_wait(barrier, count - 1)
    copies = []
    for k, peer in enumerate(peers):
        for i, (src, dst) in enumerate(((total_ref, totals_ref), (sum_ref, sums_ref))):
            copy = pltpu.make_async_remote_copy(
                src_ref=src,
                dst_ref=dst.at[me],
                send_sem=send.at[i, k],
                recv_sem=recv.at[i, k],
                device_id={"seq": peer},
                device_id_type=pl.DeviceIdType.MESH,
            )
            copy.start()
            copies.append(copy)
    own = [
        pltpu.make_async_copy(total_ref, totals_ref.at[me], local.at[0]),
        pltpu.make_async_copy(sum_ref, sums_ref.at[me], local.at[1]),
    ]
    for copy in own:
        copy.start()
    for copy in own + copies:
        copy.wait()


def share(total, sums, collective):
    count = lax.axis_size("seq")
    vmem = pl.BlockSpec(memory_space=pltpu.VMEM)
    return pl.pallas_call(
        share_kernel,
        in_specs=[vmem, vmem],
        out_specs=[vmem, vmem],
        out_shape=[
            jax.ShapeDtypeStruct((count,) + total.shape, total.dtype),
            jax.ShapeDtypeStruct((count,) + sums.shape, sums.dtype),
        ],
        scratch_shapes=[
            pltpu.SemaphoreType.DMA((2, count - 1)),
            pltpu.SemaphoreType.DMA((2, count - 1)),
            pltpu.SemaphoreType.DMA((2,)),
        ],
        compiler_params=pltpu.CompilerParams(collective_id=collective, has_side_effects=True),
        name="share",
    )(total, sums)


def shifted(value, axis, steps):
    count = lax.axis_size(axis)
    first, last = (max(0, -steps), min(count, count - steps))
    return lax.ppermute(value, axis, [(source, source + steps) for source in range(first, last)])


MESH = pl.DeviceIdType.MESH


def where_am_i():
    c, d, z = lax.axis_index("section"), lax.axis_index("dp"), lax.axis_index("seq")
    y, x = d // 2, d % 2
    flip_x, flip_y = y * 2 + (1 - x), (1 - y) * 2 + x
    return c, y, x, z, flip_x, flip_y


def greet(c, z, flip_x, flip_y, depth):
    barrier = pltpu.get_barrier_semaphore()
    peers = [{"section": 1 - c}, {"dp": flip_x}, {"dp": flip_y}]
    peers += [{"seq": lax.rem(z + o, depth)} for o in range(1, depth)]
    for peer in peers:
        pl.semaphore_signal(barrier, inc=1, device_id=peer, device_id_type=MESH)
    pl.semaphore_wait(barrier, len(peers))


def pipeline(stages, count):
    for turn in range(count + len(stages) - 1):
        for late, stage in reversed(list(enumerate(stages))):
            if 0 <= turn - late < count:
                stage(turn - late)


def gather_kernel(plan, depth, items, *refs):
    srcs, outs = refs[:items], refs[items : 2 * items]
    mine = refs[2 * items : 3 * items]
    send, recv, local = refs[3 * items :]
    c, y, x, z, flip_x, flip_y = where_am_i()
    greet(c, z, flip_x, flip_y, depth)
    near = (1 - c) * flip_y + c * flip_x
    far = (1 - c) * flip_x + c * flip_y
    near_at = (y + (1 - c) * (1 - 2 * y), x + c * (1 - 2 * x))
    far_at = (y + c * (1 - 2 * y), x + (1 - c) * (1 - 2 * x))
    both_at = (1 - y, 1 - x)
    pending = []

    def remote(k, slot, src, dst, peer):
        return pltpu.make_async_remote_copy(
            src_ref=src, dst_ref=dst, send_sem=send.at[k, slot], recv_sem=recv.at[k, slot],
            device_id=peer, device_id_type=MESH,
        )

    def start(copy):
        copy.start()
        pending.append(copy)

    def piece(k, at):
        item, _, cols = plan[k]
        return outs[item].at[at[0], at[1], :, c, :, cols]

    def first(k):
        item, layer, cols = plan[k]
        half = mine[item].shape[1]
        slot = plan[k][2].start // plan[k][2].size
        hand = remote(
            k, 0, srcs[item].at[pl.ds((1 - layer) * half, half), cols], mine[item].at[slot],
            {"section": 1 - c},
        )
        keep = pltpu.make_async_copy(
            srcs[item].at[pl.ds(layer * half, half), cols], mine[item].at[slot], local.at[k, 0]
        )

        @pl.when(c == layer)
        def _():
            hand.start()
            keep.start()

    def along_z(k):
        item, layer, cols = plan[k]
        half = mine[item].shape[1]
        slot = plan[k][2].start // plan[k][2].size
        block = mine[item].at[slot]
        hand = remote(
            k, 0, srcs[item].at[pl.ds((1 - layer) * half, half), cols], block, {"section": 1 - c}
        )
        keep = pltpu.make_async_copy(
            srcs[item].at[pl.ds(layer * half, half), cols], block, local.at[k, 0]
        )

        @pl.when(c == layer)
        def _():
            hand.wait_send()
            keep.wait()

        @pl.when(c != layer)
        def _():
            hand.wait_recv()

        for o in range(1, depth):
            start(
                remote(k, o, block, outs[item].at[y, x, z, c, :, cols], {"seq": lax.rem(z + o, depth)})
            )
        pltpu.make_async_copy(block, outs[item].at[y, x, z, c, :, cols], local.at[k, 1]).start()

    def along_near(k):
        item, _, cols = plan[k]
        block = mine[item].at[plan[k][2].start // plan[k][2].size]
        for o in range(1, depth):
            remote(
                k, o, block, outs[item].at[y, x, z, c, :, cols], {"seq": lax.rem(z + o, depth)}
            ).wait_recv()
        pltpu.make_async_copy(block, outs[item].at[y, x, z, c, :, cols], local.at[k, 1]).wait()
        own = piece(k, (y, x))
        start(remote(k, depth, own, own, {"dp": near}))
        start(remote(k, depth + 3, own, own, {"section": 1 - c}))

    def along_far(k):
        own, other = piece(k, (y, x)), piece(k, near_at)
        remote(k, depth, own, own, {"dp": near}).wait_recv()
        start(remote(k, depth + 1, own, own, {"dp": far}))
        start(remote(k, depth + 2, other, other, {"dp": far}))
        start(remote(k, depth + 4, other, other, {"section": 1 - c}))

    def across(k):
        own, other = piece(k, (y, x)), piece(k, near_at)
        remote(k, depth + 1, own, own, {"dp": far}).wait_recv()
        remote(k, depth + 2, other, other, {"dp": far}).wait_recv()
        for slot, at in ((depth + 5, far_at), (depth + 6, both_at)):
            start(remote(k, slot, piece(k, at), piece(k, at), {"section": 1 - c}))

    def finish(k):
        own = piece(k, (y, x))
        for slot in range(depth + 3, depth + 7):
            remote(k, slot, own, own, {"section": 1 - c}).wait_recv()

    for k in range(len(plan)):
        first(k)
    pipeline([along_z, along_near, along_far, across, finish], len(plan))
    for copy in pending:
        copy.wait_send()


def gather_rows(sources, layers, widths, collective):
    depth = lax.axis_size("seq")
    plan = []
    for item, (source, layer, width) in enumerate(zip(sources, layers, widths)):
        for at in range(0, source.shape[1], width):
            plan.append((item, layer, pl.ds(at, width)))
    anywhere = pl.BlockSpec(memory_space=pl.ANY)
    outs = pl.pallas_call(
        functools.partial(gather_kernel, plan, depth, len(sources)),
        in_specs=[anywhere] * len(sources),
        out_specs=[anywhere] * len(sources),
        out_shape=[
            jax.ShapeDtypeStruct((2, 2, depth, 2, s.shape[0] // 2, s.shape[1]), s.dtype)
            for s in sources
        ],
        scratch_shapes=[
            pltpu.VMEM((s.shape[1] // w, s.shape[0] // 2, w), s.dtype)
            for s, w in zip(sources, widths)
        ]
        + [
            pltpu.SemaphoreType.DMA((len(plan), depth + 7)),
            pltpu.SemaphoreType.DMA((len(plan), depth + 7)),
            pltpu.SemaphoreType.DMA((len(plan), 2)),
        ],
        compiler_params=pltpu.CompilerParams(
            collective_id=collective, has_side_effects=True, vmem_limit_bytes=VMEM_LIMIT
        ),
        name="gather_rows",
    )(*sources)
    return [
        out.reshape(4 * depth * s.shape[0], s.shape[1]) for out, s in zip(outs, sources)
    ]


def reduce_kernel(plan, depth, layer, items, olds, *refs):
    srcs, outs = refs[:items], refs[items + olds : 2 * items + olds]
    at = 2 * items + olds
    own, core, side, edge, line, done = (refs[at + i * items : at + (i + 1) * items] for i in range(6))
    send, recv, local = refs[at + 6 * items :]
    c, y, x, z, flip_x, flip_y = where_am_i()
    greet(c, z, flip_x, flip_y, depth)
    near = (1 - c) * flip_x + c * flip_y
    far = (1 - c) * flip_y + c * flip_x
    kept = (1 - c) * y + c * x
    pending = []

    def remote(k, slot, src, dst, peer):
        return pltpu.make_async_remote_copy(
            src_ref=src, dst_ref=dst, send_sem=send.at[k, slot], recv_sem=recv.at[k, slot],
            device_id=peer, device_id_type=MESH,
        )

    def start(copy):
        copy.start()
        pending.append(copy)

    def chunk(k):
        item, slot, cols = plan[k]
        half = own[item].shape[4]
        return item, slot, cols, half

    def cores(k):
        item, slot, cols, half = chunk(k)
        theirs = srcs[item].at[:, :, :, pl.ds((1 - c) * half, half), cols]
        ours = srcs[item].at[:, :, :, pl.ds(c * half, half), cols]
        return (
            remote(k, 0, theirs, core[item].at[slot], {"section": 1 - c}),
            pltpu.make_async_copy(ours, own[item].at[slot], local.at[k, 0]),
        )

    def to_core(k):
        hand, keep = cores(k)
        start(hand)
        keep.start()

    def sides(k):
        item, slot, _, _ = chunk(k)
        return [
            remote(
                k, 1 + u,
                core[item].at[slot, (1 - c) * u + c * (1 - y), (1 - c) * (1 - x) + c * u],
                side[item].at[slot, u], {"dp": near},
            )
            for u in (0, 1)
        ]

    def to_near(k):
        item, slot, _, _ = chunk(k)
        hand, keep = cores(k)
        hand.wait_recv()
        keep.wait()

        def add(i, _):
            a, b, e = i // (2 * depth), (i // depth) % 2, i % depth
            core[item][slot, a, b, e] = core[item][slot, a, b, e] + own[item][slot, a, b, e]
            return 0

        lax.fori_loop(0, 4 * depth, add, 0)
        for copy in sides(k):
            start(copy)

    def edges(k):
        item, slot, _, _ = chunk(k)
        return remote(k, 3, side[item].at[slot, 1 - kept], edge[item].at[slot], {"dp": far})

    def to_far(k):
        item, slot, _, _ = chunk(k)
        for copy in sides(k):
            copy.wait_recv()

        def add(i, _):
            u, e = i // depth, i % depth
            side[item][slot, u, e] = (
                side[item][slot, u, e]
                + core[item][slot, (1 - c) * u + c * y, (1 - c) * x + c * u, e]
            )
            return 0

        lax.fori_loop(0, 2 * depth, add, 0)
        start(edges(k))

    def lines(k):
        item, slot, _, _ = chunk(k)
        copies = []
        for o in range(1, depth):
            peer = lax.rem(z + o, depth)
            copies.append(
                remote(
                    k, 3 + o, edge[item].at[slot, peer], line[item].at[slot, o - 1], {"seq": peer}
                )
            )
        return copies

    def to_line(k):
        item, slot, _, _ = chunk(k)
        edges(k).wait_recv()

        def add(e, _):
            edge[item][slot, e] = edge[item][slot, e] + side[item][slot, kept, e]
            return 0

        lax.fori_loop(0, depth, add, 0)
        for copy in lines(k):
            start(copy)

    def ends(k):
        item, slot, cols, half = chunk(k)
        target = outs[item].at[pl.ds(c * half, half), cols]
        return (
            remote(k, 3 + depth, done[item].at[slot], target, {"section": 1 - c}),
            pltpu.make_async_copy(done[item].at[slot], target, local.at[k, 1]),
        )

    def to_end(k):
        item, slot, _, _ = chunk(k)
        for copy in lines(k):
            copy.wait_recv()
        total = edge[item][slot, z].astype(F32)
        for o in range(depth - 1):
            total = total + line[item][slot, o].astype(F32)
        done[item][slot] = total
        hand, keep = ends(k)

        @pl.when(c == layer)
        def _():
            keep.start()

        @pl.when(c != layer)
        def _():
            hand.start()

    def finish(k):
        hand, keep = ends(k)

        @pl.when(c == layer)
        def _():
            keep.wait()
            hand.wait_recv()

        @pl.when(c != layer)
        def _():
            hand.wait_send()

    pipeline([to_core, to_near, to_far, to_line, to_end, finish], len(plan))
    for copy in pending:
        copy.wait_send()


def reduce_rows(values, widths, layer, olds, collective):
    depth = lax.axis_size("seq")
    plan, scratch = [], [[] for _ in range(6)]
    for item, (value, width) in enumerate(zip(values, widths)):
        chunks, half = value.shape[2] // width, value.shape[1] // 2
        for slot in range(chunks):
            plan.append((item, slot, pl.ds(slot * width, width)))
        block = (half, width)
        scratch[0].append(pltpu.VMEM((chunks, 2, 2, depth) + block, value.dtype))
        scratch[1].append(pltpu.VMEM((chunks, 2, 2, depth) + block, value.dtype))
        scratch[2].append(pltpu.VMEM((chunks, 2, depth) + block, value.dtype))
        scratch[3].append(pltpu.VMEM((chunks, depth) + block, value.dtype))
        scratch[4].append(pltpu.VMEM((chunks, depth - 1) + block, value.dtype))
        scratch[5].append(pltpu.VMEM((chunks,) + block, F32))
    items = len(values)
    anywhere = pl.BlockSpec(memory_space=pl.ANY)
    return pl.pallas_call(
        functools.partial(reduce_kernel, plan, depth, layer, items, len(olds)),
        in_specs=[anywhere] * (items + len(olds)),
        out_specs=[anywhere] * items,
        out_shape=[jax.ShapeDtypeStruct(v.shape[1:], F32) for v in values],
        scratch_shapes=sum(scratch, [])
        + [
            pltpu.SemaphoreType.DMA((len(plan), depth + 4)),
            pltpu.SemaphoreType.DMA((len(plan), depth + 4)),
            pltpu.SemaphoreType.DMA((len(plan), 2)),
        ],
        input_output_aliases={items + i: i for i in range(len(olds))},
        compiler_params=pltpu.CompilerParams(
            collective_id=collective, has_side_effects=True, vmem_limit_bytes=VMEM_LIMIT
        ),
        name="reduce_rows",
    )(*[v.reshape((2, 2, depth) + v.shape[1:]) for v in values], *olds)


def places(lengths, count, reach):
    steps = count // CHUNKS
    base = lax.axis_index("seq") * count
    starts = jnp.cumsum(lengths) - lengths
    here = (
        base + jnp.arange(steps, dtype=jnp.int32)[:, None]
        + steps * jnp.arange(CHUNKS, dtype=jnp.int32)[None, :]
    )

    def segment(at):
        return jnp.sum((starts[:, None, None] <= at[None]).astype(jnp.int32), axis=0) - 1

    own = segment(here)
    same = jnp.stack(
        [(segment(here - reach + k) == own).astype(F32) for k in range(reach + 1)]
    )
    opens = jnp.any(starts[:, None, None] == here[None], axis=0)
    cut = jnp.where(opens, CUT, 0.0).astype(F32).reshape(count, 1)
    return same, jnp.broadcast_to(cut, (count, LANES))


def layer_forward(xin, weights, same, cut, me):
    in_weight, out_weight, sel, stepw, small, rate, gain = weights
    count = xin.shape[0]
    inner = out_weight.shape[0]
    rank, nstate = stepw.shape[0], rate.shape[0]
    reach = same.shape[0] - 1
    scale = lax.rsqrt(jnp.mean(xin * xin, axis=-1, keepdims=True) + EPS)
    normed = (xin * scale * gain).astype(BF16)
    mixed = jnp.dot(normed, in_weight, preferred_element_type=F32).astype(BF16)
    last = mixed[(count - reach * CHUNKS) :, :inner].reshape(reach, CHUNKS, inner)[:, CHUNKS - 1]
    halo = shifted(last, "seq", 1)
    act, pre, selected = select_call(mixed[:, :inner], halo, same, small, sel)
    low = selected[:, :rank].astype(BF16)
    in_map = selected[:, rank : rank + nstate]
    out_map = selected[:, rank + nstate :]
    step, sig, enter, total, before, sums, moments = forward_totals(
        low, stepw, small, act, in_map, cut, rate
    )
    totals, all_sums = share(total, sums, 1)
    full, gated, keep = forward_states(
        me, step, act, mixed, in_map, out_map, cut, rate, small, enter, before, totals, all_sums
    )
    result = xin + jnp.dot(gated, out_weight, preferred_element_type=F32)
    saved = (xin, scale, normed, mixed, halo, act, pre, low, in_map, out_map, step, sig, full, gated, keep)
    return result, moments, saved


def outer_sum(left, right):
    return lax.dot_general(left, right, (((0,), (0,)), ((), ())), preferred_element_type=F32)


def times_transposed(left, right):
    return lax.dot_general(left, right, (((1,), (1,)), ((), ())), preferred_element_type=F32)


def layer_backward(grad_out, weights, same, cut, me, saved, moments):
    in_weight, out_weight, sel, stepw, small, rate, gain = weights
    (xin, scale, normed, mixed, halo, act, pre, low, in_map, out_map, step, sig, full, gated, keep) = saved
    count, inner = act.shape
    reach = same.shape[0] - 1
    grad_low = grad_out.astype(BF16)
    dgated = times_transposed(grad_low, out_weight)
    gout = outer_sum(gated, grad_low).astype(BF16)
    dfull, dgate, gskip, enter, total, before, sums = backward_totals(
        dgated, mixed, full, act, step, out_map, cut, rate
    )
    totals, all_sums = share(total, sums, 1)
    dact, gbias, gdecay, gstepw, dsel = backward_states(
        me, step, sig, act, dfull, in_map, out_map, cut, rate, small, enter, before, totals, all_sums, keep, low, stepw
    )
    dconv, tail, spill, gsel, gsmall = conv_grad(
        mixed[:, :inner], halo, same, small, sel, act, pre, dact, dsel
    )
    late = (tail + shifted(spill, "seq", -1)).astype(BF16)
    grid = dconv.reshape(count // CHUNKS, CHUNKS, inner)
    dconv = grid.at[count // CHUNKS - reach :, CHUNKS - 1].set(late).reshape(count, inner)
    dmixed = jnp.concatenate([dconv, dgate], axis=1)
    gin = outer_sum(normed, dmixed).astype(BF16)
    dnormed = times_transposed(dmixed, in_weight)
    unit = xin * scale
    ggain = jnp.sum(dnormed * unit, axis=0)
    dunit = dnormed * gain
    grad_in = scale * (dunit - unit * jnp.mean(dunit * unit, axis=-1, keepdims=True)) + grad_out
    shards = lax.axis_size(("dp", "seq"))
    per = inner // shards
    ggain = jnp.pad(ggain.reshape(shards, -1), ((0, 0), (0, per - ggain.shape[0] // shards)))
    rows = jnp.concatenate(
        [gsel, gstepw, gdecay, gsmall[: reach + 2], gbias, gskip, ggain.reshape(1, inner), moments,
         jnp.zeros((6, inner), F32)], axis=0,
    )
    return grad_in, gin, gout, rows


AXES = ("section", "dp", "seq")


def body(
    inputs, doc_lengths, out_grad, norm_gain, in_weight, conv_weight, conv_bias, select_weight,
    step_weight, step_bias, log_decay, skip_gain, out_weight,
):
    section = lax.axis_index("section")
    me = lax.axis_index("seq").reshape(1).astype(jnp.int32)
    micro, _, count, model = inputs.shape
    taps, per = conv_weight.shape[1:]
    shards = lax.axis_size(("dp", "seq"))
    inner = per * shards
    rank, nstate = step_weight.shape[1], log_decay.shape[1]
    wide = rank + 2 * nstate

    kernels = lax.axis_size("dp") == 4 and per % LANES == 0 and in_weight.shape[1] % 32 == 0
    pad = per - norm_gain.shape[1]
    rows = jnp.concatenate(
        [select_weight[0].T, step_weight[0], log_decay[0], conv_weight[0], conv_bias, step_bias, skip_gain,
         jnp.pad(norm_gain, ((0, 0), (0, pad))), jnp.zeros((8, per), BF16)], axis=0,
    )
    if kernels:
        got = gather_rows(
            [rows, rows, in_weight[0], in_weight[0], out_weight[0], out_weight[0]],
            [0, 1, 0, 1, 0, 1], [per, per, 512, 512, 256, 256], 2,
        )
        packed = [g.reshape(shards, -1, per) for g in got[:2]]
        in_all, out_all = got[2:4], got[4:6]
    else:
        packed = lax.all_gather(rows, AXES, axis=0).reshape(2, shards, -1, per)
        in_all = lax.all_gather(in_weight[0], AXES, axis=0, tiled=True).reshape(2, model, -1)
        out_all = lax.all_gather(out_weight[0], AXES, axis=0, tiled=True).reshape(2, inner, model)
    weights = []
    for layer in range(2):
        flat = packed[layer].swapaxes(0, 1).reshape(-1, inner)
        at = wide + rank + nstate
        small = flat[at : at + 16].astype(F32)
        gain = packed[layer][:, at + taps + 3, : norm_gain.shape[1]].reshape(-1).astype(F32)
        rate = -jnp.exp(flat[wide + rank : at].astype(F32)) * LOG2E
        small = jnp.concatenate([small[: taps + 3], jnp.zeros((1, inner), F32)], axis=0)
        weights.append(
            (in_all[layer], out_all[layer], flat[:wide], flat[wide : wide + rank], small, rate, gain)
        )

    mine = lambda value: lax.dynamic_index_in_dim(value, section, 0, keepdims=False)[0]
    same, cut = places(mine(doc_lengths), count, taps - 1)
    state = interleave(mine(inputs).astype(F32))
    outs, kept = [], []
    for layer in range(2):
        state, moments, saved = layer_forward(state, weights[layer], same, cut, me)
        outs.append(state)
        kept.append((saved, moments))
    grad = interleave(mine(out_grad).astype(F32))
    grads, gins, gouts, packs = [None] * 2, [None] * 2, [None] * 2, [None] * 2
    for layer in (1, 0):
        grad, gins[layer], gouts[layer], packs[layer] = layer_backward(
            grad, weights[layer], same, cut, me, *kept[layer]
        )
        grads[layer] = grad

    packs = [pack.reshape(-1, shards, per).swapaxes(0, 1) for pack in packs]
    gins = [g.reshape(shards, -1, g.shape[1]) for g in gins]
    gouts = [g.reshape(shards, -1, model) for g in gouts]
    if kernels:
        found = []
        for layer in (1, 0):
            found = reduce_rows(
                [packs[layer], gins[layer], gouts[layer]], [per, 512, 256], layer, found, 4 - layer
            )
        rows, gin, gout = found
    else:

        def settle(parts):
            return lax.psum_scatter(jnp.stack(parts).reshape((-1,) + parts[0].shape[1:]), AXES, scatter_dimension=0)

        rows, gin, gout = settle(packs), settle(gins).astype(F32), settle(gouts).astype(F32)

    def place(values):
        first, second = (in_order(value) for value in values)
        own = jnp.where(section == 0, first, second)
        other = jnp.where(section == 0, second, first)
        other = lax.ppermute(other, "section", [(0, 1), (1, 0)])
        both = jnp.stack([jnp.where(section == 0, own, other), jnp.where(section == 0, other, own)])
        return both[None, :, None]

    at = wide + rank + nstate
    tokens = micro * inputs.shape[1] * lax.axis_size("dp") * count * lax.axis_size("seq")
    return (
        place(outs),
        place(grads),
        rows[at + taps + 3, : norm_gain.shape[1]][None],
        gin[None],
        rows[at : at + taps][None],
        rows[at + taps][None],
        rows[:wide].T[None],
        rows[wide : wide + rank][None],
        rows[at + taps + 1][None],
        rows[wide + rank : at][None],
        rows[at + taps + 2][None],
        gout[None],
        (rows[at + taps + 4 : at + taps + 6] / tokens)[None],
    )


def solution(mesh):
    vector = P("section", ("dp", "seq"))
    matrix = P("section", ("dp", "seq"), None)
    turned = P("section", None, ("dp", "seq"))
    tokens = P(None, "dp", "seq", None)
    in_specs = (
        tokens, P(None, "dp", None), tokens, vector, matrix, turned, vector, matrix, turned,
        vector, turned, vector, matrix,
    )
    result = P("section", None, "dp", "seq", None)
    out_specs = (
        result, result, vector, matrix, turned, vector, matrix, turned, vector, turned, vector,
        matrix, turned,
    )
    return jax.shard_map(body, mesh=mesh, in_specs=in_specs, out_specs=out_specs, check_vma=False)
```

time: 4150 us -> 816 us (0.20)
  other arithmetic: 1550 us -> 13.1 us
  matrix products: 838 us -> 63 us
  waiting for transfers between devices: 669 us -> 0.02 us
  Pallas kernels: 0 us -> 649 us
  blocking collectives: 559 us -> 0 us
  local copies, waits for them, and re-layouts: 491 us -> 66.3 us
    dynamic_update_slice x192 -> x0, other arithmetic: 729 us -> none  [the longest x96 665 us: stepper(): products = lax.dynamic_update_index_in_dim(products, product, place, 1)]
    dot_general x42 -> x4, matrix products: 731 us -> 19.7 us  [the longest x2 12.5 us: layer_forward(): mixed = jnp.dot(normed, in_weight, preferred_element_type=F32).astype(BF16)]
    reduce_scatter x5 -> x0, waiting for transfers between devices: 657 us -> none  [the longest x1 351 us: body(): lax.psum_scatter(totals[1], ('dp', 'seq'), scatter_dimension=0, tiled=True)]
    pallas_call x0 -> x19, Pallas kernels: none -> 649 us  [the longest x2 200 us: reduce_rows(): pl.pallas_call(functools.partial(reduce_kernel, plan, depth, layer, items...]
    all_gather x19 -> x0, blocking collectives: 442 us -> none  [the longest x6 90.1 us: entering_2(): gathered = jax.tree.map(lambda a: lax.all_gather(a, axis), part)]
    add x119 -> x2, other arithmetic: 305 us -> 0.08 us  [the longest x1 0.07 us: places(): here - reach + k]
    dot_general x7 -> x0, other arithmetic: 206 us -> none  [the longest x3 75.1 us: backward_row(): jnp.einsum('tnd,nd->td', rate_grad, decay_rate, precision=highest)]
    slice x33 -> x14, local copies, waits for them, and re-layouts: 215 us -> 10.7 us  [the longest x2 3.65 us: layer_forward(): out_map = selected[:, rank + nstate:]]
  transfers between devices with their start and end apart: 19 -> 6, of which waited for: 8 -> 0; matrix products, arithmetic and copies ran while one was open for 39% -> 10% of each run, Pallas kernels for 0% -> 25%
where the time goes in v1:
time: 816 us; the launch traced here: 804 us
  Pallas kernels  649 us (80%)
  local copies, waits for them, and re-layouts  66.3 us (8%)
  matrix products  63 us (8%)
  other arithmetic  13.1 us (2%)
  starting transfers between devices  10.8 us (1%)
    pallas_call x2, Pallas kernels, reduce_rows(): pl.pallas_call(functools.partial(reduce_kernel, plan, depth, layer, items...  200 us
    pallas_call x1, Pallas kernels, gather_rows(): pl.pallas_call(functools.partial(gather_kernel, plan, depth, len(sources)...  182 us
    pallas_call x2, Pallas kernels, backward_states(): pl.pallas_call(backward_states_kernel, grid=(blocks,), in_specs=[pl.Block...  88.3 us
    pallas_call x2, Pallas kernels, forward_states(): pl.pallas_call(forward_states_kernel, grid=(blocks,), in_specs=[pl.BlockS...  45.6 us
    pallas_call x4, Pallas kernels, share(): pl.pallas_call(share_kernel, in_specs=[vmem, vmem], out_specs=[vmem, vmem...  43.8 us
    pallas_call x2, Pallas kernels, backward_totals(): pl.pallas_call(backward_totals_kernel, grid=(blocks,), in_specs=[cols(cou...  34 us
    pallas_call x2, Pallas kernels, forward_totals(): pl.pallas_call(forward_totals_kernel, grid=(inner // LANES,), in_specs=[w...  32.9 us
    concatenate x11, local copies, waits for them, and re-layouts, layer_backward(): jnp.concatenate([gsel, gstepw, gdecay, gsmall[:reach + 2], gbias, gskip,...  24 us
  transfers between devices with their start and end apart: 6, of which 0 were waited for; matrix products, arithmetic and copies ran while one was open for 10% of the time, Pallas kernels for 25%

profile of v1, /device:TPU:0, one launch (start us, length us, event | category | flops | bytes accessed | tf_op | source)
XLA Modules:
  0.0 804.3 jit_solution(15982054509627810046)
XLA Ops:
  0.7 2.1 constant_dynamic-slice_fusion
  3.7 3.0 concatenate.62.refs_0_.refs_1_
  6.7 182.4 %gather_rows.1 = (bf16[2,2,4,2,96,128]{5,4,3,2,1,0:T(8,128)(2,1)}, bf16[2,2,4,2,96,128]{5,4,3,2,1,0:T(8,128)(2,1)}, bf16[2,2,4,2,32,4096]{5,4,3,2,1,0:T(8,128)(2...) custom-call(bf16[192,128]{1,0:T(8,128)(2,1)} %concatenate.62.refs_0_, ...), custom_call_target="tpu_custom_call" | custom-call | tf_op jit(solution)/shard_map/gather_rows/pallas_call | solution.py:848
  190.0 6.3 convolution_convert_fusion.3.gate_ref
  196.4 3.2 collective-permute-start
  204.5 5.1 fusion.12.dgated_ref
  215.5 4.7 conv_select.2
  220.3 1.8 fusion.33
  224.4 16.4 %forward_totals.2 = (f32[256,2048]{1,0:T(8,128)}, f32[256,2048]{1,0:T(8,128)}, f32[16,8,2048]{2,1,0:T(8,128)}, bf16[16,2048]{1,0:T(8,128)(2,1)}, f32[8,2048]{1,0...) custom-call(bf16[256,64]{1,0:T(8,128)(2,1)} %slice.256.low_ref, bf16[64,2048]{1,0:T(8,128)(2,1)} %bitcast.282, ...), custom_call_target="tpu_custom_call" | custom-call | tf_op jit(solution)/shard_map/forward_totals/pallas_call | solution.py:197
  240.8 14.0 %share.4 = (bf16[4,16,2048]{2,1,0:T(8,128)(2,1)}, f32[4,1,2048]{2,1,0:T(1,128)}) custom-call(bf16[16,2048]{1,0:T(8,128)(2,1)} %get-tuple-element.124.total_ref, f32[1,2048]{1,0:T(1,128)} %get-tuple-element.125.sum_ref), custom_call_target="tpu_custom_call" | custom-call | tf_op jit(solution)/shard_map/share/pallas_call | solution.py:682
  254.8 22.8 %forward_states.2 = (f32[256,2048]{1,0:T(8,128)}, bf16[256,2048]{1,0:T(8,128)(2,1)}, f32[16,16,264,128]{3,2,1,0:T(8,128)}) custom-call(s32[1]{0:T(128)} %bitcast.3.me_ref, f32[256,2048]{1,0:T(8,128)} %get-tuple-element.121.step_ref, bf16[256,2048]{1,0:T(8,128)(2,1)} %get-tuple-element.120.act_ref, bf16[256,4096]{1,0:T(8,128)(2,1)} %copy-done, ...), custom_call_target="tpu_custom_call" | custom-call | tf_op jit(solution)/shard_map/forward_states/pallas_call | solution.py:300
  277.6 4.3 multiply_reduce_fusion.4
  281.9 6.2 convolution_convert_fusion.2.gate_ref
  288.9 4.8 collective-permute-start.1
  296.8 1.6 copy.215
  298.4 1.7 copy.213
  301.3 4.9 conv_select.3
  306.1 1.8 fusion.32
  309.5 16.4 %forward_totals.3 = (f32[256,2048]{1,0:T(8,128)}, f32[256,2048]{1,0:T(8,128)}, f32[16,8,2048]{2,1,0:T(8,128)}, bf16[16,2048]{1,0:T(8,128)(2,1)}, f32[8,2048]{1,0...) custom-call(bf16[256,64]{1,0:T(8,128)(2,1)} %slice.255.low_ref, bf16[64,2048]{1,0:T(8,128)(2,1)} %bitcast.284, ...), custom_call_target="tpu_custom_call" | custom-call | tf_op jit(solution)/shard_map/forward_totals/pallas_call | solution.py:197
  325.9 10.4 %share.5 = (bf16[4,16,2048]{2,1,0:T(8,128)(2,1)}, f32[4,1,2048]{2,1,0:T(1,128)}) custom-call(bf16[16,2048]{1,0:T(8,128)(2,1)} %get-tuple-element.137.total_ref, f32[1,2048]{1,0:T(1,128)} %get-tuple-element.138.sum_ref), custom_call_target="tpu_custom_call" | custom-call | tf_op jit(solution)/shard_map/share/pallas_call | solution.py:682
  336.3 22.8 %forward_states.3 = (f32[256,2048]{1,0:T(8,128)}, bf16[256,2048]{1,0:T(8,128)(2,1)}, f32[16,16,264,128]{3,2,1,0:T(8,128)}) custom-call(s32[1]{0:T(128)} %bitcast.3.me_ref, f32[256,2048]{1,0:T(8,128)} %get-tuple-element.134.step_ref, bf16[256,2048]{1,0:T(8,128)(2,1)} %get-tuple-element.133.act_ref, bf16[256,4096]{1,0:T(8,128)(2,1)} %copy-done.1, ...), custom_call_target="tpu_custom_call" | custom-call | tf_op jit(solution)/shard_map/forward_states/pallas_call | solution.py:300
  359.1 16.9 %backward_totals.2 = (f32[256,2048]{1,0:T(8,128)}, bf16[256,2048]{1,0:T(8,128)(2,1)}, f32[1,2048]{1,0:T(1,128)}, f32[16,8,2048]{2,1,0:T(8,128)}, bf16[16,2048]{1...) custom-call(f32[256,2048]{1,0:T(8,128)} %fusion.12.dgated_ref, bf16[256,4096]{1,0:T(8,128)(2,1)} %copy-done.1, ...), custom_call_target="tpu_custom_call" | custom-call | tf_op jit(solution)/shard_map/backward_totals/pallas_call | solution.py:388
  376.0 9.4 %share.6 = (bf16[4,16,2048]{2,1,0:T(8,128)(2,1)}, f32[4,1,2048]{2,1,0:T(1,128)}) custom-call(bf16[16,2048]{1,0:T(8,128)(2,1)} %get-tuple-element.151.total_ref, f32[1,2048]{1,0:T(1,128)} %get-tuple-element.152.sum_ref), custom_call_target="tpu_custom_call" | custom-call | tf_op jit(solution)/shard_map/share/pallas_call | solution.py:682
  385.4 44.2 %backward_states.2 = (f32[256,2048]{1,0:T(8,128)}, f32[1,2048]{1,0:T(1,128)}, f32[16,2048]{1,0:T(8,128)}, f32[64,2048]{1,0:T(8,128)}, bf16[256,96]{1,0:T(8,128)(2,1)}) custom-call(s32[1]{0:T(128)} %bitcast.3.me_ref, f32[256,2048]{1,0:T(8,128)} %get-tuple-element.134.step_ref, f32[256,2048]{1,0:T(8,128)} %get-tuple-element.146.sig_ref, ...), custom_call_target="tpu_custom_call" | custom-call | tf_op jit(solution)/shard_map/backward_states/pallas_call | solution.py:521
  429.6 6.5 conv_grad.2
  437.6 2.1 copy_bitcast_fusion
  440.6 3.5 convolution_convert_fusion.4
  444.2 1.6 scatter.6
  445.8 7.5 convolution_convert_fusion
  453.3 6.1 multiply_reduce_fusion
  459.4 2.9 fusion.2
  462.4 3.5 convolution_convert_fusion.5
  465.8 2.6 fusion.21.dgated_ref
  468.5 17.1 %backward_totals.3 = (f32[256,2048]{1,0:T(8,128)}, bf16[256,2048]{1,0:T(8,128)(2,1)}, f32[1,2048]{1,0:T(1,128)}, f32[16,8,2048]{2,1,0:T(8,128)}, bf16[16,2048]{1...) custom-call(f32[256,2048]{1,0:T(8,128)} %fusion.21.dgated_ref, bf16[256,4096]{1,0:T(8,128)(2,1)} %copy-done, ...), custom_call_target="tpu_custom_call" | custom-call | tf_op jit(solution)/shard_map/backward_totals/pallas_call | solution.py:388
  485.6 10.0 %share.7 = (bf16[4,16,2048]{2,1,0:T(8,128)(2,1)}, f32[4,1,2048]{2,1,0:T(1,128)}) custom-call(bf16[16,2048]{1,0:T(8,128)(2,1)} %get-tuple-element.166.total_ref, f32[1,2048]{1,0:T(1,128)} %get-tuple-element.167.sum_ref), custom_call_target="tpu_custom_call" | custom-call | tf_op jit(solution)/shard_map/share/pallas_call | solution.py:682
  495.6 44.2 %backward_states.3 = (f32[256,2048]{1,0:T(8,128)}, f32[1,2048]{1,0:T(1,128)}, f32[16,2048]{1,0:T(8,128)}, f32[64,2048]{1,0:T(8,128)}, bf16[256,96]{1,0:T(8,128)(2,1)}) custom-call(s32[1]{0:T(128)} %bitcast.3.me_ref, f32[256,2048]{1,0:T(8,128)} %get-tuple-element.121.step_ref, f32[256,2048]{1,0:T(8,128)} %get-tuple-element.144.sig_ref, ...), custom_call_target="tpu_custom_call" | custom-call | tf_op jit(solution)/shard_map/backward_states/pallas_call | solution.py:521
  539.8 6.4 conv_grad.3
  547.6 2.1 copy_bitcast_fusion.1
  553.0 1.6 copy.127
  554.6 1.8 copy.126
  556.4 8.7 %concatenate.85 = f32[192,16,128]{2,0,1:T(8,128)} concatenate(f32[96,16,128]{2,0,1:T(8,128)} %copy_bitcast_fusion, f32[64,16,128]{2,0,1:T(8,128)} %copy_bitcast_fusion.4, f32[16,16,128]{2,0,1:T(8,128)S(1)} %copy_bitcast_fusion.12, f32[5,16,128]{2,0,1:T(8,128)S(1)} %slice_bitcast_fusion.2, f32[1,16,128]{2,0,1:T(1,128)} %bitcast.320, f32[1,16,128]{2,0,1:T(1,128)} %bitcast.319, ...), dimensions={0} | concatenate | bytes 3145728 | tf_op jit(solution)/shard_map/concatenate | solution.py:1151
  565.1 100.4 %reduce_rows.2 = (f32[192,128]{1,0:T(8,128)}, f32[64,4096]{1,0:T(8,128)}, f32[128,1024]{1,0:T(8,128)}) custom-call(f32[2,2,4,192,128]{4,3,2,1,0:T(8,128)} %bitcast.253, bf16[2,2,4,64,4096]{4,3,2,1,0:T(8,128)(2,1)} %bitcast.249, bf16[2,2,4,128,1024]{4,3,2,1,0:T(8,128)(2,1)} %bitcast.251), custom_call_target="tpu_custom_call" | custom-call | tf_op jit(solution)/shard_map/reduce_rows/pallas_call | solution.py:1045
  666.3 1.6 scatter.9
  668.0 7.8 convolution_convert_fusion.1
  675.8 7.2 multiply_reduce_fusion.1
  683.1 7.0 concatenate.76
  690.1 99.2 %reduce_rows.3 = (f32[192,128]{1,0:T(8,128)}, f32[64,4096]{1,0:T(8,128)}, f32[128,1024]{1,0:T(8,128)}) custom-call(f32[2,2,4,192,128]{4,3,2,1,0:T(8,128)} %bitcast.254, bf16[2,2,4,64,4096]{4,3,2,1,0:T(8,128)(2,1)} %bitcast.250, bf16[2,2,4,128,1024]{4,3,2,1,0:T(8,128)(2,1)} %bitcast.252, ...), custom_call_target="tpu_custom_call", output_to_operand_aliasing={{0}: (3, {}), {1}: (4, {}), {2}: (5, {})} | custom-call | tf_op jit(solution)/shard_map/reduce_rows/pallas_call | solution.py:1045
  790.7 1.9 fusion.4
  (182 shorter events, 41.7 us)
Async XLA Ops:
  0.6 2.9 copy-start.44
  0.7 3.0 copy-start.31
  0.7 3.0 copy-start.33
  0.7 3.0 copy-start.36
  0.7 3.0 copy-start.37
  0.7 3.0 copy-start.38
  0.7 3.0 copy-start.39
  0.7 3.0 copy-start.40
  3.6 192.8 %copy-start.28 = (f32[32,8]{1,0:T(8,128)}, f32[32,8]{1,0:T(8,128)S(1)}, u32[]{:S(2)}) copy-start(f32[32,8]{1,0:T(8,128)S(1)} %add_rsqrt_fusion) | copy-start | bytes 3076
  190.0 9.6 %copy-start.20 = (bf16[2,2,4,2,96,128]{5,4,3,2,1,0:T(8,128)(2,1)S(1)}, bf16[2,2,4,2,96,128]{5,4,3,2,1,0:T(8,128)(2,1)}, u32[]{:S(2)}) copy-start(bf16[2,2,4,2,96,128]{5,4,3,2,1,0:T(8,128)(2,1)} %get-tuple-element.130) | copy-start | bytes 2359300
  190.0 11.0 %copy-start.19 = (bf16[2,2,4,2,96,128]{5,4,3,2,1,0:T(8,128)(2,1)S(1)}, bf16[2,2,4,2,96,128]{5,4,3,2,1,0:T(8,128)(2,1)}, u32[]{:S(2)}) copy-start(bf16[2,2,4,2,96,128]{5,4,3,2,1,0:T(8,128)(2,1)} %get-tuple-element.117) | copy-start | bytes 2359300
  190.0 12.4 %copy-start.42 = (s32[2,1,4]{2,1,0:T(1,128)S(1)}, s32[2,1,4]{2,1,0:T(1,128)}, u32[]{:S(2)}) copy-start(s32[2,1,4]{2,1,0:T(1,128)} %param.18) | copy-start | bytes 100
  196.4 14.2 %copy-start = (bf16[256,4096]{1,0:T(8,128)(2,1)}, bf16[256,4096]{1,0:T(8,128)(2,1)S(1)}, u32[]{:S(2)}) copy-start(bf16[256,4096]{1,0:T(8,128)(2,1)S(1)} %convolution_convert_fusion.3.gate_ref) | copy-start | bytes 6291460
  196.4 18.5 %collective-permute-start = (bf16[3,2048]{1,0:T(4,128)(2,1)S(1)}, bf16[3,2048]{1,0:T(4,128)(2,1)S(1)}, u32[]{:S(2)}, u32[]{:S(2)}) collective-permute-start(bf16[3,2048]{1,0:T(4,128)(2,1)S(1)} %bitcast.318), channel_id=1, source_target_pairs={{0,1},{1,2},{2,3},{4,5},{5,6},{6,7},{8,9},{9,10},{10,11},{12,13},{... | collective-permute-start | bytes 36872 | tf_op jit(solution)/shard_map/ppermute | solution.py:703
  201.0 8.7 %copy-start.41 = (pred[8]{0:T(512)(128)(4,1)S(1)}, pred[8]{0:T(512)(128)(4,1)}, u32[]{:S(2)}) copy-start(pred[8]{0:T(512)(128)(4,1)} %constant.123.clone.1) | copy-start | bytes 28
  204.5 7.1 copy-start.5
  281.9 6.2 copy-start.11
  281.9 11.8 %copy-start.4 = (bf16[16,192,128]{2,0,1:T(8,128)(2,1)S(1)}, bf16[16,192,128]{2,0,1:T(8,128)(2,1)}, u32[]{:S(2)}) copy-start(bf16[16,192,128]{2,0,1:T(8,128)(2,1)} %copy.209) | copy-start | bytes 2359300
  288.1 37.8 %copy-start.1 = (bf16[256,4096]{1,0:T(8,128)(2,1)}, bf16[256,4096]{1,0:T(8,128)(2,1)S(1)}, u32[]{:S(2)}) copy-start(bf16[256,4096]{1,0:T(8,128)(2,1)S(1)} %convolution_convert_fusion.2.gate_ref) | copy-start | bytes 6291460
  288.9 12.3 %collective-permute-start.1 = (bf16[3,2048]{1,0:T(4,128)(2,1)}, bf16[3,2048]{1,0:T(4,128)(2,1)}, u32[]{:S(2)}, u32[]{:S(2)}) collective-permute-start(bf16[3,2048]{1,0:T(4,128)(2,1)} %bitcast.247), channel_id=1, source_target_pairs={{0,1},{1,2},{2,3},{4,5},{5,6},{6,7},{8,9},{9,10},{10,11},{12,13},{... | collective-permute-start | bytes 36872 | tf_op jit(solution)/shard_map/ppermute | solution.py:703
  429.6 10.1 %copy-start.22 = (f32[64,2048]{1,0:T(8,128)S(1)}, f32[64,2048]{1,0:T(8,128)}, u32[]{:S(2)}) copy-start(f32[64,2048]{1,0:T(8,128)} %get-tuple-element.185) | copy-start | bytes 1572868
  429.6 11.0 %copy-start.25 = (f32[16,2048]{1,0:T(8,128)S(1)}, f32[16,2048]{1,0:T(8,128)}, u32[]{:S(2)}) copy-start(f32[16,2048]{1,0:T(8,128)} %get-tuple-element.186) | copy-start | bytes 393220
  429.6 11.0 %copy-start.7 = (bf16[256,2048]{1,0:T(8,128)(2,1)S(1)}, bf16[256,2048]{1,0:T(8,128)(2,1)}, u32[]{:S(2)}) copy-start(bf16[256,2048]{1,0:T(8,128)(2,1)} %get-tuple-element.141) | copy-start | bytes 3145732
  429.6 11.0 %copy-start.8 = (bf16[1,1,256,1024]{3,2,1,0:T(8,128)(2,1)S(1)}, bf16[1,1,256,1024]{3,2,1,0:T(8,128)(2,1)}, u32[]{:S(2)}) copy-start(bf16[1,1,256,1024]{3,2,1,0:T(8,128)(2,1)} %get-tuple-element.286) | copy-start | bytes 1572868
  436.1 8.0 collective-permute-start.3
  440.6 3.5 copy-start.27
  440.6 3.5 copy-start.30
  440.6 5.2 copy-start.12
  445.8 7.5 copy-start.15
  445.8 7.5 copy-start.17
  453.3 6.1 copy-start.9
  453.3 6.1 copy-start.13
  453.3 6.1 copy-start.43
  459.4 3.0 copy-start.6
  462.4 3.5 copy-start.2
  539.8 9.9 %copy-start.21 = (f32[64,2048]{1,0:T(8,128)S(1)}, f32[64,2048]{1,0:T(8,128)}, u32[]{:S(2)}) copy-start(f32[64,2048]{1,0:T(8,128)} %get-tuple-element.178) | copy-start | bytes 1572868
  539.8 13.2 %copy-start.18 = (f32[8,32,1024]{2,0,1:T(8,128)S(1)}, f32[8,32,1024]{2,0,1:T(8,128)}, u32[]{:S(2)}) copy-start(f32[8,32,1024]{2,0,1:T(8,128)} %get-tuple-element.264) | copy-start | bytes 3145732
  546.3 119.3 %collective-permute-start.4 = (f32[3,2048]{1,0:T(4,128)}, f32[3,2048]{1,0:T(4,128)}, u32[]{:S(2)}, u32[]{:S(2)}) collective-permute-start(f32[3,2048]{1,0:T(4,128)} %get-tuple-element.175), channel_id=1, source_target_pairs={{1,0},{2,1},{3,2},{5,4},{6,5},{7,6},{9,8},{10,9},{11,10},{13,12},{... | collective-permute-start | bytes 73736 | tf_op jit(solution)/shard_map/ppermute | solution.py:703
  554.6 242.8 %collective-permute-start.2 = (f32[256,1024]{1,0:T(8,128)}, f32[256,1024]{1,0:T(8,128)}, u32[]{:S(2)}, u32[]{:S(2)}) collective-permute-start(f32[256,1024]{1,0:T(8,128)} %bitcast.35), channel_id=1, source_target_pairs={{0,16},{16,0},{1,17},{17,1},{2,18},{18,2},{3,19},{19,3},{4,20},{20... | collective-permute-start | bytes 3145736 | tf_op jit(solution)/shard_map/ppermute | solution.py:1240
  565.1 100.4 %copy-start.29 = (f32[3,2048]{1,0:T(4,128)S(1)}, f32[3,2048]{1,0:T(4,128)}, u32[]{:S(2)}) copy-start(f32[3,2048]{1,0:T(4,128)} %get-tuple-element.174) | copy-start | bytes 73732
  668.0 7.8 copy-start.14
  668.0 7.8 copy-start.16
  675.7 7.4 copy-start.24
  675.7 7.4 copy-start.32
  675.8 7.3 copy-start.34
  675.8 7.3 copy-start.35
  789.3 3.9 copy-start.23
  793.2 7.1 collective-permute-start.5
  (3 other events, 4.8 us)

commit v2 on v1

v2 whole, which is shorter than its diff:
```python
import functools
import math

import jax
import jax.numpy as jnp
from jax import lax
from jax.experimental import pallas as pl
from jax.experimental.pallas import tpu as pltpu
from jax.sharding import PartitionSpec as P

EPS = 1e-05
LOG2E = math.log2(math.e)
LN2 = math.log(2.0)
CUT = 1e30
LANES = 128
CHUNKS = 8
VMEM_LIMIT = 66_000_000
F32 = jnp.float32
BF16 = jnp.bfloat16


def silu_slope(values):
    sigma = jax.nn.sigmoid(values)
    return sigma * (1.0 + values * (1.0 - sigma))


def interleave(rows):
    count = rows.shape[0]
    return rows.reshape(CHUNKS, count // CHUNKS, -1).swapaxes(0, 1).reshape(count, -1)


def in_order(rows):
    count = rows.shape[0]
    return rows.reshape(count // CHUNKS, CHUNKS, -1).swapaxes(0, 1).reshape(count, -1)


def column_params(**kw):
    return pltpu.CompilerParams(
        dimension_semantics=("arbitrary",), vmem_limit_bytes=VMEM_LIMIT, **kw
    )


def cols(rows, width=LANES):
    return pl.BlockSpec((rows, width), lambda j: (0, j))


def whole(*shape):
    return pl.BlockSpec(shape, lambda j: (0,) * len(shape))


def conv_taps(conv_ref, halo_ref, steps, reach):
    width = conv_ref.shape[1]
    own = conv_ref[...].astype(F32).reshape(steps, CHUNKS, width)
    tail = own[steps - reach :]
    moved = pltpu.roll(tail.reshape(reach * CHUNKS, width), 1, 0).reshape(reach, CHUNKS, width)
    first = lax.broadcasted_iota(jnp.int32, moved.shape, 1) == 0
    halo = halo_ref[...].astype(F32)[:, None, :]
    head = jnp.where(first, jnp.broadcast_to(halo, moved.shape), moved)
    return jnp.concatenate([head, own], axis=0)


def select_kernel(conv_ref, halo_ref, same_ref, small_ref, sel_ref, act_ref, pre_ref, out_ref, acc):
    j = pl.program_id(0)
    count, width = conv_ref.shape
    reach = halo_ref.shape[0]
    steps = count // CHUNKS
    ext = conv_taps(conv_ref, halo_ref, steps, reach)
    pre = jnp.broadcast_to(small_ref[reach + 1 : reach + 2, :], (count, width)).reshape(
        steps, CHUNKS, width
    )
    for k in range(reach + 1):
        weight = small_ref[k : k + 1, :]
        same = same_ref[k][:, :, None]
        pre = pre + (weight[None] * ext[k : k + steps]) * same
    pre = pre.reshape(count, width)
    pre_ref[...] = pre
    act = (pre * jax.nn.sigmoid(pre)).astype(BF16)
    act_ref[...] = act

    @pl.when(j == 0)
    def _():
        acc[...] = jnp.zeros_like(acc)

    acc[...] += lax.dot_general(
        act, sel_ref[...], (((1,), (1,)), ((), ())), preferred_element_type=F32
    )
    out_ref[...] = acc[...]


def select_call(conv_in, halo, same, small, sel):
    count, inner = conv_in.shape
    width = min(512, inner)
    wide = sel.shape[0]
    return pl.pallas_call(
        select_kernel,
        grid=(inner // width,),
        in_specs=[
            cols(count, width),
            cols(halo.shape[0], width),
            whole(*same.shape),
            cols(small.shape[0], width),
            cols(wide, width),
        ],
        out_specs=[cols(count, width), cols(count, width), whole(count, wide)],
        out_shape=[
            jax.ShapeDtypeStruct((count, inner), BF16),
            jax.ShapeDtypeStruct((count, inner), F32),
            jax.ShapeDtypeStruct((count, wide), F32),
        ],
        scratch_shapes=[pltpu.VMEM((count, wide), F32)],
        compiler_params=column_params(),
        name="conv_select",
    )(conv_in, halo, same, small, sel)


def spread(dst, src_ref, nstate, at):
    for n in range(nstate):
        dst[n] = jnp.broadcast_to(src_ref[:, at + n : at + n + 1], dst.shape[1:])


def chunk_links(ends, sums, rates, backward):
    row = lax.broadcasted_iota(jnp.int32, (CHUNKS, LANES), 0)
    gains = [jnp.exp2(sums * rate) for rate in rates]
    ends = list(ends)
    total = sums
    k = 1
    while k < CHUNKS:
        turn = CHUNKS - k if backward else k
        mask = row < CHUNKS - k if backward else row >= k
        ends = [
            jnp.where(mask, g * pltpu.roll(e, turn, 0) + e, e) for g, e in zip(gains, ends)
        ]
        gains = [jnp.where(mask, g * pltpu.roll(g, turn, 0), g) for g in gains]
        total = jnp.where(mask, pltpu.roll(total, turn, 0) + total, total)
        k *= 2
    turn = CHUNKS - 1 if backward else 1
    mask = row < CHUNKS - 1 if backward else row >= 1
    entering = [jnp.where(mask, pltpu.roll(e, turn, 0), 0.0) for e in ends]
    before = jnp.where(mask, pltpu.roll(total, turn, 0), 0.0)
    last = 0 if backward else CHUNKS - 1
    return entering, [e[last : last + 1] for e in ends], before, total[last : last + 1]


def rate_rows(rate_ref, nstate):
    return [jnp.broadcast_to(rate_ref[n : n + 1, :], (CHUNKS, LANES)) for n in range(nstate)]


def arriving_state(me, totals_ref, sums_ref, lanes, rate_ref, backward):
    devices = totals_ref.shape[0]
    state = jnp.zeros(rate_ref.shape, F32)
    order = range(devices - 1, 0, -1) if backward else range(devices - 1)
    for k in order:
        passed = jnp.exp2(rate_ref[...] * sums_ref[k, :, lanes]) * state
        passed = passed + totals_ref[k, :, lanes].astype(F32)
        state = jnp.where((k > me) if backward else (k < me), passed, state)
    return state


def conv_grad_kernel(
    conv_ref, halo_ref, same_ref, small_ref, sel_ref, act_ref, pre_ref, dact_ref, dsel_ref,
    dconv_ref, tail_ref, spill_ref, gsel_ref, gsmall_ref,
):
    count, width = conv_ref.shape
    reach = halo_ref.shape[0]
    steps = count // CHUNKS
    ext = conv_taps(conv_ref, halo_ref, steps, reach)
    dsel = dsel_ref[...]
    gsel_ref[...] = lax.dot_general(
        dsel, act_ref[...], (((0,), (0,)), ((), ())), preferred_element_type=F32
    )
    dact = dact_ref[...] + jnp.dot(dsel, sel_ref[...], preferred_element_type=F32)
    dpre = dact * silu_slope(pre_ref[...])
    gsmall_ref[reach + 1 : reach + 2, :] = jnp.sum(dpre, axis=0, keepdims=True)
    dpre = dpre.reshape(steps, CHUNKS, width)
    parts = []
    for k in range(reach + 1):
        masked = dpre * same_ref[k][:, :, None]
        gsmall_ref[k : k + 1, :] = jnp.sum(
            (masked * ext[k : k + steps]).reshape(count, width), axis=0, keepdims=True
        )
        parts.append(masked * small_ref[k : k + 1, :][None])
    own = parts[reach]
    for k in range(reach):
        back = reach - k
        own = own + jnp.concatenate(
            [parts[k][back:], jnp.zeros((back, CHUNKS, width), F32)], axis=0
        )
    heads = []
    for e in range(reach):
        total = parts[0][e]
        for k in range(1, e + 1):
            total = total + parts[k][e - k]
        heads.append(total)
    head = jnp.stack(heads)
    spill_ref[...] = head[:, 0, :]
    row = lax.broadcasted_iota(jnp.int32, head.shape, 1)
    moved = pltpu.roll(head.reshape(reach * CHUNKS, width), reach * CHUNKS - 1, 0)
    moved = jnp.where(row == CHUNKS - 1, 0.0, moved.reshape(head.shape))
    tail = own[steps - reach :] + moved
    tail_ref[...] = tail[:, CHUNKS - 1, :]
    dconv = jnp.concatenate([own[: steps - reach], tail], axis=0)
    dconv_ref[...] = dconv.reshape(count, width).astype(BF16)


def conv_grad(conv_in, halo, same, small, sel, act, pre, dact, dsel):
    count, inner = act.shape
    width = min(512, inner)
    reach = halo.shape[0]
    wide = sel.shape[0]
    return pl.pallas_call(
        conv_grad_kernel,
        grid=(inner // width,),
        in_specs=[
            cols(count, width),
            cols(reach, width),
            whole(*same.shape),
            cols(small.shape[0], width),
            cols(wide, width),
            cols(count, width),
            cols(count, width),
            cols(count, width),
            whole(count, wide),
        ],
        out_specs=[
            cols(count, width),
            cols(reach, width),
            cols(reach, width),
            cols(wide, width),
            cols(8, width),
        ],
        out_shape=[
            jax.ShapeDtypeStruct((count, inner), BF16),
            jax.ShapeDtypeStruct((reach, inner), F32),
            jax.ShapeDtypeStruct((reach, inner), F32),
            jax.ShapeDtypeStruct((wide, inner), F32),
            jax.ShapeDtypeStruct((8, inner), F32),
        ],
        compiler_params=column_params(),
        name="conv_grad",
    )(conv_in, halo, same, small, sel, act, pre, dact, dsel)


def shifted(value, axis, steps):
    count = lax.axis_size(axis)
    first, last = (max(0, -steps), min(count, count - steps))
    return lax.ppermute(value, axis, [(source, source + steps) for source in range(first, last)])


MESH = pl.DeviceIdType.MESH


def where_am_i():
    c, d, z = lax.axis_index("section"), lax.axis_index("dp"), lax.axis_index("seq")
    y, x = d // 2, d % 2
    flip_x, flip_y = y * 2 + (1 - x), (1 - y) * 2 + x
    return c, y, x, z, flip_x, flip_y


def peers_of(depth):
    c, y, x, z, flip_x, flip_y = where_am_i()
    peers = [{"section": 1 - c}, {"dp": flip_x}, {"dp": flip_y}]
    return peers + [{"seq": lax.rem(z + o, depth)} for o in range(1, depth)]


def hail(depth):
    barrier = pltpu.get_barrier_semaphore()
    for peer in peers_of(depth):
        pl.semaphore_signal(barrier, inc=1, device_id=peer, device_id_type=MESH)


def await_hails(depth):
    pl.semaphore_wait(pltpu.get_barrier_semaphore(), 2 + depth)


def greet(depth):
    hail(depth)
    await_hails(depth)


def pipeline(stages, count, lags):
    for turn in range(count + lags[-1]):
        for lag, stage in zip(lags, stages):
            if 0 <= turn - lag < count:
                stage(turn - lag)


class Gather:
    def __init__(self, depth, layer, width, base, src, out, mine, send, recv, local):
        self.depth, self.layer, self.width, self.base = depth, layer, width, base
        self.src, self.out, self.mine = src, out, mine
        self.send, self.recv, self.local = send, recv, local
        self.count = mine.shape[0]
        c, y, x, z, flip_x, flip_y = where_am_i()
        self.c, self.y, self.x, self.z = c, y, x, z
        self.near = {"dp": (1 - c) * flip_y + c * flip_x}
        self.far = {"dp": (1 - c) * flip_x + c * flip_y}
        self.near_at = (y + (1 - c) * (1 - 2 * y), x + c * (1 - 2 * x))
        self.far_at = (y + c * (1 - 2 * y), x + (1 - c) * (1 - 2 * x))
        self.partner = {"section": 1 - c}

    def cols(self, k, base=0):
        if isinstance(k, int):
            return pl.ds(base + k * self.width, self.width)
        return pl.ds(pl.multiple_of(base + k * self.width, LANES), self.width)

    def remote(self, k, slot, src, dst, peer):
        return pltpu.make_async_remote_copy(
            src_ref=src, dst_ref=dst, send_sem=self.send.at[k, slot], recv_sem=self.recv.at[k, slot],
            device_id=peer, device_id_type=MESH,
        )

    def piece(self, k, at):
        return self.out.at[at[0], at[1], :, self.c, :, self.cols(k)]

    def hand(self, k):
        half = self.mine.shape[1]
        src = self.src.at[pl.ds((1 - self.layer) * half, half), self.cols(k, self.base)]
        return self.remote(k, 0, src, self.mine.at[k], self.partner)

    def keep(self, k):
        half = self.mine.shape[1]
        src = self.src.at[pl.ds(self.layer * half, half), self.cols(k, self.base)]
        return pltpu.make_async_copy(src, self.mine.at[k], self.local.at[k, 0])

    def line(self, k):
        target = self.out.at[self.y, self.x, self.z, self.c, :, self.cols(k)]
        return [
            self.remote(k, o, self.mine.at[k], target, {"seq": lax.rem(self.z + o, self.depth)})
            for o in range(1, self.depth)
        ]

    def place(self, k):
        target = self.out.at[self.y, self.x, self.z, self.c, :, self.cols(k)]
        return pltpu.make_async_copy(self.mine.at[k], target, self.local.at[k, 1])

    def move(self, k, slot, at, peer):
        return self.remote(k, self.depth + slot, self.piece(k, at), self.piece(k, at), peer)

    def near_own(self, k):
        return self.move(k, 0, (self.y, self.x), self.near)

    def far_own(self, k):
        return self.move(k, 1, (self.y, self.x), self.far)

    def far_other(self, k):
        return self.move(k, 2, self.near_at, self.far)

    def crossings(self, k):
        places = ((self.y, self.x), self.near_at, self.far_at, (1 - self.y, 1 - self.x))
        return [lambda i=i, at=at: self.move(k, 3 + i, at, self.partner) for i, at in enumerate(places)]

    def first(self, k):
        @pl.when(self.c == self.layer)
        def _():
            self.hand(k).start()
            self.keep(k).start()

    def along_z(self, k):
        @pl.when(self.c == self.layer)
        def _():
            self.hand(k).wait_send()
            self.keep(k).wait()

        @pl.when(self.c != self.layer)
        def _():
            self.hand(k).wait_recv()

        for copy in self.line(k):
            copy.start()
        self.place(k).start()

    def along_near(self, k):
        for copy in self.line(k):
            copy.wait_recv()
        self.place(k).wait()
        self.near_own(k).start()
        self.crossings(k)[0]().start()

    def along_far(self, k):
        self.near_own(k).wait_recv()
        self.far_own(k).start()
        self.far_other(k).start()
        self.crossings(k)[1]().start()

    def across(self, k):
        self.far_own(k).wait_recv()
        self.far_other(k).wait_recv()
        self.crossings(k)[2]().start()
        self.crossings(k)[3]().start()

    def finish(self, k):
        for copy in self.crossings(k):
            copy().wait()
        for copy in self.line(k) + [self.near_own(k), self.far_own(k), self.far_other(k)]:
            copy.wait_send()

    def stages(self):
        return [self.along_z, self.along_near, self.along_far, self.across, self.finish]


def gather_scratch(specs, depth):
    scratch = []
    for rows, columns, width, dtype in specs:
        chunks = columns // width
        scratch += [
            pltpu.VMEM((chunks, rows // 2, width), dtype),
            pltpu.SemaphoreType.DMA((chunks, depth + 7)),
            pltpu.SemaphoreType.DMA((chunks, depth + 7)),
            pltpu.SemaphoreType.DMA((chunks, 2)),
        ]
    return scratch


def gather_shape(rows, columns, depth, dtype):
    return jax.ShapeDtypeStruct((2, 2, depth, 2, rows // 2, columns), dtype)


def gather_kernel(tasks, depth, *refs):
    count = len(tasks)
    srcs, outs, rest = refs[:count], refs[count : 2 * count], refs[2 * count :]
    greet(depth)
    work = []
    for i, (layer, width, base) in enumerate(tasks):
        gather = Gather(depth, layer, width, base, srcs[i], outs[i], *rest[4 * i : 4 * i + 4])
        work += [(gather, k) for k in range(gather.count)]
    for gather, k in work:
        gather.first(k)
    pipeline(
        [lambda i, s=s: work[i][0].stages()[s](work[i][1]) for s in range(5)],
        len(work), (0, 2, 4, 6, 8),
    )


def gather_rows(sources, tasks, columns, collective):
    depth = lax.axis_size("seq")
    anywhere = pl.BlockSpec(memory_space=pl.ANY)
    outs = pl.pallas_call(
        functools.partial(gather_kernel, tasks, depth),
        in_specs=[anywhere] * len(sources),
        out_specs=[anywhere] * len(sources),
        out_shape=[
            gather_shape(s.shape[0], n, depth, s.dtype) for s, n in zip(sources, columns)
        ],
        scratch_shapes=gather_scratch(
            [(s.shape[0], n, t[1], s.dtype) for s, t, n in zip(sources, tasks, columns)], depth
        ),
        compiler_params=pltpu.CompilerParams(
            collective_id=collective, has_side_effects=True, vmem_limit_bytes=VMEM_LIMIT
        ),
        name="gather_rows",
    )(*sources)
    return [flat_rows(out) for out in outs]


def flat_rows(out):
    return out.reshape(-1, out.shape[-1])


class Reduce:
    def __init__(self, depth, layer, width, src, out, own, core, side, edge, line, done, send, recv, local):
        self.depth, self.layer, self.width, self.src, self.out = depth, layer, width, src, out
        self.own, self.core, self.side, self.edge, self.line = own, core, side, edge, line
        self.done, self.send, self.recv, self.local = done, send, recv, local
        self.count = own.shape[0]
        self.half = own.shape[4]
        c, y, x, z, flip_x, flip_y = where_am_i()
        self.c, self.y, self.x, self.z = c, y, x, z
        self.near = {"dp": (1 - c) * flip_x + c * flip_y}
        self.far = {"dp": (1 - c) * flip_y + c * flip_x}
        self.kept = (1 - c) * y + c * x
        self.partner = {"section": 1 - c}

    def cols(self, k):
        if isinstance(k, int):
            return pl.ds(k * self.width, self.width)
        return pl.ds(pl.multiple_of(k * self.width, LANES), self.width)

    def remote(self, k, slot, src, dst, peer):
        return pltpu.make_async_remote_copy(
            src_ref=src, dst_ref=dst, send_sem=self.send.at[k, slot], recv_sem=self.recv.at[k, slot],
            device_id=peer, device_id_type=MESH,
        )

    def hand(self, k):
        theirs = self.src.at[:, :, :, pl.ds((1 - self.c) * self.half, self.half), self.cols(k)]
        return self.remote(k, 0, theirs, self.core.at[k], self.partner)

    def keep(self, k):
        ours = self.src.at[:, :, :, pl.ds(self.c * self.half, self.half), self.cols(k)]
        return pltpu.make_async_copy(ours, self.own.at[k], self.local.at[k, 0])

    def sides(self, k):
        c = self.c
        return [
            self.remote(
                k, 1 + u,
                self.core.at[k, (1 - c) * u + c * (1 - self.y), (1 - c) * (1 - self.x) + c * u],
                self.side.at[k, u], self.near,
            )
            for u in (0, 1)
        ]

    def edges(self, k):
        return self.remote(k, 3, self.side.at[k, 1 - self.kept], self.edge.at[k], self.far)

    def lines(self, k):
        copies = []
        for o in range(1, self.depth):
            peer = lax.rem(self.z + o, self.depth)
            copies.append(
                self.remote(k, 3 + o, self.edge.at[k, peer], self.line.at[k, o - 1], {"seq": peer})
            )
        return copies

    def target(self):
        return pl.ds(self.c * self.half, self.half)

    def give(self, k):
        target = self.out.at[self.target(), self.cols(k)]
        return self.remote(k, 3 + self.depth, self.done.at[k], target, self.partner)

    def take(self, k):
        target = self.out.at[self.target(), self.cols(k)]
        return pltpu.make_async_copy(self.done.at[k], target, self.local.at[k, 1])

    def to_core(self, k):
        self.hand(k).start()
        self.keep(k).start()

    def to_near(self, k):
        self.hand(k).wait_recv()
        self.keep(k).wait()
        core, own, depth = self.core, self.own, self.depth

        def add(i, _):
            a, b, e = i // (2 * depth), (i // depth) % 2, i % depth
            core[k, a, b, e] = core[k, a, b, e] + own[k, a, b, e]
            return 0

        lax.fori_loop(0, 4 * depth, add, 0)
        for copy in self.sides(k):
            copy.start()

    def to_far(self, k):
        for copy in self.sides(k):
            copy.wait_recv()
        core, side, depth, c = self.core, self.side, self.depth, self.c

        def add(i, _):
            u, e = i // depth, i % depth
            kept = core[k, (1 - c) * u + c * self.y, (1 - c) * self.x + c * u, e]
            side[k, u, e] = side[k, u, e] + kept
            return 0

        lax.fori_loop(0, 2 * depth, add, 0)
        self.edges(k).start()

    def to_line(self, k):
        self.edges(k).wait_recv()
        edge, side = self.edge, self.side

        def add(e, _):
            edge[k, e] = edge[k, e] + side[k, self.kept, e]
            return 0

        lax.fori_loop(0, self.depth, add, 0)
        for copy in self.lines(k):
            copy.start()

    def to_end(self, k):
        for copy in self.lines(k):
            copy.wait_recv()
        total = self.edge[k, self.z].astype(F32)
        for o in range(self.depth - 1):
            total = total + self.line[k, o].astype(F32)
        self.done[k] = total

        @pl.when(self.c == self.layer)
        def _():
            self.take(k).start()

        @pl.when(self.c != self.layer)
        def _():
            self.give(k).start()

    def finish(self, k):
        @pl.when(self.c == self.layer)
        def _():
            self.take(k).wait()
            self.give(k).wait_recv()

        @pl.when(self.c != self.layer)
        def _():
            self.give(k).wait_send()

        for copy in [self.hand(k), self.edges(k)] + self.sides(k) + self.lines(k):
            copy.wait_send()

    def stages(self):
        return [self.to_core, self.to_near, self.to_far, self.to_line, self.to_end, self.finish]


def reduce_scratch(specs, depth):
    scratch = []
    for rows, columns, width, dtype in specs:
        chunks, block = columns // width, (rows // 2, width)
        scratch += [
            pltpu.VMEM((chunks, 2, 2, depth) + block, dtype),
            pltpu.VMEM((chunks, 2, 2, depth) + block, dtype),
            pltpu.VMEM((chunks, 2, depth) + block, dtype),
            pltpu.VMEM((chunks, depth) + block, dtype),
            pltpu.VMEM((chunks, depth - 1) + block, dtype),
            pltpu.VMEM((chunks,) + block, F32),
            pltpu.SemaphoreType.DMA((chunks, depth + 4)),
            pltpu.SemaphoreType.DMA((chunks, depth + 4)),
            pltpu.SemaphoreType.DMA((chunks, 2)),
        ]
    return scratch


def by_chip(value, depth):
    return value.reshape((2, 2, depth) + value.shape[1:])


def reduce_kernel(tasks, depth, *refs):
    count = len(tasks)
    srcs, outs, rest = refs[:count], refs[count : 2 * count], refs[2 * count :]
    greet(depth)
    work = []
    for i, (layer, width) in enumerate(tasks):
        item = Reduce(depth, layer, width, srcs[i], outs[i], *rest[9 * i : 9 * i + 9])
        work += [(item, k) for k in range(item.count)]
    pipeline(
        [lambda i, s=s: work[i][0].stages()[s](work[i][1]) for s in range(6)],
        len(work), (0, 1, 3, 5, 7, 9),
    )


def reduce_rows(values, tasks, collective):
    depth = lax.axis_size("seq")
    anywhere = pl.BlockSpec(memory_space=pl.ANY)
    return pl.pallas_call(
        functools.partial(reduce_kernel, tasks, depth),
        in_specs=[anywhere] * len(values),
        out_specs=[anywhere] * len(values),
        out_shape=[jax.ShapeDtypeStruct(v.shape[1:], F32) for v in values],
        scratch_shapes=reduce_scratch(
            [v.shape[1:] + (t[1], v.dtype) for v, t in zip(values, tasks)], depth
        ),
        compiler_params=pltpu.CompilerParams(
            collective_id=collective, has_side_effects=True, vmem_limit_bytes=VMEM_LIMIT
        ),
        name="reduce_rows",
    )(*[by_chip(v, depth) for v in values])


def scan_map(phases, shift=0):
    def index(p, j, last):
        if phases == 2:
            return shift + j
        if phases == 0:
            return shift + j * (1 - p) + last * p
        return shift + j * p

    return index


def spec(rows, last, phases, width=LANES):
    index = scan_map(phases)
    return pl.BlockSpec((rows, width), lambda p, j: (0, index(p, j, last)))


def fixed(*shape):
    return pl.BlockSpec(shape, lambda p, j: (0,) * len(shape))


def timetable(turn, blocks, weight, slots, works):
    total = sum(count for count, _ in works)
    if not total:
        return
    span = (blocks - 1) * (1 + weight) + 1 - slots[-1]
    assert total * weight <= span + weight

    def chunk(at, start):
        past = jnp.where(at < blocks, at, blocks + (at - blocks) * weight) - start
        return jnp.where((past < 0) | (at < 0), -1, past * total // span)

    for stage, start in enumerate(slots):
        k = chunk(turn, start)
        due = (k != chunk(turn - 1, start)) & (k < total)
        base = 0
        for count, stages in works:
            local = k - base

            @pl.when(due & (local >= 0) & (local < count))
            def _(stages=stages, local=local, stage=stage):
                stages[stage](local)

            base += count

    @pl.when(turn == 2 * blocks - 1)
    def _():
        for count, stages in works:
            lax.fori_loop(0, count, lambda k, _, s=stages[-1]: (s(k), 0)[1], 0)


def exchange(total_ref, sum_ref, totals_ref, sums_ref, send, recv):
    count = totals_ref.shape[0]
    me = lax.axis_index("seq")
    copies = []
    for o in range(1, count):
        peer = {"seq": lax.rem(me + o, count)}
        for i, (src, dst) in enumerate(((total_ref, totals_ref), (sum_ref, sums_ref))):
            copies.append(
                pltpu.make_async_remote_copy(
                    src_ref=src, dst_ref=dst.at[me], send_sem=send.at[i, o - 1],
                    recv_sem=recv.at[i, o - 1], device_id=peer, device_id_type=MESH,
                )
            )
    for copy in copies:
        copy.start()
    for copy in copies:
        copy.wait()


def forward_scan_kernel(
    tasks, depth, lead, stepw_ref, small_ref, act_ref, sel_ref, cut_ref, rate_ref, *refs
):
    hosted = len(tasks)
    srcs, refs = refs[:hosted], refs[hosted:]
    (step_ref, sig_ref, moment_ref, full_ref, keep_ref), refs = refs[:5], refs[5:]
    gouts, refs = refs[:hosted], refs[hosted:]
    (low, inb, outb, decay, drives, enter, befores, total_ref, sum_ref, totals_ref, sums_ref, send, recv), rest = refs[:13], refs[13:]
    count = act_ref.shape[0]
    nstate = rate_ref.shape[0]
    rank = low.shape[1]
    p, j = pl.program_id(0), pl.program_id(1)
    blocks = pl.num_programs(1)
    turn = p * blocks + j
    me = lax.axis_index("seq")
    lanes = pl.ds(pl.multiple_of(j * LANES, LANES), LANES)
    gathers = [
        Gather(depth, layer, width, base, srcs[i], gouts[i], *rest[4 * i : 4 * i + 4])
        for i, (layer, width, base, _) in enumerate(tasks)
    ]

    @pl.when(turn == 0)
    def _():
        hail(depth)
        low[...] = sel_ref[:, :rank].astype(BF16)
        spread(inb, sel_ref, nstate, rank)
        spread(outb, sel_ref, nstate, rank + nstate)

    @pl.when(turn == 1)
    def _():
        await_hails(depth)
        for gather in gathers:
            lax.fori_loop(0, gather.count, lambda k, _, g=gather: (g.first(k), 0)[1], 0)

    timetable(turn, lead, 1, (2, 5, 9, 14), [(g.count, g.stages()) for g in gathers])

    @pl.when(p == 0)
    def _():
        pre = jnp.dot(low[...], stepw_ref[...], preferred_element_type=F32) + small_ref[5:6, :]
        near = jnp.exp(-jnp.abs(pre))
        step_all = jnp.maximum(pre, 0.0) + jnp.log1p(near)
        step_ref[...] = step_all
        sig_ref[...] = jnp.where(pre >= 0.0, 1.0, near) / (1.0 + near)
        moment_ref[0:1, :] = jnp.sum(step_all, axis=0, keepdims=True)
        moment_ref[1:2, :] = jnp.sum(step_all * step_all, axis=0, keepdims=True)
        rates = rate_rows(rate_ref, nstate)

        def body(pair, carry):
            states, sums = carry
            act = act_ref[pl.ds(pl.multiple_of(pair * 16, 16), 16), :].astype(F32)
            for half in (0, 1):
                at = pl.ds(pl.multiple_of(pair * 16 + half * 8, 8), 8)
                step = step_ref[at, :]
                away = step + cut_ref[at, :]
                drive = step * act[half * 8 : half * 8 + 8]
                drives[j, at, :] = drive
                sums = sums + away
                new = []
                for n in range(nstate):
                    gain = jnp.exp2(away * rates[n])
                    decay[j, n, at, :] = gain
                    new.append(gain * states[n] + drive * inb[n, at, :])
                states = tuple(new)
            return states, sums

        zero = jnp.zeros((CHUNKS, LANES), F32)
        ends, sums = lax.fori_loop(0, count // 16, body, ((zero,) * nstate, zero), unroll=2)
        entering, totals, before, total = chunk_links(ends, sums, rates, False)
        for n in range(nstate):
            enter[j, n] = entering[n]
        total_ref[:, lanes] = jnp.concatenate(totals, axis=0).astype(total_ref.dtype)
        befores[j] = before
        sum_ref[:, lanes] = total

    @pl.when(turn == blocks)
    def _():
        exchange(total_ref, sum_ref, totals_ref, sums_ref, send, recv)

    @pl.when(p == 1)
    def _():
        rates = rate_rows(rate_ref, nstate)
        arrived = arriving_state(me, totals_ref, sums_ref, lanes, rate_ref, False)
        before = befores[j]
        states = tuple(
            enter[j, n] + jnp.exp2(before * rates[n]) * arrived[n : n + 1, :] for n in range(nstate)
        )
        skip = jnp.broadcast_to(small_ref[6:7, :], (CHUNKS, LANES))

        def body(pair, states):
            rows = pl.ds(pl.multiple_of(pair * 16, 16), 16)
            act = act_ref[rows, :].astype(F32)
            held = []
            for half in (0, 1):
                at = pl.ds(pl.multiple_of(pair * 16 + half * 8, 8), 8)
                held.append(states)
                drive = drives[j, at, :]
                out = skip * act[half * 8 : half * 8 + 8]
                new = []
                for n in range(nstate):
                    state = decay[j, n, at, :] * states[n] + drive * inb[n, at, :]
                    out = out + state * outb[n, at, :]
                    new.append(state)
                states = tuple(new)
                full_ref[at, :] = out
            for n in range(nstate):
                both = jnp.concatenate([held[0][n], held[1][n]], axis=0)
                keep_ref[0, n, rows, :] = both.astype(keep_ref.dtype)
            return states

        ends = lax.fori_loop(0, count // 16, body, states, unroll=2)
        for n in range(nstate):
            both = jnp.concatenate([ends[n], ends[n]], axis=0)
            keep_ref[0, n, count : count + 16, :] = both.astype(keep_ref.dtype)


def forward_scan(stepw, small, act, selected, cut, rate, sources, tasks, collective):
    count, inner = act.shape
    nstate, rank = rate.shape[0], stepw.shape[0]
    depth = lax.axis_size("seq")
    blocks = inner // LANES
    last = blocks - 1
    anywhere = pl.BlockSpec(memory_space=pl.ANY)
    outs = pl.pallas_call(
        functools.partial(forward_scan_kernel, tasks, depth, blocks),
        grid=(2, blocks),
        in_specs=[
            spec(rank, last, 0),
            spec(small.shape[0], last, 2),
            spec(count, last, 2),
            fixed(*selected.shape),
            fixed(count, LANES),
            spec(nstate, last, 2),
        ]
        + [anywhere] * len(tasks),
        out_specs=[
            spec(count, last, 0),
            spec(count, last, 0),
            spec(2, last, 0),
            spec(count, last, 1),
            pl.BlockSpec((1, nstate, count + 16, LANES), lambda p, j: (j * p, 0, 0, 0)),
        ]
        + [anywhere] * len(tasks),
        out_shape=[
            jax.ShapeDtypeStruct((count, inner), F32),
            jax.ShapeDtypeStruct((count, inner), F32),
            jax.ShapeDtypeStruct((2, inner), F32),
            jax.ShapeDtypeStruct((count, inner), F32),
            jax.ShapeDtypeStruct((blocks, nstate, count + 16, LANES), BF16),
        ]
        + [gather_shape(s.shape[0], t[3], depth, s.dtype) for s, t in zip(sources, tasks)],
        scratch_shapes=[
            pltpu.VMEM((count, rank), BF16),
            pltpu.VMEM((nstate, count, LANES), F32),
            pltpu.VMEM((nstate, count, LANES), F32),
            pltpu.VMEM((blocks, nstate, count, LANES), F32),
            pltpu.VMEM((blocks, count, LANES), F32),
            pltpu.VMEM((blocks, nstate, CHUNKS, LANES), F32),
            pltpu.VMEM((blocks, CHUNKS, LANES), F32),
            pltpu.VMEM((nstate, inner), BF16),
            pltpu.VMEM((1, inner), F32),
            pltpu.VMEM((depth, nstate, inner), BF16),
            pltpu.VMEM((depth, 1, inner), F32),
            pltpu.SemaphoreType.DMA((2, depth - 1)),
            pltpu.SemaphoreType.DMA((2, depth - 1)),
        ]
        + gather_scratch([(s.shape[0], t[3], t[1], s.dtype) for s, t in zip(sources, tasks)], depth),
        compiler_params=pltpu.CompilerParams(
            dimension_semantics=("arbitrary", "arbitrary"), collective_id=collective,
            has_side_effects=True, vmem_limit_bytes=VMEM_LIMIT,
        ),
        name="forward_scan",
    )(stepw, small, act, selected, cut, rate, *sources)
    return outs[:5], [flat_rows(out) for out in outs[5:]]


def backward_scan_kernel(
    tasks, depth, lead, dfull_ref, step_ref, cut_ref, rate_ref, sel_ref, act_ref, sig_ref, keep_ref,
    small_ref, stepw_ref, *refs
):
    hosted = len(tasks)
    srcs, refs = refs[:hosted], refs[hosted:]
    (dact_ref, gbias_ref, gskip_ref, gdecay_ref, gstepw_ref, dsel_ref), refs = refs[:6], refs[6:]
    gouts, refs = refs[:hosted], refs[hosted:]
    (
        low, inb, outb, decay, enter, befores, total_ref, sum_ref, totals_ref, sums_ref,
        din_acc, dout_acc, decay_acc, dlow_acc, dstep_buf, send, recv,
    ), rest = refs[:17], refs[17:]
    count = act_ref.shape[0]
    nstate = rate_ref.shape[0]
    rank = low.shape[1]
    pairs = count // 16
    p, j = pl.program_id(0), pl.program_id(1)
    blocks = pl.num_programs(1)
    turn = p * blocks + j
    me = lax.axis_index("seq")
    lanes = pl.ds(pl.multiple_of(j * LANES, LANES), LANES)
    items = [
        Reduce(depth, layer, width, srcs[i], gouts[i], *rest[9 * i : 9 * i + 9])
        for i, (layer, width) in enumerate(tasks)
    ]

    @pl.when(turn == 0)
    def _():
        hail(depth)
        low[...] = sel_ref[:, :rank].astype(BF16)
        spread(inb, sel_ref, nstate, rank)
        spread(outb, sel_ref, nstate, rank + nstate)
        din_acc[...] = jnp.zeros_like(din_acc)
        dout_acc[...] = jnp.zeros_like(dout_acc)
        dlow_acc[...] = jnp.zeros_like(dlow_acc)

    @pl.when(turn == 1)
    def _():
        await_hails(depth)

    timetable(
        turn, lead, 2, (1, 4, 8, 11, 14), [(item.count, item.stages()) for item in items]
    )

    @pl.when(p == 0)
    def _():
        rates = rate_rows(rate_ref, nstate)

        def body(step_back, carry):
            states, sums = carry
            pair = pairs - 1 - step_back
            for half in (1, 0):
                at = pl.ds(pl.multiple_of(pair * 16 + half * 8, 8), 8)
                away = step_ref[at, :] + cut_ref[at, :]
                grad = dfull_ref[at, :]
                sums = sums + away
                new = []
                for n in range(nstate):
                    gain = jnp.exp2(away * rates[n])
                    decay[j, n, at, :] = gain
                    new.append(gain * (states[n] + outb[n, at, :] * grad))
                states = tuple(new)
            return states, sums

        zero = jnp.zeros((CHUNKS, LANES), F32)
        ends, sums = lax.fori_loop(0, pairs, body, ((zero,) * nstate, zero), unroll=2)
        entering, totals, before, total = chunk_links(ends, sums, rates, True)
        for n in range(nstate):
            enter[j, n] = entering[n]
        total_ref[:, lanes] = jnp.concatenate(totals, axis=0).astype(total_ref.dtype)
        befores[j] = before
        sum_ref[:, lanes] = total

    @pl.when(turn == blocks)
    def _():
        exchange(total_ref, sum_ref, totals_ref, sums_ref, send, recv)

    @pl.when(p == 1)
    def _():
        rates = rate_rows(rate_ref, nstate)
        arrived = arriving_state(me, totals_ref, sums_ref, lanes, rate_ref, True)
        before = befores[j]
        states = tuple(
            enter[j, n] + jnp.exp2(before * rates[n]) * arrived[n : n + 1, :] for n in range(nstate)
        )
        skip = jnp.broadcast_to(small_ref[6:7, :], (CHUNKS, LANES))
        for n in range(nstate):
            decay_acc[n] = jnp.zeros((CHUNKS, LANES), F32)
            last = keep_ref[0, n, count : count + 16, :].astype(F32)[0:CHUNKS]
            dout_acc[n, pl.ds(count, CHUNKS), :] += last * dfull_ref[pl.ds(count - CHUNKS, CHUNKS), :]

        def body(step_back, carry):
            states, gskip = carry
            pair = pairs - 1 - step_back
            rows = pl.ds(pl.multiple_of(pair * 16, 16), 16)
            act = act_ref[rows, :].astype(F32)
            held = [keep_ref[0, n, rows, :].astype(F32) for n in range(nstate)]
            sums = [None] * nstate
            for half in (1, 0):
                at = pl.ds(pl.multiple_of(pair * 16 + half * 8, 8), 8)
                step = step_ref[at, :]
                act_now = act[half * 8 : half * 8 + 8]
                drive = step * act_now
                grad = dfull_ref[at, :]
                gskip = gskip + grad * act_now
                if half:
                    earlier = dfull_ref[pl.ds(pl.multiple_of(pair * 16, 8), 8), :]
                else:
                    earlier = dfull_ref[pl.ds(pl.multiple_of(jnp.maximum(pair * 16 - 8, 0), 8), 8), :]
                by_rate = jnp.zeros((CHUNKS, LANES), F32)
                mapped = jnp.zeros((CHUNKS, LANES), F32)
                new = []
                for n in range(nstate):
                    prior = held[n][half * 8 : half * 8 + 8]
                    adjoint = states[n] + outb[n, at, :] * grad
                    passed = adjoint * decay[j, n, at, :]
                    rho = passed * prior
                    by_rate = by_rate + rho * rates[n]
                    mapped = mapped + adjoint * inb[n, at, :]
                    sums[n] = rho * step if half else sums[n] + rho * step
                    din_acc[n, at, :] += adjoint * drive
                    dout_acc[n, at, :] += prior * earlier
                    new.append(passed)
                states = tuple(new)
                dstep_buf[at, :] = by_rate * LN2 + act_now * mapped
                dact_ref[at, :] = step * mapped + skip * grad
            for n in range(nstate):
                decay_acc[n] += sums[n]
            return states, gskip

        _, gskip = lax.fori_loop(0, pairs, body, (states, jnp.zeros((CHUNKS, LANES), F32)))
        gskip_ref[...] = jnp.sum(gskip, axis=0, keepdims=True)
        for n in range(nstate):
            gdecay_ref[n : n + 1, :] = (rate_ref[n : n + 1, :] * LN2) * jnp.sum(
                decay_acc[n], axis=0, keepdims=True
            )
        dpre = dstep_buf[...] * sig_ref[...]
        gbias_ref[...] = jnp.sum(dpre, axis=0, keepdims=True)
        low_dpre = dpre.astype(BF16)
        gstepw_ref[...] = lax.dot_general(
            low[...], low_dpre, (((0,), (0,)), ((), ())), preferred_element_type=F32
        )
        dlow_acc[...] += lax.dot_general(
            low_dpre, stepw_ref[...], (((1,), (1,)), ((), ())), preferred_element_type=F32
        )

    @pl.when(turn == 2 * lead - 1)
    def _():
        column = lax.broadcasted_iota(jnp.int32, (LANES, nstate), 1)
        din = jnp.zeros((count, nstate), F32)
        dout = jnp.zeros((count, nstate), F32)
        for n in range(nstate):
            pick = (column == n).astype(BF16)
            din = din + jnp.dot(din_acc[n].astype(BF16), pick, preferred_element_type=F32)
            part = dout_acc[n, CHUNKS : count + CHUNKS, :].astype(BF16)
            dout = dout + jnp.dot(part, pick, preferred_element_type=F32)
        dsel_ref[...] = jnp.concatenate([dlow_acc[...], din, dout], axis=1).astype(BF16)


def backward_scan(
    dfull, step, cut, rate, selected, act, sig, keep, small, stepw, sources, tasks, collective
):
    count, inner = act.shape
    nstate, rank = rate.shape[0], stepw.shape[0]
    depth = lax.axis_size("seq")
    blocks = inner // LANES
    last = blocks - 1
    anywhere = pl.BlockSpec(memory_space=pl.ANY)
    outs = pl.pallas_call(
        functools.partial(backward_scan_kernel, tasks, depth, blocks),
        grid=(2, blocks),
        in_specs=[
            spec(count, last, 2),
            spec(count, last, 2),
            fixed(count, LANES),
            spec(nstate, last, 2),
            fixed(*selected.shape),
            spec(count, last, 1),
            spec(count, last, 1),
            pl.BlockSpec((1, nstate, count + 16, LANES), lambda p, j: (j * p, 0, 0, 0)),
            spec(small.shape[0], last, 1),
            spec(rank, last, 1),
        ]
        + [anywhere] * len(tasks),
        out_specs=[
            spec(count, last, 1),
            spec(1, last, 1),
            spec(1, last, 1),
            spec(nstate, last, 1),
            spec(rank, last, 1),
            fixed(*selected.shape),
        ]
        + [anywhere] * len(tasks),
        out_shape=[
            jax.ShapeDtypeStruct((count, inner), F32),
            jax.ShapeDtypeStruct((1, inner), F32),
            jax.ShapeDtypeStruct((1, inner), F32),
            jax.ShapeDtypeStruct((nstate, inner), F32),
            jax.ShapeDtypeStruct((rank, inner), F32),
            jax.ShapeDtypeStruct(selected.shape, BF16),
        ]
        + [jax.ShapeDtypeStruct(s.shape[1:], F32) for s in sources],
        scratch_shapes=[
            pltpu.VMEM((count, rank), BF16),
            pltpu.VMEM((nstate, count, LANES), F32),
            pltpu.VMEM((nstate, count, LANES), F32),
            pltpu.VMEM((blocks, nstate, count, LANES), F32),
            pltpu.VMEM((blocks, nstate, CHUNKS, LANES), F32),
            pltpu.VMEM((blocks, CHUNKS, LANES), F32),
            pltpu.VMEM((nstate, inner), BF16),
            pltpu.VMEM((1, inner), F32),
            pltpu.VMEM((depth, nstate, inner), BF16),
            pltpu.VMEM((depth, 1, inner), F32),
            pltpu.VMEM((nstate, count, LANES), F32),
            pltpu.VMEM((nstate, count + CHUNKS, LANES), F32),
            pltpu.VMEM((nstate, CHUNKS, LANES), F32),
            pltpu.VMEM((count, rank), F32),
            pltpu.VMEM((count, LANES), F32),
            pltpu.SemaphoreType.DMA((2, depth - 1)),
            pltpu.SemaphoreType.DMA((2, depth - 1)),
        ]
        + reduce_scratch([s.shape[1:] + (t[1], s.dtype) for s, t in zip(sources, tasks)], depth),
        compiler_params=pltpu.CompilerParams(
            dimension_semantics=("arbitrary", "arbitrary"), collective_id=collective,
            has_side_effects=True, vmem_limit_bytes=VMEM_LIMIT,
        ),
        name="backward_scan",
    )(dfull, step, cut, rate, selected, act, sig, keep, small, stepw, *[by_chip(s, depth) for s in sources])
    return outs[:6], outs[6:]


def places(lengths, count, reach):
    steps = count // CHUNKS
    base = lax.axis_index("seq") * count
    starts = jnp.cumsum(lengths) - lengths
    here = (
        base + jnp.arange(steps, dtype=jnp.int32)[:, None]
        + steps * jnp.arange(CHUNKS, dtype=jnp.int32)[None, :]
    )

    def segment(at):
        return jnp.sum((starts[:, None, None] <= at[None]).astype(jnp.int32), axis=0) - 1

    own = segment(here)
    same = jnp.stack(
        [(segment(here - reach + k) == own).astype(F32) for k in range(reach + 1)]
    )
    opens = jnp.any(starts[:, None, None] == here[None], axis=0)
    cut = jnp.where(opens, CUT, 0.0).astype(F32).reshape(count, 1)
    return same, jnp.broadcast_to(cut, (count, LANES))


def layer_forward(xin, in_conv, other, same, cut, host, collective):
    sel, stepw, small, rate, gain = other
    count = xin.shape[0]
    inner = in_conv.shape[1]
    reach = same.shape[0] - 1
    scale = lax.rsqrt(jnp.mean(xin * xin, axis=-1, keepdims=True) + EPS)
    normed = (xin * scale * gain).astype(BF16)
    conv_in = jnp.dot(normed, in_conv, preferred_element_type=F32).astype(BF16)
    last = conv_in[(count - reach * CHUNKS) :].reshape(reach, CHUNKS, inner)[:, CHUNKS - 1]
    halo = shifted(last, "seq", 1)
    act, pre, selected = select_call(conv_in, halo, same, small, sel)
    (step, sig, moments, full, keep), got = forward_scan(
        stepw, small, act, selected, cut, rate, host[0], host[1], collective
    )
    return (scale, normed, conv_in, halo, act, pre, selected, step, sig, full, keep), moments, got


def layer_output(xin, normed, full, in_gate, out_weight):
    gate = jnp.dot(normed, in_gate, preferred_element_type=F32).astype(BF16)
    wide = gate.astype(F32)
    gated = (full * (wide * jax.nn.sigmoid(wide))).astype(BF16)
    return xin + jnp.dot(gated, out_weight, preferred_element_type=F32), gate, gated


def outer_sum(left, right):
    return lax.dot_general(left, right, (((0,), (0,)), ((), ())), preferred_element_type=F32)


def times_transposed(left, right):
    return lax.dot_general(left, right, (((1,), (1,)), ((), ())), preferred_element_type=F32)


def layer_backward(grad_out, weights, same, cut, saved, moments, host, collective):
    in_conv, in_gate, out_weight, sel, stepw, small, rate, gain = weights
    (xin, scale, normed, conv_in, halo, act, pre, selected, step, sig, full, keep, gate, gated) = saved
    count, inner = act.shape
    reach = same.shape[0] - 1
    grad_low = grad_out.astype(BF16)
    dgated = times_transposed(grad_low, out_weight)
    gout = outer_sum(gated, grad_low).astype(BF16)
    wide = gate.astype(F32)
    dfull = dgated * (wide * jax.nn.sigmoid(wide))
    dgate = (dgated * full * silu_slope(wide)).astype(BF16)
    gin_gate = outer_sum(normed, dgate).astype(BF16)
    sources, tasks = host(gout, gin_gate)
    (dact, gbias, gskip, gdecay, gstepw, dsel), found = backward_scan(
        dfull, step, cut, rate, selected, act, sig, keep, small, stepw, sources, tasks, collective
    )
    dconv, tail, spill, gsel, gsmall = conv_grad(
        conv_in, halo, same, small, sel, act, pre, dact, dsel
    )
    late = (tail + shifted(spill, "seq", -1)).astype(BF16)
    grid = dconv.reshape(count // CHUNKS, CHUNKS, inner)
    dconv = grid.at[count // CHUNKS - reach :, CHUNKS - 1].set(late).reshape(count, inner)
    gin_conv = outer_sum(normed, dconv).astype(BF16)
    dnormed = times_transposed(dconv, in_conv) + times_transposed(dgate, in_gate)
    unit = xin * scale
    ggain = jnp.sum(dnormed * unit, axis=0)
    dunit = dnormed * gain
    grad_in = scale * (dunit - unit * jnp.mean(dunit * unit, axis=-1, keepdims=True)) + grad_out
    shards = lax.axis_size(("dp", "seq"))
    per = inner // shards
    ggain = jnp.pad(ggain.reshape(shards, -1), ((0, 0), (0, per - ggain.shape[0] // shards)))
    rows = jnp.concatenate(
        [gsel, gstepw, gdecay, gsmall[: reach + 2], gbias, gskip, ggain.reshape(1, inner), moments,
         jnp.zeros((6, inner), F32)], axis=0,
    )
    return grad_in, gin_conv, gin_gate, gout, rows, found


AXES = ("section", "dp", "seq")


def body(
    inputs, doc_lengths, out_grad, norm_gain, in_weight, conv_weight, conv_bias, select_weight,
    step_weight, step_bias, log_decay, skip_gain, out_weight,
):
    section = lax.axis_index("section")
    micro, _, count, model = inputs.shape
    taps, per = conv_weight.shape[1:]
    shards = lax.axis_size(("dp", "seq"))
    inner = per * shards
    rank, nstate = step_weight.shape[1], log_decay.shape[1]
    wide = rank + 2 * nstate

    kernels = lax.axis_size("dp") == 4 and per % LANES == 0 and in_weight.shape[1] % 32 == 0
    pad = per - norm_gain.shape[1]
    rows = jnp.concatenate(
        [select_weight[0].T, step_weight[0], log_decay[0], conv_weight[0], conv_bias, step_bias, skip_gain,
         jnp.pad(norm_gain, ((0, 0), (0, pad))), jnp.zeros((8, per), BF16)], axis=0,
    )
    in_half, out_half = in_weight[0], out_weight[0]
    if kernels:
        packs = gather_rows(
            [rows, rows, in_half, in_half],
            [(0, per, 0), (1, per, 0), (0, 256, 0), (0, 256, inner)], [per, per, inner, inner], 2,
        )
        packed = [g.reshape(shards, -1, per) for g in packs[:2]]
        in_conv, in_gate = [packs[2], None], [packs[3], None]
        outs_weight = lax.all_gather(out_half, AXES, axis=0, tiled=True).reshape(2, inner, model)
        hosts = [([in_half], [(1, 256, base, inner)]) for base in (0, inner)]
    else:
        packed = lax.all_gather(rows, AXES, axis=0).reshape(2, shards, -1, per)
        in_all = lax.all_gather(in_half, AXES, axis=0, tiled=True).reshape(2, model, -1)
        in_conv, in_gate = in_all[:, :, :inner], in_all[:, :, inner:]
        outs_weight = lax.all_gather(out_half, AXES, axis=0, tiled=True).reshape(2, inner, model)
        hosts = [([], []), ([], [])]
    others = []
    for layer in range(2):
        flat = packed[layer].swapaxes(0, 1).reshape(-1, inner)
        at = wide + rank + nstate
        small = flat[at : at + 16].astype(F32)
        gain = packed[layer][:, at + taps + 3, : norm_gain.shape[1]].reshape(-1).astype(F32)
        rate = -jnp.exp(flat[wide + rank : at].astype(F32)) * LOG2E
        small = jnp.concatenate([small[: taps + 3], jnp.zeros((1, inner), F32)], axis=0)
        others.append((flat[:wide], flat[wide : wide + rank], small, rate, gain))

    mine = lambda value: lax.dynamic_index_in_dim(value, section, 0, keepdims=False)[0]
    same, cut = places(mine(doc_lengths), count, taps - 1)
    state = interleave(mine(inputs).astype(F32))
    outs, kept, weights = [], [], []
    for layer in range(2):
        saved, moments, got = layer_forward(
            state, in_conv[layer], others[layer], same, cut, hosts[layer], 5 + layer
        )
        if kernels:
            (in_gate if layer else in_conv)[1] = got[0]
        result, gate, gated = layer_output(
            state, saved[1], saved[9], in_gate[layer], outs_weight[layer]
        )
        weights.append((in_conv[layer], in_gate[layer], outs_weight[layer]) + others[layer])
        kept.append(((state,) + saved + (gate, gated), moments))
        state = result
        outs.append(state)
    grad = interleave(mine(out_grad).astype(F32))
    def split(value):
        return value.reshape(shards, -1, value.shape[1])

    grads = [None] * 2
    parts, sums = [None] * 2, [{}, {}]
    for layer in (1, 0):
        if not kernels:
            host = lambda gout, gin_gate: ([], [])
        elif layer == 1:
            host = lambda gout, gin_gate: ([split(gout), split(gin_gate)], [(1, 128), (1, 256)])
        else:
            host = lambda gout, gin_gate: ([split(gout), parts[1][1]], [(0, 128), (1, 256)])
        grad, gin_conv, gin_gate, gout, pack, found = layer_backward(
            grad, weights[layer], same, cut, *kept[layer], host, 7 + layer
        )
        grads[layer] = grad
        pack = pack.reshape(-1, shards, per).swapaxes(0, 1)
        parts[layer] = [pack, split(gin_conv), split(gin_gate), split(gout)]
        if kernels and layer == 1:
            sums[1][3], sums[1][2] = found
        elif kernels:
            sums[0][3], sums[1][1] = found

    if kernels:
        sums[0][2], sums[0][1], sums[0][0], sums[1][0] = reduce_rows(
            [parts[0][2], parts[0][1], parts[0][0], parts[1][0]],
            [(0, 256), (0, 256), (0, per), (1, per)], 3,
        )
        rows, gin_conv, gin_gate, gout = (
            jnp.where(section == 0, sums[0][i], sums[1][i]) for i in range(4)
        )
    else:
        found = []
        for pair in zip(*parts):
            both = jnp.stack(pair).reshape((-1,) + pair[0].shape[1:])
            found.append(lax.psum_scatter(both, AXES, scatter_dimension=0).astype(F32))
        rows, gin_conv, gin_gate, gout = found
    gin = jnp.concatenate([gin_conv, gin_gate], axis=1)

    def place(values):
        first, second = (in_order(value) for value in values)
        own = jnp.where(section == 0, first, second)
        other = jnp.where(section == 0, second, first)
        other = lax.ppermute(other, "section", [(0, 1), (1, 0)])
        both = jnp.stack([jnp.where(section == 0, own, other), jnp.where(section == 0, other, own)])
        return both[None, :, None]

    at = wide + rank + nstate
    tokens = micro * inputs.shape[1] * lax.axis_size("dp") * count * lax.axis_size("seq")
    return (
        place(outs),
        place(grads),
        rows[at + taps + 3, : norm_gain.shape[1]][None],
        gin[None],
        rows[at : at + taps][None],
        rows[at + taps][None],
        rows[:wide].T[None],
        rows[wide : wide + rank][None],
        rows[at + taps + 1][None],
        rows[wide + rank : at][None],
        rows[at + taps + 2][None],
        gout[None],
        (rows[at + taps + 4 : at + taps + 6] / tokens)[None],
    )


def solution(mesh):
    vector = P("section", ("dp", "seq"))
    matrix = P("section", ("dp", "seq"), None)
    turned = P("section", None, ("dp", "seq"))
    tokens = P(None, "dp", "seq", None)
    in_specs = (
        tokens, P(None, "dp", None), tokens, vector, matrix, turned, vector, matrix, turned,
        vector, turned, vector, matrix,
    )
    result = P("section", None, "dp", "seq", None)
    out_specs = (
        result, result, vector, matrix, turned, vector, matrix, turned, vector, turned, vector,
        matrix, turned,
    )
    return jax.shard_map(body, mesh=mesh, in_specs=in_specs, out_specs=out_specs, check_vma=False)
```

time: 816 us -> 602 us (0.74)
  Pallas kernels: 649 us -> 440 us
  local copies, waits for them, and re-layouts: 66.3 us -> 49.3 us
  between operations: 2 us -> 15.2 us
    pallas_call x15 -> x6, Pallas kernels: 627 us -> 417 us  [the longest x2 172 us: backward_scan(): pl.pallas_call(functools.partial(backward_scan_kernel, tasks, depth, bloc...]
    slice x12 -> x6, local copies, waits for them, and re-layouts: 9.68 us -> 0.15 us  [the longest x4 0.09 us: body(): others.append((flat[:wide], flat[wide:wide + rank], small, rate, gain))]
    dot_general x4 -> x6, matrix products: 19.7 us -> 25 us  [the longest x2 11.7 us: layer_output(): gate = jnp.dot(normed, in_gate, preferred_element_type=F32).astype(BF16)]
    dot_general x4 -> x6, matrix products: 21.1 us -> 18.4 us  [times_transposed(): lax.dot_general(left, right, (((1,), (1,)), ((), ())), preferred_element_...]
    dot_general x4 -> x6, matrix products: 22.1 us -> 21.2 us  [outer_sum(): lax.dot_general(left, right, (((0,), (0,)), ((), ())), preferred_element_...]
  transfers between devices with their start and end apart: 6 -> 7, of which waited for: 0 -> 1; matrix products, arithmetic and copies ran while one was open for 10% -> 15% of each run, Pallas kernels for 25% -> 50%
where the time goes in v2:
time: 602 us; the launch traced here: 595 us
  Pallas kernels  440 us (73%)
  matrix products  64.6 us (11%)
  local copies, waits for them, and re-layouts  49.3 us (8%)
  other arithmetic  15.3 us (3%)
  between operations  15.2 us (3%)
  starting transfers between devices  8.71 us (1%)
    pallas_call x2, Pallas kernels, backward_scan(): pl.pallas_call(functools.partial(backward_scan_kernel, tasks, depth, bloc...  172 us
    pallas_call x2, Pallas kernels, forward_scan(): pl.pallas_call(functools.partial(forward_scan_kernel, tasks, depth, block...  101 us
    pallas_call x1, Pallas kernels, gather_rows(): pl.pallas_call(functools.partial(gather_kernel, tasks, depth), in_specs=[...  78 us
    pallas_call x1, Pallas kernels, reduce_rows(): pl.pallas_call(functools.partial(reduce_kernel, tasks, depth), in_specs=[...  66.1 us
    dot_general x6, matrix products, outer_sum(): lax.dot_general(left, right, (((0,), (0,)), ((), ())), preferred_element_...  21.2 us
    dot_general x6, matrix products, times_transposed(): lax.dot_general(left, right, (((1,), (1,)), ((), ())), preferred_element_...  18.4 us
    concatenate x11, local copies, waits for them, and re-layouts, layer_backward(): jnp.concatenate([gsel, gstepw, gdecay, gsmall[:reach + 2], gbias, gskip,...  17.1 us
    pallas_call x2, Pallas kernels, conv_grad(): pl.pallas_call(conv_grad_kernel, grid=(inner // width,), in_specs=[cols(c...  12.9 us
  transfers between devices with their start and end apart: 7, of which 1 were waited for; matrix products, arithmetic and copies ran while one was open for 15% of the time, Pallas kernels for 50%

profile of v2, /device:TPU:0, one launch (start us, length us, event | category | flops | bytes accessed | tf_op | source)
XLA Modules:
  0.0 594.6 jit_solution(11554109371381591350)
XLA Ops:
  8.6 5.8 concatenate.59.refs_0_.refs_1_
  14.4 78.0 %gather_rows.1 = (bf16[2,2,4,2,96,128]{5,4,3,2,1,0:T(8,128)(2,1)}, bf16[2,2,4,2,96,128]{5,4,3,2,1,0:T(8,128)(2,1)}, bf16[2,2,4,2,32,2048]{5,4,3,2,1,0:T(8,128)(2,1)}, bf16[2,2,4,2,32,2048]{5,4,3,2,1,0:T(8,128)(2,1)}) custom-call(bf16[192,128]{1,0:T(8,128)(2,1)} %concatenate.59.refs_0_.refs_1_, bf16[192,128]{1,0:T(8,128)(2,1)} %concatenate.59.refs_0_.refs_1_, ...), custom_call_target="tpu_custom_call" | custom-call | tf_op jit(solution)/shard_map/gather_rows/pallas_call | solution.py:437
  93.3 1.1 constant_dynamic-slice_fusion.2
  94.8 3.9 convolution_convert_fusion.8.conv_ref
  99.7 2.8 collective-permute-start
  104.3 1.1 convert_bitcast_fusion
  105.4 4.8 convolution_convert_fusion.7
  118.3 4.7 conv_select.2
  123.8 52.3 %forward_scan.2 = (f32[256,2048]{1,0:T(8,128)}, f32[256,2048]{1,0:T(8,128)}, f32[2,2048]{1,0:T(2,128)}, f32[256,2048]{1,0:T(8,128)}, bf16[16,16,272,128]{3,2,1,0...) custom-call(bf16[64,2048]{1,0:T(8,128)(2,1)} %bitcast.308, f32[8,2048]{1,0:T(8,128)} %get-tuple-element.238.small_ref, ...), custom_call_target="tpu_custom_call" | custom-call | tf_op jit(solution)/shard_map/forward_scan/pallas_call | solution.py:848
  176.1 5.4 multiply_reduce_fusion.4
  181.7 1.3 convolution_convert_fusion.6.conv_ref
  184.1 2.4 collective-permute-start.1
  186.5 2.8 fusion.2
  189.9 5.1 conv_select.3
  195.0 48.8 %forward_scan.3 = (f32[256,2048]{1,0:T(8,128)}, f32[256,2048]{1,0:T(8,128)}, f32[2,2048]{1,0:T(2,128)}, f32[256,2048]{1,0:T(8,128)}, bf16[16,16,272,128]{3,2,1,0...) custom-call(bf16[64,2048]{1,0:T(8,128)(2,1)} %bitcast.310, f32[8,2048]{1,0:T(8,128)} %get-tuple-element.237.small_ref, ...), custom_call_target="tpu_custom_call" | custom-call | tf_op jit(solution)/shard_map/forward_scan/pallas_call | solution.py:848
  243.8 6.9 %fusion.17 = (bf16[256,2048]{1,0:T(8,128)(2,1)S(1)}, f32[256,2048]{1,0:T(8,128)}, bf16[256,2048]{1,0:T(8,128)(2,1)S(1)}) fusion(f32[256,2048]{1,0:T(8,128)} %fusion.2, f32[256,2048]{1,0:T(8,128)} %get-tuple-element.99, bf16[256,1024]{1,0:T(8,128)(2,1)S(1)} %multiply_convert_fusion.3, bf16[1024,2048]{1,0:T(8,128)(2,1)} %bitcast.287), kind=kOutput, calls=%fused_computation.35 | convolution fusion | flops 1081081856 | bytes 13107200 | tf_op jit(solution)/shard_map/dot_general | solution.py:1171
  250.8 3.8 convolution_convert_fusion.4
  254.6 3.3 convolution_convert_fusion.3
  257.9 85.5 %backward_scan.2 = (f32[256,2048]{1,0:T(8,128)}, f32[1,2048]{1,0:T(1,128)}, f32[1,2048]{1,0:T(1,128)}, f32[16,2048]{1,0:T(8,128)}, f32[64,2048]{1,0:T(8,128)}, /...) custom-call(f32[256,2048]{1,0:T(8,128)} %get-tuple-element.219.dfull_ref, ...), custom_call_target="tpu_custom_call" | custom-call | tf_op jit(solution)/shard_map/backward_scan/pallas_call | solution.py:1069
  343.4 6.4 %conv_grad.2 = (bf16[256,2048]{1,0:T(8,128)(2,1)}, f32[3,2048]{1,0:T(4,128)}, f32[3,2048]{1,0:T(4,128)}, f32[96,2048]{1,0:T(8,128)}, f32[8,2048]{1,0:T(8,128)}) custom-call(bf16[256,2048]{1,0:T(8,128)(2,1)} %copy-done.2, bf16[3,2048]{1,0:T(4,128)(2,1)} %copy-done.36, f32[4,32,8]{2,1,0:T(8,128)} %copy.154.same_ref, f32[8,2048]{1,0:T(8,128)} %get-tuple-element.237.small_ref, ...), custom_call_target="tpu_custom_call" | custom-call | tf_op jit(solution)/shard_map/conv_grad/pallas_call | solution.py:210
  349.9 1.6 collective-permute-start.3
  351.5 2.1 copy_bitcast_fusion
  353.6 1.9 copy_bitcast_fusion.4
  356.3 3.6 fusion.26
  360.0 3.4 convolution_convert_fusion.1
  364.0 1.7 multiply_reduce_fusion
  366.7 2.7 fusion.19
  369.5 1.6 copy.160
  371.8 3.5 convolution_convert_fusion.2
  375.3 3.7 fusion.10
  379.0 86.8 %backward_scan.3 = (f32[256,2048]{1,0:T(8,128)}, f32[1,2048]{1,0:T(1,128)}, f32[1,2048]{1,0:T(1,128)}, f32[16,2048]{1,0:T(8,128)}, f32[64,2048]{1,0:T(8,128)}, /...) custom-call(f32[256,2048]{1,0:T(8,128)} %get-tuple-element.217.dfull_ref, ...), custom_call_target="tpu_custom_call" | custom-call | tf_op jit(solution)/shard_map/backward_scan/pallas_call | solution.py:1069
  465.7 6.5 %conv_grad.3 = (bf16[256,2048]{1,0:T(8,128)(2,1)}, f32[3,2048]{1,0:T(4,128)}, f32[3,2048]{1,0:T(4,128)}, f32[96,2048]{1,0:T(8,128)}, f32[8,2048]{1,0:T(8,128)}) custom-call(bf16[256,2048]{1,0:T(8,128)(2,1)} %copy-done.1, bf16[3,2048]{1,0:T(4,128)(2,1)} %copy-done.35, f32[4,32,8]{2,1,0:T(8,128)} %copy.154.same_ref, f32[8,2048]{1,0:T(8,128)} %get-tuple-element.238.small_ref, ...), custom_call_target="tpu_custom_call" | custom-call | tf_op jit(solution)/shard_map/conv_grad/pallas_call | solution.py:210
  472.2 1.4 collective-permute-start.4
  473.6 1.2 copy_bitcast_fusion.1
  475.8 3.7 convolution_convert_fusion
  481.0 1.6 copy.159
  482.7 6.0 %concatenate.80 = f32[192,16,128]{2,0,1:T(8,128)} concatenate(f32[96,16,128]{2,0,1:T(8,128)S(1)} %copy-done.9, f32[64,16,128]{2,0,1:T(8,128)S(1)} %copy-done.10, f32[16,16,128]{2,0,1:T(8,128)S(1)} %copy_bitcast_fusion.12, f32[5,16,128]{2,0,1:T(8,128)S(1)} %slice_bitcast_fusion.10, f32[1,16,128]{2,0,1:T(1,128)} %bitcast.339, f32[1,16,128]{2,0,1:T(1,128)} %bitcast.340, ...), dimensions={0} | concatenate | bytes 3145728 | tf_op jit(solution)/shard_map/concatenate | solution.py:1216
  489.5 1.6 scatter.9
  491.1 3.9 fusion.23
  495.1 3.5 bitcast_convert_fusion
  498.6 2.8 multiply_reduce_fusion.1
  501.5 4.4 concatenate.71
  505.9 66.1 %reduce_rows.1 = (f32[64,2048]{1,0:T(8,128)}, f32[64,2048]{1,0:T(8,128)}, f32[192,128]{1,0:T(8,128)}, f32[192,128]{1,0:T(8,128)}) custom-call(bf16[2,2,4,64,2048]{4,3,2,1,0:T(8,128)(2,1)} %bitcast.275, bf16[2,2,4,64,2048]{4,3,2,1,0:T(8,128)(2,1)} %bitcast.293, f32[2,2,4,192,128]{4,3,2,1,0:T(8,128)} %bitcast.286, f32[2,2,4,192,128]{4,3,2,1,0:T(8,128)} %bitcast.285), custom_call_target="tpu_custom_call" | custom-call | tf_op jit(solution)/shard_map/reduce_rows/pallas_call | solution.py:642
  574.7 2.5 fusion.21
  581.7 1.0 maximum_bitcast_fusion.2
  582.7 1.5 bitcast_select_fusion.3
  584.2 1.5 maximum_bitcast_fusion
  586.0 1.5 maximum_bitcast_fusion.1
  (208 shorter events, 30.0 us)
Async XLA Ops:
  7.2 168.9 %all-gather.3.cloned.1.call-start = ((), (), s32[]{:S(2)}) async-start(), calls=%async_computation | async-start | bytes 8650752 | tf_op jit(solution)/shard_map/all_gather | solution.py:1252
  94.8 10.6 %copy-start.19 = (bf16[32,8,1024]{2,0,1:T(8,128)(2,1)}, bf16[32,8,1024]{2,0,1:T(8,128)(2,1)S(1)}, u32[]{:S(2)}) copy-start(bf16[32,8,1024]{2,0,1:T(8,128)(2,1)S(1)} %multiply_convert_fusion.4) | copy-start | bytes 1572868
  94.8 7.8 %copy-start.18 = (bf16[2,2,4,2,96,128]{5,4,3,2,1,0:T(8,128)(2,1)S(1)}, bf16[2,2,4,2,96,128]{5,4,3,2,1,0:T(8,128)(2,1)}, u32[]{:S(2)}) copy-start(bf16[2,2,4,2,96,128]{5,4,3,2,1,0:T(8,128)(2,1)} %get-tuple-element.89) | copy-start | bytes 2359300
  99.6 3.5 copy-start.17
  99.6 4.0 copy-start.44
  99.7 18.0 %collective-permute-start = (bf16[3,2048]{1,0:T(4,128)(2,1)S(1)}, bf16[3,2048]{1,0:T(4,128)(2,1)S(1)}, u32[]{:S(2)}, u32[]{:S(2)}) collective-permute-start(bf16[3,2048]{1,0:T(4,128)(2,1)S(1)} %bitcast.337), channel_id=1, source_target_pairs={{0,1},{1,2},{2,3},{4,5},{5,6},{6,7},{8,9},{9,10},{10,11},{12,13},{... | collective-permute-start | bytes 36872 | tf_op jit(solution)/shard_map/ppermute | solution.py:246
  105.4 4.8 copy-start.43
  105.4 5.5 copy-start.32
  176.1 5.6 copy-start.47
  176.1 10.3 %copy-start.45 = (bf16[1,4096,1024]{2,1,0:T(8,128)(2,1)S(1)}, bf16[1,4096,1024]{2,1,0:T(8,128)(2,1)}, u32[]{:S(2)}) copy-start(bf16[1,4096,1024]{2,1,0:T(8,128)(2,1)} %all-gather.3.cloned.1.call-done) | copy-start | bytes 25165828
  181.7 4.8 copy-start.28
  184.1 5.2 collective-permute-start.1
  243.8 7.0 %copy-start.29 = (bf16[1,1,256,1024]{3,2,1,0:T(8,128)(2,1)S(1)}, bf16[1,1,256,1024]{3,2,1,0:T(8,128)(2,1)}, u32[]{:S(2)}) copy-start(bf16[1,1,256,1024]{3,2,1,0:T(8,128)(2,1)} %constant_dynamic-slice_fusion) | copy-start | bytes 1572868
  243.8 7.0 %copy-start.49 = (f32[256,2048]{1,0:T(8,128)S(1)}, f32[256,2048]{1,0:T(8,128)}, u32[]{:S(2)}) copy-start(f32[256,2048]{1,0:T(8,128)} %get-tuple-element.99) | copy-start | bytes 6291460
  250.8 3.8 copy-start.53
  250.8 3.8 copy-start.7
  349.8 5.7 copy-start.34
  349.9 5.7 copy-start.38
  349.9 6.2 %copy-start.39 = (f32[3,2048]{1,0:T(4,128)S(1)}, f32[3,2048]{1,0:T(4,128)}, u32[]{:S(2)}) copy-start(f32[3,2048]{1,0:T(4,128)} %get-tuple-element.109) | copy-start | bytes 73732
  349.9 6.2 %copy-start.16 = (bf16[256,2048]{1,0:T(8,128)(2,1)S(1)}, bf16[256,2048]{1,0:T(8,128)(2,1)}, u32[]{:S(2)}) copy-start(bf16[256,2048]{1,0:T(8,128)(2,1)} %get-tuple-element.108) | copy-start | bytes 3145732
  349.9 6.2 %collective-permute-start.3 = (f32[3,2048]{1,0:T(4,128)}, f32[3,2048]{1,0:T(4,128)S(1)}, u32[]{:S(2)}, u32[]{:S(2)}) collective-permute-start(f32[3,2048]{1,0:T(4,128)} %get-tuple-element.110), channel_id=1, source_target_pairs={{1,0},{2,1},{3,2},{5,4},{6,5},{7,6},{9,8},{10,9},{11,10},{13,12},{... | collective-permute-start | bytes 73736 | tf_op jit(solution)/shard_map/ppermute | solution.py:246
  356.3 9.4 %slice-start = ((s8[8388608]{0:T(1024)(128)(4,1)}), s8[4194304]{0:T(1024)(128)(4,1)S(1)}, s32[]{:S(2)}) async-start(s8[8388608]{0:T(1024)(128)(4,1)} %bitcast.345), calls=%async_computation.1 | async-start | bytes 8388608
  359.9 3.5 copy-start.5
  359.9 3.5 copy-start.6
  359.9 4.0 copy-start.8
  360.0 5.7 slice-start.1
  366.7 4.3 copy-start.52
  369.5 5.8 copy-start.15
  371.0 211.7 %collective-permute-start.2 = (f32[256,1024]{1,0:T(8,128)}, f32[256,1024]{1,0:T(8,128)}, u32[]{:S(2)}, u32[]{:S(2)}) collective-permute-start(f32[256,1024]{1,0:T(8,128)} %bitcast.36), channel_id=1, source_target_pairs={{0,16},{16,0},{1,17},{17,1},{2,18},{18,2},{3,19},{19,3},{4,20},{20... | collective-permute-start | bytes 3145736 | tf_op jit(solution)/shard_map/ppermute | solution.py:1331
  465.7 9.1 %copy-start.25 = (f32[64,2048]{1,0:T(8,128)S(1)}, f32[64,2048]{1,0:T(8,128)}, u32[]{:S(2)}) copy-start(f32[64,2048]{1,0:T(8,128)} %get-tuple-element.120) | copy-start | bytes 1572868
  472.2 3.5 copy-start.33
  472.2 3.5 copy-start
  472.2 3.5 copy-start.12
  472.2 16.5 %collective-permute-start.4 = (f32[3,2048]{1,0:T(4,128)}, f32[3,2048]{1,0:T(4,128)}, u32[]{:S(2)}, u32[]{:S(2)}) collective-permute-start(f32[3,2048]{1,0:T(4,128)} %get-tuple-element.118), channel_id=1, source_target_pairs={{1,0},{2,1},{3,2},{5,4},{6,5},{7,6},{9,8},{10,9},{11,10},{13,12},{... | collective-permute-start | bytes 73736 | tf_op jit(solution)/shard_map/ppermute | solution.py:246
  475.8 3.7 copy-start.23
  475.8 3.7 copy-start.24
  475.8 4.6 copy-start.37
  475.8 5.2 copy-start.14
  479.5 3.2 copy-start.9
  479.5 3.2 copy-start.10
  491.1 3.9 copy-start.20
  491.1 3.9 copy-start.51
  495.1 3.5 copy-start.13
  495.1 3.5 copy-start.46
  498.6 2.9 copy-start.11
  498.6 2.9 copy-start.31
  498.6 2.9 copy-start.40
  577.9 7.8 %collective-permute-start.5 = (f32[256,1024]{1,0:T(8,128)S(1)}, f32[256,1024]{1,0:T(8,128)S(1)}, u32[]{:S(2)}, u32[]{:S(2)}) collective-permute-start(f32[256,1024]{1,0:T(8,128)S(1)} %bitcast.318), channel_id=1, source_target_pairs={{0,16},{16,0},{1,17},{17,1},{2,18},{18,2},{3,19},{19,3},{4,20},{20... | collective-permute-start | bytes 3145736 | tf_op jit(solution)/shard_map/ppermute | solution.py:1331
  (16 other events, 26.6 us)
Sparse Core Ops, SparseCore 0:
  11.0 97.5 all-gather.2
